TPU v7x, 32 devices: a whole 2x2x4 slice. The times are simulated.
32 devices in a mesh: grp: 2 (over y), band: 8 (over z, x), filt: 2 (over core).
Axes of the slice: x: 2, y: 2, z: 4, core: 2. Of those that a mesh axis runs over, the one named last changes fastest.
Arguments:
- coeff_maps: bfloat16 [128, 64, 512], P(('grp', 'filt'), 'band'), parts along dimension 0, may hold values from -0.75 to 0.75
- image: bfloat16 [6, 64, 512], P('grp', 'band'), parts along dimension 0, may hold values from -24 to 24
- target: bfloat16 [1024, 2, 3, 64, 64], P(('grp', 'band'), None, None, 'filt'), parts along dimension 0, may hold values from -1.5 to 1.5
- dual_rim: float32 [128, 768], P(('grp', 'filt')), parts along dimension 0, may hold values from -18 to 18, as said below
Outputs:
- dict_spectra: bfloat16 [1024, 2, 3, 64, 64], P(('grp', 'band'), None, None, 'filt'), parts along dimension 0
- dictionary: float32 [128, 768], P(('grp', 'filt')), parts along dimension 0
There are 2 independent parts, one for each index of `grp`. A program takes and returns all parts, laid end to end along the dimension named above; each array names one. Nothing has to cross between parts.
Inputs may be any that keep to these rules, and one draw needn't show every extreme that they name: `dual_rim`: a scaled dual variable on the filters' support.
All inputs are finite; a program needn't handle non-finite values.
Results may differ from a plain program's by a relative error of at most 0.0059.
Values may be sent and summed in bfloat16 or wider, within the bound.
No kernel may reach another device: no remote copies, remote signals or barrier semaphores. Data moves between devices by JAX's collectives and lax.ppermute only.
A program may use at most 128 MiB of HBM per device.

v0:
```python
import math

import jax
import jax.numpy as jnp
from jax import lax
from jax.sharding import PartitionSpec as P

K = 16


penalty = 1.0


def forward_columns(length):
    ramp = jnp.arange(length, dtype=jnp.int32)
    phases = ramp[:, None] * ramp[None, :] % length
    angles = phases.astype(jnp.float32) * (2.0 * math.pi / length)
    factor = 1.0 / math.sqrt(length)
    lookup = jnp.stack([jnp.cos(angles) * factor, -jnp.sin(angles) * factor], axis=2)
    return lookup.reshape(length, 2 * length).astype(jnp.bfloat16)


def forward_rows(length):
    ramp = jnp.arange(length, dtype=jnp.int32)
    phases = ramp[:, None] * ramp[None, :] % length
    angles = phases.astype(jnp.float32) * (2.0 * math.pi / length)
    factor = 1.0 / math.sqrt(length)
    return jnp.stack([jnp.cos(angles) * factor, jnp.sin(angles) * factor], axis=0).astype(
        jnp.bfloat16
    )


def inverse_rows(length, width):
    ramp = jnp.arange(length, dtype=jnp.int32)
    reach = jnp.arange(width, dtype=jnp.int32)
    phases = ramp[:, None] * reach[None, :] % length
    angles = phases.astype(jnp.float32) * (2.0 * math.pi / length)
    factor = 1.0 / math.sqrt(length)
    return jnp.stack([jnp.cos(angles) * factor, jnp.sin(angles) * factor], axis=1)


def inverse_columns(length, total_cols, width):
    freqs = jnp.arange(length, dtype=jnp.int32)
    reach = jnp.arange(width, dtype=jnp.int32)
    phases = freqs[:, None] * reach[None, :] % total_cols
    angles = phases.astype(jnp.float32) * (2.0 * math.pi / total_cols)
    factor = 1.0 / math.sqrt(total_cols)
    return jnp.stack([jnp.cos(angles) * factor, jnp.sin(angles) * factor], axis=1)


def spectra(slab_rows, lookup, freqs, members):
    height = slab_rows.shape[0]
    products = jnp.einsum("hk,tgh->ktg", slab_rows, lookup, preferred_element_type=jnp.float32)
    products = products.reshape(freqs, 2, members, 2, height)
    real_part = products[:, 0, :, 0] + products[:, 1, :, 1]
    imag_part = products[:, 1, :, 0] - products[:, 0, :, 1]
    return (real_part, imag_part)


def body(coeff_maps, image, target, dual_rim):
    filters, band_rows, width_cols = coeff_maps.shape
    channels = image.shape[0]
    band_count = lax.axis_size("band")
    height = band_rows * band_count
    per_band = width_cols // band_count
    col_lookup = forward_columns(width_cols)
    row_lookup = forward_rows(height)
    col_maps = jnp.einsum("mrn,nk->rkm", coeff_maps, col_lookup, preferred_element_type=jnp.float32)
    col_maps = col_maps.astype(jnp.bfloat16).reshape(band_rows, 2 * width_cols * filters)
    col_image = jnp.einsum("crn,nk->rkc", image, col_lookup, preferred_element_type=jnp.float32)
    col_image = col_image.astype(jnp.bfloat16).reshape(band_rows, 2 * width_cols * channels)
    got_maps, got_image = (
        lax.all_to_all(col_maps, "band", split_axis=1, concat_axis=0, tiled=True),
        lax.all_to_all(col_image, "band", split_axis=1, concat_axis=0, tiled=True),
    )
    x_re, x_im = spectra(got_maps, row_lookup, per_band, filters)
    s_re, s_im = spectra(got_image, row_lookup, per_band, channels)
    v_full = target.astype(jnp.float32)
    v_re = v_full[:, 0]
    v_im = v_full[:, 1]
    energy = jnp.sum(x_re * x_re + x_im * x_im, axis=1)
    cross_re = jnp.sum(x_re[:, None] * v_re - x_im[:, None] * v_im, axis=2)
    cross_im = jnp.sum(x_re[:, None] * v_im + x_im[:, None] * v_re, axis=2)
    energy, cross_re, cross_im = (
        lax.psum(energy.astype(jnp.bfloat16), "filt").astype(jnp.float32),
        lax.psum(cross_re.astype(jnp.bfloat16), "filt").astype(jnp.float32),
        lax.psum(cross_im.astype(jnp.bfloat16), "filt").astype(jnp.float32),
    )
    denom = penalty + energy[:, None, :]
    coef_re = (s_re - cross_re) / denom
    coef_im = (s_im - cross_im) / denom
    dict_real = v_re + x_re[:, None] * coef_re[:, :, None] + x_im[:, None] * coef_im[:, :, None]
    dict_imag = v_im + x_re[:, None] * coef_im[:, :, None] - x_im[:, None] * coef_re[:, :, None]
    dict_full = jnp.stack([dict_real, dict_imag], axis=1)
    dict_spectra = dict_full.astype(jnp.bfloat16)
    rim_lookup = inverse_rows(height, K)
    folded = jnp.einsum("qpcmg,gty->qpcmty", dict_full, rim_lookup, precision=lax.Precision.HIGHEST)
    rim_real = folded[:, 0, :, :, 0] - folded[:, 1, :, :, 1]
    rim_imag = folded[:, 0, :, :, 1] + folded[:, 1, :, :, 0]
    start_sum = jnp.zeros((filters, channels, K, K), jnp.float32)
    running = start_sum
    pieces = (
        lax.all_gather(rim_real.astype(jnp.bfloat16), "band", axis=0, tiled=True).astype(
            jnp.float32
        ),
        lax.all_gather(rim_imag.astype(jnp.bfloat16), "band", axis=0, tiled=True).astype(
            jnp.float32
        ),
    )
    length = pieces[0].shape[0]
    lookup = inverse_columns(length, width_cols, K)
    running = running + jnp.einsum(
        "qcmy,qx->mcyx", pieces[0], lookup[:, 0], precision=lax.Precision.HIGHEST
    )
    spatial = running - jnp.einsum(
        "qcmy,qx->mcyx", pieces[1], lookup[:, 1], precision=lax.Precision.HIGHEST
    )
    joined = spatial.reshape(filters, channels * K * K) + dual_rim
    spread = jnp.sqrt(jnp.mean(joined * joined, axis=1, keepdims=True))
    dictionary = joined / jnp.maximum(spread, 1.0)
    return (dict_spectra, dictionary)


def solution(mesh):
    placed = (
        P(("grp", "filt"), "band", None),
        P("grp", "band", None),
        P(("grp", "band"), None, None, "filt", None),
        P(("grp", "filt"), None),
    )
    return jax.shard_map(
        body,
        mesh=mesh,
        in_specs=placed,
        out_specs=(P(("grp", "band"), None, None, "filt", None), P(("grp", "filt"), None)),
        check_vma=False,
    )
```

profile of v0, /device:TPU:0, one launch (start us, length us, event | category | flops | bytes accessed | tf_op | source)
XLA Modules:
  0.0 297.8 jit_solution(11534772521772797656)
XLA Ops:
  7.2 4.4 %multiply_convert_fusion = (bf16[512,512,1]{1,0,2:T(8,128)(2,1)S(1)}, bf16[512,512,1]{1,0,2:T(8,128)(2,1)S(1)}) fusion(), kind=kLoop, calls=%fused_computation.42 | loop fusion | flops 4980736 | bytes 1048576 | tf_op jit(solution)/shard_map/convert.3
  11.6 0.1 pad_maximum_fusion.2
  11.7 1.0 copy.59
  12.7 0.4 convert_element_type.110
  13.1 0.4 fusion.15
  13.5 0.7 copy.69
  14.2 0.6 all_to_all.32
  14.9 0.9 copy.70
  15.7 7.3 %all-to-all-start.1 = ((bf16[8,8,384]{2,0,1:T(8,128)(2,1)}), bf16[8,8,384]{2,0,1:T(8,128)(2,1)S(1)}, u32[]{:S(2)}, u32[]{:S(2)}) async-start(bf16[8,8,384]{2,0,1:T(8,128)(2,1)} %copy.70), calls=%async_computation.1 | async-start | bytes 98304 | tf_op jit(solution)/shard_map/all_to_all | solution.py:74
  23.0 0.5 fusion.11
  23.5 1.0 copy.62
  24.5 2.3 all_to_all.28
  26.8 1.1 copy.63
  27.9 1.9 all-to-all-done.1
  29.8 4.1 %all-to-all-start = ((bf16[8,8,4096]{2,0,1:T(8,128)(2,1)}), bf16[8,8,4096]{2,0,1:T(8,128)(2,1)S(1)}, u32[]{:S(2)}, u32[]{:S(2)}) async-start(bf16[8,8,4096]{2,0,1:T(8,128)(2,1)} %copy.63), calls=%async_computation | async-start | bytes 1048576 | tf_op jit(solution)/shard_map/all_to_all | solution.py:73
  33.9 0.0 all-gather.7.cloned.1.call-start
  33.9 0.1 sine_multiply_fusion
  34.0 0.2 multiply_convert_fusion.2
  34.1 6.4 %copy_convert_fusion = f32[64,2,3,32,64]{4,0,3,2,1:T(8,128)} fusion(bf16[64,2,3,32,64]{4,3,2,1,0:T(8,128)(2,1)} %param.6), kind=kLoop, calls=%fused_computation.12 | loop fusion | flops 786432 | bytes 4718592 | tf_op jit(solution)/shard_map/convert_element_type | solution.py:78
  40.5 0.1 copy.71
  40.6 0.1 dot_general.35
  40.7 0.2 fusion.39
  40.9 6.9 %all-to-all-done = bf16[8,8,4096]{2,0,1:T(8,128)(2,1)S(1)} async-done(((bf16[8,8,4096]{2,0,1:T(8,128)(2,1)}), bf16[8,8,4096]{2,0,1:T(8,128)(2,1)S(1)}, u32[]{:S(2)}, u32[]{:S(2)}) %all-to-all-start) | async-done | bytes 524320 | tf_op jit(solution)/shard_map/all_to_all | solution.py:73
  47.9 0.5 copy.64
  48.4 0.9 fusion.22
  49.2 0.7 add_reduce_fusion
  49.9 0.6 slice-done
  50.5 1.4 slice-done.1
  51.9 1.1 fusion.4
  53.0 3.9 %all-reduce = (bf16[64,3,64]{2,0,1:T(8,128)(2,1)S(1)}, bf16[64,64]{1,0:T(8,128)(2,1)S(1)}, bf16[64,3,64]{2,0,1:T(8,128)(2,1)S(1)}) all-reduce(bf16[64,3,64]{2,0,1:T(8,128)(2,1)S(1)} %get-tuple-element.11, bf16[64,64]{1,0:T(8,128)(2,1)S(1)} %get-tuple-element.17, ...), channel_id=1, replica_groups=mesh['grp'=2,'band'=8,'filt'=2] {'filt'}, use_global_device_ids=true, to_apply=%region_5.6 | all-reduce | flops 28672 | bytes 114688 | tf_op jit(solution)/shard_map/psum | solution.py:87
  57.0 4.5 %multiply_add_fusion = (f32[64,1,3,32,64]{4,0,3,2,1:T(8,128)S(1)}, f32[64,1,3,32,64]{4,0,3,2,1:T(8,128)S(1)}) fusion(f32[64,2,3,32,64]{4,0,3,2,1:T(8,128)} %copy_convert_fusion, f32[64,3,64]{2,0,1:T(8,128)S(1)} %get-tuple-element.25, f32[64,32,64]{2,0,1:T(8,128)} %copy-done.3, f32[64,3,64]{2,0,1:T(8,128)S(1)} %get-tuple-element.24, f32[64,32,64]{2,0,1:T(8,128)} %copy-done.2), kind=kLoop, calls=%fused_computation.14 | loop fusion | flops 3145728 | bytes 7438336 | tf_op jit(solution)/shard_map/add | solution.py:92
  61.5 17.3 %fusion = f32[64,2,3,32,2,16]{0,5,4,3,2,1:T(8,128)S(1)} fusion(f32[64,1,3,32,64]{4,0,3,2,1:T(8,128)S(1)} %get-tuple-element.21, f32[64,1,3,32,64]{4,0,3,2,1:T(8,128)S(1)} %get-tuple-element.20, f32[64,1,16]{0,2,1:T(8,128)S(1)} %get-tuple-element.30, f32[64,1,16]{0,2,1:T(8,128)S(1)} %get-tuple-element.31), kind=kOutput, calls=%fused_computation.1 | convolution fusion | flops 302778368 | bytes 4726784 | tf_op jit(solution)/shard_map/qpcmg,gty->qpcmty/dot_general | solution.py:97
  78.9 1.1 fusion.30
  80.0 2.7 copy.77
  82.7 0.0 all-gather.7.cloned.1.call-update
  82.7 0.3 all-gather.5.cloned.1.call-start
  83.0 2.7 copy.75
  85.7 2.4 fusion.2
  88.1 3.7 %copy.80 = bf16[64,2,3,32,64]{4,3,2,1,0:T(8,128)(2,1)} copy(bf16[64,2,3,32,64]{4,0,3,2,1:T(8,128)(2,1)S(1)} %fusion.2) | data formatting | bytes 3145728
  91.7 89.3 %all-gather.7.cloned.1.call-done = bf16[512,1,3,32,1,16]{3,5,4,2,1,0:T(8,128)(2,1)} async-done(((bf16[64,1,3,32,1,16]{3,5,4,2,1,0:T(8,128)(2,1)}), bf16[512,1,3,32,1,16]{3,5,4,2,1,0:T(8,128)(2,1)}) %all-gather.7.cloned.1.call-update) | async-done | bytes 1572880 | tf_op jit(solution)/shard_map/all_gather | solution.py:106
  181.0 6.4 %copy.78 = bf16[512,1,3,32,1,16]{0,3,5,2,4,1:T(8,128)(2,1)S(1)} copy(bf16[512,1,3,32,1,16]{3,5,4,2,1,0:T(8,128)(2,1)} %all-gather.7.cloned.1.call-done) | data formatting | bytes 3145728 | tf_op jit(solution)/shard_map/all_gather | solution.py:106
  187.4 3.2 %fusion.7 = f32[16,3,32,16]{2,0,3,1:T(8,128)S(1)} fusion(bf16[512,1,3,32,1,16]{0,3,5,2,4,1:T(8,128)(2,1)S(1)} %copy.78), kind=kOutput, calls=%fused_computation.15 | convolution fusion | flops 151117824 | bytes 1671168 | tf_op jit(solution)/shard_map/qcmy,qx->mcyx/dot_general | solution.py:115
  190.5 89.9 %all-gather.5.cloned.1.call-done = bf16[512,1,3,32,1,16]{3,5,4,2,1,0:T(8,128)(2,1)} async-done(((bf16[64,1,3,32,1,16]{3,5,4,2,1,0:T(8,128)(2,1)}), bf16[512,1,3,32,1,16]{3,5,4,2,1,0:T(8,128)(2,1)}) %all-gather.5.cloned.1.call-update) | async-done | bytes 1572880 | tf_op jit(solution)/shard_map/all_gather | solution.py:103
  280.4 6.4 %copy.76 = bf16[512,1,3,32,1,16]{0,3,5,2,4,1:T(8,128)(2,1)S(1)} copy(bf16[512,1,3,32,1,16]{3,5,4,2,1,0:T(8,128)(2,1)} %all-gather.5.cloned.1.call-done) | data formatting | bytes 3145728 | tf_op jit(solution)/shard_map/all_gather | solution.py:103
  286.8 3.2 %fusion.12 = f32[16,3,32,16]{2,0,3,1:T(8,128)S(1)} fusion(f32[16,3,32,16]{2,0,3,1:T(8,128)S(1)} %fusion.7, bf16[512,1,3,32,1,16]{0,3,5,2,4,1:T(8,128)(2,1)S(1)} %copy.76), kind=kOutput, calls=%fused_computation.24 | convolution fusion | flops 151142400 | bytes 1769472 | tf_op jit(solution)/shard_map/qcmy,qx->mcyx/dot_general | solution.py:112
  290.0 0.2 copy.79
  290.1 0.1 multiply_reduce_fusion
  290.3 0.7 broadcast_divide_fusion
  (19 shorter events, 0.1 us)
Async XLA Ops:
  7.2 15.8 %copy-start = (bf16[32,8,512]{2,1,0:T(8,128)(2,1)S(1)}, bf16[32,8,512]{2,1,0:T(8,128)(2,1)}, u32[]{:S(2)}) copy-start(bf16[32,8,512]{2,1,0:T(8,128)(2,1)} %param.4) | copy-start | bytes 786436
  11.6 1.6 copy-start.5
  15.7 14.0 %all-to-all-start.1 = ((bf16[8,8,384]{2,0,1:T(8,128)(2,1)}), bf16[8,8,384]{2,0,1:T(8,128)(2,1)S(1)}, u32[]{:S(2)}, u32[]{:S(2)}) async-start(bf16[8,8,384]{2,0,1:T(8,128)(2,1)} %copy.70), calls=%async_computation.1 | async-start | bytes 98304 | tf_op jit(solution)/shard_map/all_to_all | solution.py:74
  29.8 18.1 %all-to-all-start = ((bf16[8,8,4096]{2,0,1:T(8,128)(2,1)}), bf16[8,8,4096]{2,0,1:T(8,128)(2,1)S(1)}, u32[]{:S(2)}, u32[]{:S(2)}) async-start(bf16[8,8,4096]{2,0,1:T(8,128)(2,1)} %copy.63), calls=%async_computation | async-start | bytes 1048576 | tf_op jit(solution)/shard_map/all_to_all | solution.py:73
  33.9 147.1 %all-gather.7.cloned.1.call-start = ((), (), s32[]{:S(2)}) async-start(), calls=%async_computation.3 | async-start | bytes 7077888 | tf_op jit(solution)/shard_map/all_gather | solution.py:106
  48.3 2.2 slice-start
  48.3 3.6 %slice-start.1 = ((s8[6291456]{0:T(1024)(128)(4,1)}), s8[2097152]{0:T(1024)(128)(4,1)S(1)}, s32[]{:S(2)}) async-start(s8[6291456]{0:T(1024)(128)(4,1)} %bitcast.128), calls=%async_computation.5 | async-start | bytes 4194304
  49.9 3.1 %copy-start.2 = (f32[64,32,64]{2,0,1:T(8,128)}, f32[64,32,64]{2,0,1:T(8,128)S(1)}, u32[]{:S(2)}) copy-start(f32[64,32,64]{2,0,1:T(8,128)S(1)} %get-tuple-element.18) | copy-start | bytes 1572868
  49.9 3.1 %copy-start.3 = (f32[64,32,64]{2,0,1:T(8,128)}, f32[64,32,64]{2,0,1:T(8,128)S(1)}, u32[]{:S(2)}) copy-start(f32[64,32,64]{2,0,1:T(8,128)S(1)} %get-tuple-element.19) | copy-start | bytes 1572868
  61.5 17.4 %copy-start.1 = (f32[64,1,3,32,64]{4,0,3,2,1:T(8,128)}, f32[64,1,3,32,64]{4,0,3,2,1:T(8,128)S(1)}, u32[]{:S(2)}) copy-start(f32[64,1,3,32,64]{4,0,3,2,1:T(8,128)S(1)} %get-tuple-element.21) | copy-start | bytes 4718596
  82.7 197.7 %all-gather.5.cloned.1.call-start = ((), (), s32[]{:S(2)}) async-start(), calls=%async_computation.2 | async-start | bytes 7077888 | tf_op jit(solution)/shard_map/all_gather | solution.py:103
  190.5 99.6 %copy-start.4 = (f32[32,768]{1,0:T(8,128)S(1)}, f32[32,768]{1,0:T(8,128)}, u32[]{:S(2)}) copy-start(f32[32,768]{1,0:T(8,128)} %param.7) | copy-start | bytes 294916
Sparse Core Ops, SparseCore 0:
  82.9 98.1 all-gather.6
  183.2 97.1 all-gather.4
where the time goes:
time: 298 us
  waiting for transfers between devices  188 us (63%)
  local copies, waits for them, and re-layouts  32.7 us (11%)
  matrix products  25.6 us (9%)
  other arithmetic  21.7 us (7%)
  between operations  14.3 us (5%)
  starting transfers between devices  11.6 us (4%)
  blocking collectives  3.9 us (1%)
    all_gather x1, waiting for transfers between devices, body(): lax.all_gather(rim_real.astype(jnp.bfloat16), 'band', axis=0, tiled=True)  89.9 us
    all_gather x1, waiting for transfers between devices, body(): lax.all_gather(rim_imag.astype(jnp.bfloat16), 'band', axis=0, tiled=True)  89.3 us
    dot_general x1, matrix products, body(): jnp.einsum('qpcmg,gty->qpcmty', dict_full, rim_lookup, precision=lax.Prec...  17.3 us
    all_to_all x1, starting transfers between devices, body(): lax.all_to_all(col_image, 'band', split_axis=1, concat_axis=0, tiled=True)  7.25 us
    all_to_all x1, waiting for transfers between devices, body(): lax.all_to_all(col_maps, 'band', split_axis=1, concat_axis=0, tiled=True)  6.91 us
    convert_element_type x1, other arithmetic, body(): v_full = target.astype(jnp.float32)  6.37 us
    all_gather x1, local copies, waits for them, and re-layouts, body(): lax.all_gather(rim_imag.astype(jnp.bfloat16), 'band', axis=0, tiled=True)  6.36 us
    all_gather x1, local copies, waits for them, and re-layouts, body(): lax.all_gather(rim_real.astype(jnp.bfloat16), 'band', axis=0, tiled=True)  6.36 us
  transfers between devices with their start and end apart: 4, of which 4 were waited for; matrix products, arithmetic and copies ran while one was open for 9% of the time, Pallas kernels for 0%

commit v1 on v0

v1 whole, which is shorter than its diff:
```python
import math

import jax
import jax.numpy as jnp
import numpy as np
from jax import lax
from jax.experimental import pallas as pl
from jax.experimental.pallas import tpu as pltpu
from jax.sharding import PartitionSpec as P

K = 16
LANES = 128
HALF = 64

penalty = 1.0

bf16 = jnp.bfloat16
f32 = jnp.float32


def column_table(length, bands):
    ramp = np.arange(length)
    angles = (ramp[:, None] * ramp[None, :] % length) * (2.0 * math.pi / length)
    factor = 1.0 / math.sqrt(length)
    table = np.stack([np.cos(angles) * factor, -np.sin(angles) * factor], axis=1)
    table = table.reshape(length, 2, bands, length // bands).transpose(0, 2, 1, 3)
    return table.reshape(length, 2 * length).astype(np.float32).astype(bf16)


def row_table(height, band_rows):
    ramp = np.arange(height)
    angles = (ramp[:, None] * ramp[None, :] % height) * (2.0 * math.pi / height)
    factor = 1.0 / math.sqrt(height)
    cos, sin = np.cos(angles) * factor, np.sin(angles) * factor
    both = np.stack(
        [np.concatenate([cos, -sin], axis=1), np.concatenate([sin, cos], axis=1)]
    )
    both = both.reshape(2, height // band_rows, band_rows, 2 * height)
    table = np.zeros((2, height // band_rows, 2, band_rows, 2, 2 * height))
    table[:, :, 0, :, 0] = both
    table[:, :, 1, :, 1] = both
    return table.reshape(4 * height, 4 * height).astype(np.float32).astype(bf16)


def angle_tables(height, columns, width):
    reach = np.arange(width)
    rows = (np.arange(height)[:, None] * reach[None, :] % height) * (2.0 * math.pi / height)
    rows = np.repeat(rows, width, axis=1)
    cols = (np.arange(columns)[:, None] * reach[None, :] % columns) * (2.0 * math.pi / columns)
    cols = np.tile(cols, (1, width))
    factor = 1.0 / math.sqrt(height * columns)
    row_pair = np.stack([np.cos(rows) * factor, np.sin(rows) * factor])
    col_pair = np.stack([np.cos(cols), np.sin(cols)])
    return row_pair.astype(np.float32), col_pair.astype(np.float32)


def low_lanes(shape):
    return lax.broadcasted_iota(jnp.int32, shape, len(shape) - 1) < HALF


def columns_kernel(maps_ref, image_ref, table_ref, out_ref):
    bands = out_ref.shape[0]
    rows = maps_ref.shape[0]
    for b in range(bands):
        table = table_ref[:, b * LANES : (b + 1) * LANES]
        out_ref[b, :rows] = jnp.dot(maps_ref[...], table, preferred_element_type=f32).astype(bf16)
        out_ref[b, rows:] = jnp.dot(image_ref[...], table, preferred_element_type=f32).astype(bf16)


def prepare_kernel(target_ref, row_ref, col_ref, packed_ref, inverse_ref):
    freqs, _, channels, filters, height = target_ref.shape

    def step(q, carry):
        for c in range(channels):
            packed_ref[q, c] = jnp.concatenate(
                [target_ref[q, 0, c].astype(f32), target_ref[q, 1, c].astype(f32)], axis=-1
            )
        cos_col = col_ref[0, pl.ds(q, 1), :]
        sin_col = col_ref[1, pl.ds(q, 1), :]
        cos_row = row_ref[0]
        sin_row = row_ref[1]
        inverse_ref[q, :height] = (cos_row * cos_col - sin_row * sin_col).astype(bf16)
        inverse_ref[q, height:] = (-(sin_row * cos_col) - cos_row * sin_col).astype(bf16)
        return carry

    lax.fori_loop(0, freqs, step, 0, unroll=2)


def rows_kernel(got_ref, table_ref, packed_ref, x_ref, image_ref, own_ref, send_ref, one_ref, two_ref):
    freqs, channels, filters, _ = packed_ref.shape
    sources, rows, _ = got_ref.shape
    band_rows = rows // (filters + channels)
    pair = 2 * band_rows
    table = table_ref[...]

    def transform(start):
        block = got_ref[:, start : start + pair, :].reshape(sources * pair, LANES)
        turned = block.T
        left = jnp.concatenate([turned[:freqs], turned[freqs:]], axis=1)
        return jnp.dot(left, table, preferred_element_type=f32)

    for j in range(filters // 2):
        both = transform(j * pair)
        x_ref[pl.ds(2 * j, freqs, stride=filters), :] = both[:, :LANES]
        x_ref[pl.ds(2 * j + 1, freqs, stride=filters), :] = both[:, LANES:]
    for c in range(channels):
        first = min(c, channels - 2)
        both = transform((filters + first) * band_rows)
        part = (c - first) * LANES
        image_ref[c * freqs : (c + 1) * freqs, :] = both[:, part : part + LANES]

    group = 8

    def step(i, carry):
        q0 = pl.multiple_of(i * group, group)
        x = x_ref[pl.ds(pl.multiple_of(q0 * filters, group * filters), group * filters), :]
        y = pltpu.roll(x, HALF, 1)
        x = x.reshape(group, filters, LANES)
        y = y.reshape(group, filters, LANES)
        one_ref[pl.ds(channels * freqs + q0, group), :] = jnp.sum(x * x, axis=1)
        for c in range(channels):
            v = packed_ref[pl.ds(q0, group), c]
            one_ref[pl.ds(c * freqs + q0, group), :] = jnp.sum(x * v, axis=1)
            two_ref[pl.ds(c * freqs + q0, group), :] = jnp.sum(y * v, axis=1)
        return carry

    lax.fori_loop(0, freqs // group, step, 0)
    top = channels * freqs
    one = one_ref[:top]
    two = two_ref[...]
    low = low_lanes(one.shape)
    cross = jnp.where(low, one - pltpu.roll(one, HALF, 1), two + pltpu.roll(two, HALF, 1))
    energy = one_ref[top:]
    energy = energy + pltpu.roll(energy, HALF, 1)
    own_ref[:top] = cross
    own_ref[top:] = energy
    send_ref[:top] = cross.astype(bf16)
    send_ref[top:] = energy.astype(bf16)


def solve_kernel(
    x_ref, packed_ref, image_ref, own_ref, peer_ref, inverse_ref, out_ref, rim_ref, re_ref, im_ref
):
    freqs, channels, filters, _ = packed_ref.shape
    top = channels * freqs
    total = own_ref[...] + peer_ref[...].astype(f32)
    denom = penalty + total[top:]
    low = low_lanes(denom.shape)
    for c in range(channels):
        span = slice(c * freqs, (c + 1) * freqs)
        coef = (image_ref[span] - total[span]) / denom
        turned = pltpu.roll(coef, HALF, 1)
        re_ref[span] = jnp.where(low, coef, -turned)
        im_ref[span] = jnp.where(low, turned, coef)

    def step(i, acc):
        sides = []
        for k in range(2):
            q = 2 * i + k
            x = x_ref[pl.ds(pl.multiple_of(q * filters, filters), filters), :]
            y = pltpu.roll(x, HALF, 1)
            parts = []
            for c in range(channels):
                d = (
                    packed_ref[q, c]
                    + x * re_ref[pl.ds(c * freqs + q, 1), :]
                    + y * im_ref[pl.ds(c * freqs + q, 1), :]
                )
                d = d.astype(bf16)
                out_ref[q, 0, c] = d[:, :HALF]
                out_ref[q, 1, c] = d[:, HALF:]
                parts.append(d)
            sides.append(jnp.concatenate(parts, axis=0))
        left = jnp.concatenate(sides, axis=1)
        right = inverse_ref[pl.ds(2 * i, 2)].reshape(2 * LANES, inverse_ref.shape[2])
        return acc + jnp.dot(left, right, preferred_element_type=f32)

    acc = jnp.zeros(rim_ref.shape, f32)
    acc = lax.fori_loop(0, freqs // 2, step, acc, unroll=2)
    rim_ref[...] = acc.astype(bf16)


def finish_kernel(*refs):
    part_refs, dual_ref, out_ref = refs[:-2], refs[-2], refs[-1]
    filters = dual_ref.shape[0]
    sums = [r[...].astype(f32) for r in part_refs]
    while len(sums) > 1:
        sums = [sums[i] + sums[i + 1] for i in range(0, len(sums), 2)]
    area = sums[0].shape[1]
    channels = sums[0].shape[0] // filters
    joined = [
        sums[0][c * filters : (c + 1) * filters] + dual_ref[:, c * area : (c + 1) * area]
        for c in range(channels)
    ]
    squares = sum(jnp.sum(w * w, axis=1, keepdims=True) for w in joined)
    spread = jnp.sqrt(squares / (channels * area))
    scale = jnp.maximum(spread, 1.0)
    for c in range(channels):
        out_ref[:, c * area : (c + 1) * area] = joined[c] / scale


def params():
    return pltpu.CompilerParams(vmem_limit_bytes=48 * 1024 * 1024)


def plain(coeff_maps, image, target, dual_rim):
    filters, band_rows, width_cols = coeff_maps.shape
    channels = image.shape[0]
    bands = lax.axis_size("band")
    height = band_rows * bands
    freqs = width_cols // bands
    table = jnp.asarray(column_table(width_cols, bands)).reshape(width_cols, bands, 2 * freqs)
    stacked = jnp.concatenate([coeff_maps, image], axis=0)
    send = jnp.einsum("mrn,nbk->brmk", stacked, table, preferred_element_type=f32)
    got = lax.all_to_all(send.astype(bf16), "band", split_axis=0, concat_axis=0)
    got = got.reshape(height, filters + channels, 2, freqs)
    ramp = jnp.arange(height, dtype=jnp.int32)
    angles = (ramp[:, None] * ramp[None, :] % height).astype(f32) * (2.0 * math.pi / height)
    factor = 1.0 / math.sqrt(height)
    lookup = jnp.stack([jnp.cos(angles) * factor, jnp.sin(angles) * factor]).astype(bf16)
    both = jnp.einsum("hmpq,tgh->ptqmg", got, lookup, preferred_element_type=f32)
    re = both[0, 0] + both[1, 1]
    im = both[1, 0] - both[0, 1]
    x_re, s_re = re[:, :filters], re[:, filters:]
    x_im, s_im = im[:, :filters], im[:, filters:]
    v_re = target[:, 0].astype(f32)
    v_im = target[:, 1].astype(f32)
    energy = jnp.sum(x_re * x_re + x_im * x_im, axis=1)
    cross_re = jnp.sum(x_re[:, None] * v_re - x_im[:, None] * v_im, axis=2)
    cross_im = jnp.sum(x_re[:, None] * v_im + x_im[:, None] * v_re, axis=2)
    sums = jnp.concatenate([cross_re, cross_im, energy[:, None]], axis=1)
    sums = lax.psum(sums.astype(bf16), "filt").astype(f32)
    denom = penalty + sums[:, 2 * channels :]
    coef_re = ((s_re - sums[:, :channels]) / denom)[:, :, None]
    coef_im = ((s_im - sums[:, channels : 2 * channels]) / denom)[:, :, None]
    d_re = v_re + x_re[:, None] * coef_re + x_im[:, None] * coef_im
    d_im = v_im + x_re[:, None] * coef_im - x_im[:, None] * coef_re
    reach = jnp.arange(K, dtype=jnp.int32)
    rows = (ramp[:, None] * reach[None, :] % height).astype(f32) * (2.0 * math.pi / height)
    cols = lax.axis_index("band") * freqs + jnp.arange(freqs, dtype=jnp.int32)
    cols = (cols[:, None] * reach[None, :] % width_cols).astype(f32) * (2.0 * math.pi / width_cols)
    turn = rows[None, :, :, None] + cols[:, None, None, :]
    factor = 1.0 / math.sqrt(height * width_cols)
    exact = lax.Precision.HIGHEST
    spatial = jnp.einsum("qcmg,qgyx->mcyx", d_re, jnp.cos(turn) * factor, precision=exact)
    spatial -= jnp.einsum("qcmg,qgyx->mcyx", d_im, jnp.sin(turn) * factor, precision=exact)
    spatial = lax.psum(spatial.reshape(dual_rim.shape), "band")
    joined = spatial + dual_rim
    spread = jnp.sqrt(jnp.mean(joined * joined, axis=1, keepdims=True))
    dict_spectra = jnp.stack([d_re, d_im], axis=1).astype(bf16)
    return (dict_spectra, joined / jnp.maximum(spread, 1.0))


def body(coeff_maps, image, target, dual_rim):
    filters, band_rows, width_cols = coeff_maps.shape
    channels = image.shape[0]
    bands = lax.axis_size("band")
    height = band_rows * bands
    freqs = width_cols // bands
    rows = (filters + channels) * band_rows
    if (2 * freqs, 2 * height, 16 % band_rows, filters % 2, bands & (bands - 1)) != (LANES, LANES, 0, 0, 0):
        return plain(coeff_maps, image, target, dual_rim)

    send = pl.pallas_call(
        columns_kernel,
        out_shape=jax.ShapeDtypeStruct((bands, rows, LANES), bf16),
        compiler_params=params(),
        name="columns",
    )(
        coeff_maps.reshape(filters * band_rows, width_cols),
        image.reshape(channels * band_rows, width_cols),
        jnp.asarray(column_table(width_cols, bands)),
    )
    got = lax.all_to_all(send, "band", split_axis=0, concat_axis=0)

    row_pair, col_pair = angle_tables(height, width_cols, K)
    first = lax.axis_index("band") * freqs
    col_mine = lax.dynamic_slice_in_dim(jnp.asarray(col_pair), first, freqs, axis=1)
    packed, inverse = pl.pallas_call(
        prepare_kernel,
        out_shape=(
            jax.ShapeDtypeStruct((freqs, channels, filters, LANES), f32),
            jax.ShapeDtypeStruct((freqs, LANES, K * K), bf16),
        ),
        compiler_params=params(),
        name="prepare",
    )(target, jnp.asarray(row_pair), col_mine)

    lines = (channels + 1) * freqs
    x, lit, own, sums = pl.pallas_call(
        rows_kernel,
        out_shape=(
            jax.ShapeDtypeStruct((freqs * filters, LANES), f32),
            jax.ShapeDtypeStruct((channels * freqs, LANES), f32),
            jax.ShapeDtypeStruct((lines, LANES), f32),
            jax.ShapeDtypeStruct((lines, LANES), bf16),
        ),
        scratch_shapes=[
            pltpu.VMEM((lines, LANES), f32),
            pltpu.VMEM((channels * freqs, LANES), f32),
        ],
        compiler_params=params(),
        name="rows",
    )(got, jnp.asarray(row_table(height, band_rows)), packed)

    peer = lax.ppermute(sums, "filt", [(0, 1), (1, 0)])

    dict_spectra, rim = pl.pallas_call(
        solve_kernel,
        out_shape=(
            jax.ShapeDtypeStruct(target.shape, bf16),
            jax.ShapeDtypeStruct((channels * filters, K * K), bf16),
        ),
        scratch_shapes=[
            pltpu.VMEM((channels * freqs, LANES), f32),
            pltpu.VMEM((channels * freqs, LANES), f32),
        ],
        compiler_params=params(),
        name="solve",
    )(x, packed, lit, own, peer, inverse)

    parts = [rim] + [
        lax.ppermute(rim, "band", [(i, i ^ k) for i in range(bands)]) for k in range(1, bands)
    ]
    dictionary = pl.pallas_call(
        finish_kernel,
        out_shape=jax.ShapeDtypeStruct(dual_rim.shape, f32),
        compiler_params=params(),
        name="finish",
    )(*parts, dual_rim)
    return (dict_spectra, dictionary)


def solution(mesh):
    placed = (
        P(("grp", "filt"), "band", None),
        P("grp", "band", None),
        P(("grp", "band"), None, None, "filt", None),
        P(("grp", "filt"), None),
    )
    return jax.shard_map(
        body,
        mesh=mesh,
        in_specs=placed,
        out_specs=(P(("grp", "band"), None, None, "filt", None), P(("grp", "filt"), None)),
        check_vma=False,
    )
```

time: 298 us -> 56.2 us (0.19)
  waiting for transfers between devices: 188 us -> 11.7 us
  local copies, waits for them, and re-layouts: 32.7 us -> 3.83 us
  matrix products: 25.6 us -> 0 us
  other arithmetic: 21.7 us -> 0 us
  Pallas kernels: 0 us -> 21.1 us
  between operations: 14.3 us -> 0.68 us
  starting transfers between devices: 11.6 us -> 18.5 us
  blocking collectives: 3.9 us -> 0 us
    all_gather x2 -> x0, waiting for transfers between devices: 179 us -> none  [the longest x1 89.9 us: body(): lax.all_gather(rim_real.astype(jnp.bfloat16), 'band', axis=0, tiled=True)]
    dot_general x7 -> x0, matrix products: 25.6 us -> none  [the longest x1 17.3 us: body(): jnp.einsum('qpcmg,gty->qpcmty', dict_full, rim_lookup, precision=lax.Prec...]
    pallas_call x0 -> x5, Pallas kernels: none -> 21.1 us  [the longest x1 7.76 us: body(): pl.pallas_call(prepare_kernel, out_shape=(jax.ShapeDtypeStruct((freqs, ch...]
    all_gather x2 -> x0, local copies, waits for them, and re-layouts: 12.7 us -> none  [the longest x1 6.36 us: body(): lax.all_gather(rim_imag.astype(jnp.bfloat16), 'band', axis=0, tiled=True)]
    ppermute x0 -> x8, starting transfers between devices: none -> 11.2 us  [the longest x7 11.1 us: body(): lax.ppermute(rim, 'band', [(i, i ^ k) for i in range(bands)])]
    convert_element_type x3 -> x0, other arithmetic: 9.85 us -> none  [the longest x1 6.37 us: body(): v_full = target.astype(jnp.float32)]
    convert_element_type x5 -> x0, local copies, waits for them, and re-layouts: 7.55 us -> none  [the longest x1 2.73 us: body(): rim_imag.astype(jnp.bfloat16)]
    all_to_all x4 -> x0, local copies, waits for them, and re-layouts: 4.87 us -> none  [the longest x2 3.35 us: body(): lax.all_to_all(col_maps, 'band', split_axis=1, concat_axis=0, tiled=True)]
  transfers between devices with their start and end apart: 4 -> 9, of which waited for: 4 -> 7; matrix products, arithmetic and copies ran while one was open for 9% -> 2% of each run, Pallas kernels for 0% -> 14%
where the time goes in v1:
time: 56.2 us; the launch traced here: 55.7 us
  Pallas kernels  21.1 us (38%)
  starting transfers between devices  18.5 us (33%)
  waiting for transfers between devices  11.7 us (21%)
  local copies, waits for them, and re-layouts  3.83 us (7%)
  between operations  0.68 us (1%)
    ppermute x7, starting transfers between devices, body(): lax.ppermute(rim, 'band', [(i, i ^ k) for i in range(bands)])  11.1 us
    pallas_call x1, Pallas kernels, body(): pl.pallas_call(prepare_kernel, out_shape=(jax.ShapeDtypeStruct((freqs, ch...  7.76 us
    pallas_call x1, Pallas kernels, body(): pl.pallas_call(solve_kernel, out_shape=(jax.ShapeDtypeStruct(target.shape...  7.64 us
    all_to_all x1, starting transfers between devices, body(): got = lax.all_to_all(send, 'band', split_axis=0, concat_axis=0)  7.25 us
    all_to_all x1, waiting for transfers between devices, body(): got = lax.all_to_all(send, 'band', split_axis=0, concat_axis=0)  6.95 us
    ppermute x7, waiting for transfers between devices, body(): lax.ppermute(rim, 'band', [(i, i ^ k) for i in range(bands)])  3.53 us
    pallas_call x1, Pallas kernels, body(): pl.pallas_call(rows_kernel, out_shape=(jax.ShapeDtypeStruct((freqs * filt...  3.13 us
    unnamed x12, local copies, waits for them, and re-layouts  2.92 us
  transfers between devices with their start and end apart: 9, of which 7 were waited for; matrix products, arithmetic and copies ran while one was open for 2% of the time, Pallas kernels for 14%

profile of v1, /device:TPU:0, one launch (start us, length us, event | category | flops | bytes accessed | tf_op | source)
XLA Modules:
  0.0 55.7 jit_solution(17521141881373654983)
XLA Ops:
  0.6 0.0 copy-start
  0.6 1.2 %copy-done = bf16[512,1024]{1,0:T(8,128)(2,1)S(1)} copy-done((bf16[512,1024]{1,0:T(8,128)(2,1)S(1)}, bf16[512,1024]{1,0:T(8,128)(2,1)}, u32[]{:S(2)}) %copy-start) | copy-done | bytes 1048600
  1.9 0.0 copy-start.1
  1.9 0.9 %copy-done.1 = bf16[32,8,512]{2,1,0:T(8,128)(2,1)S(1)} copy-done((bf16[32,8,512]{2,1,0:T(8,128)(2,1)S(1)}, bf16[32,8,512]{2,1,0:T(8,128)(2,1)}, u32[]{:S(2)}) %copy-start.1) | copy-done | bytes 262168
  2.8 0.0 copy-start.5
  2.8 0.7 %copy-done.5 = bf16[3,8,512]{2,1,0:T(8,128)(2,1)S(1)} copy-done((bf16[3,8,512]{2,1,0:T(8,128)(2,1)S(1)}, bf16[3,8,512]{2,1,0:T(8,128)(2,1)}, u32[]{:S(2)}) %copy-start.5) | copy-done | bytes 24600
  3.5 0.0 copy-start.2
  3.5 0.0 copy-start.3
  3.6 1.7 %columns.1 = bf16[8,280,128]{2,1,0:T(8,128)(2,1)} custom-call(bf16[256,512]{1,0:T(8,128)(2,1)S(1)} %bitcast.2, bf16[24,512]{1,0:T(8,128)(2,1)S(1)} %bitcast.3, bf16[512,1024]{1,0:T(8,128)(2,1)S(1)} %copy-done), custom_call_target="tpu_custom_call" | custom-call | tf_op jit(solution)/shard_map/columns/pallas_call | solution.py:264
  5.3 7.3 %all-to-all-start = ((bf16[8,280,128]{2,1,0:T(8,128)(2,1)}), bf16[8,280,128]{2,1,0:T(8,128)(2,1)}, u32[]{:S(2)}, u32[]{:S(2)}) async-start(bf16[8,280,128]{2,1,0:T(8,128)(2,1)} %columns.1), calls=%async_computation | async-start | bytes 1146880 | tf_op jit(solution)/shard_map/all_to_all | solution.py:274
  12.5 0.9 %constant_dynamic-slice_fusion.col_ref = f32[2,64,256]{2,1,0:T(8,128)S(1)} fusion(f32[2,512,256]{2,1,0:T(8,128)} %constant.21.clone, s32[]{:T(128)S(6)} %select_n.3), kind=kLoop, calls=%fused_computation | loop fusion | bytes 262148 | tf_op jit(solution)/shard_map/dynamic_slice | solution.py:278
  13.4 0.0 copy-done.2
  13.5 7.8 %prepare.1 = (f32[64,3,32,128]{3,2,1,0:T(8,128)S(1)}, bf16[64,128,256]{2,1,0:T(8,128)(2,1)}) custom-call(bf16[64,2,3,32,64]{4,3,2,1,0:T(8,128)(2,1)} %target_ref.1, f32[2,64,256]{2,1,0:T(8,128)S(1)} %copy-done.2, f32[2,64,256]{2,1,0:T(8,128)S(1)} %constant_dynamic-slice_fusion.col_ref), custom_call_target="tpu_custom_call" | custom-call | tf_op jit(solution)/shard_map/prepare/pallas_call | solution.py:279
  21.2 7.0 %all-to-all-done.got_ref = bf16[8,280,128]{2,1,0:T(8,128)(2,1)} async-done(((bf16[8,280,128]{2,1,0:T(8,128)(2,1)}), bf16[8,280,128]{2,1,0:T(8,128)(2,1)}, u32[]{:S(2)}, u32[]{:S(2)}) %all-to-all-start) | async-done | bytes 573472 | tf_op jit(solution)/shard_map/all_to_all | solution.py:274
  28.2 0.0 copy-done.3
  28.2 3.1 %rows.1 = (f32[2048,128]{1,0:T(8,128)S(1)}, f32[192,128]{1,0:T(8,128)S(1)}, f32[256,128]{1,0:T(8,128)S(1)}, bf16[256,128]{1,0:T(8,128)(2,1)S(1)}) custom-call(bf16[8,280,128]{2,1,0:T(8,128)(2,1)} %all-to-all-done.got_ref, bf16[256,256]{1,0:T(8,128)(2,1)S(1)} %copy-done.3, f32[64,3,32,128]{3,2,1,0:T(8,128)S(1)} %get-tuple-element.10.packed_ref), custom_call_target="tpu_custom_call" | custom-call | tf_op jit(solution)/shard_map/rows/pallas_call | solution.py:290
  31.3 0.1 collective-permute-start
  31.4 1.2 %collective-permute-done.peer_ref = bf16[256,128]{1,0:T(8,128)(2,1)S(1)} collective-permute-done((bf16[256,128]{1,0:T(8,128)(2,1)S(1)}, bf16[256,128]{1,0:T(8,128)(2,1)S(1)}, u32[]{:S(2)}, u32[]{:S(2)}) %collective-permute-start) | collective-permute-done | bytes 65568 | tf_op jit(solution)/shard_map/ppermute | solution.py:306
  32.6 0.0 copy-start.4
  32.6 7.6 %solve.1 = (bf16[64,2,3,32,64]{4,3,2,1,0:T(8,128)(2,1)}, bf16[96,256]{1,0:T(8,128)(2,1)S(1)}) custom-call(f32[2048,128]{1,0:T(8,128)S(1)} %get-tuple-element.11.x_ref, f32[64,3,32,128]{3,2,1,0:T(8,128)S(1)} %get-tuple-element.10.packed_ref, f32[192,128]{1,0:T(8,128)S(1)} %get-tuple-element.12.image_ref, f32[256,128]{1,0:T(8,128)S(1)} %get-tuple-element.13.own_ref, ...), custom_call_target="tpu_custom_call" | custom-call | tf_op jit(solution)/shard_map/solve/pallas_call | solution.py:308
  40.3 2.4 %collective-permute-start.7 = (bf16[96,256]{1,0:T(8,128)(2,1)S(1)}, bf16[96,256]{1,0:T(8,128)(2,1)S(1)}, u32[]{:S(2)}, u32[]{:S(2)}) collective-permute-start(bf16[96,256]{1,0:T(8,128)(2,1)S(1)} %get-tuple-element.17.refs_0_), channel_id=1, source_target_pairs={{0,14},{2,12},{4,10},{6,8},{8,6},{10,4},{12,2},{14,0},{1,15},{3,13... | collective-permute-start | bytes 147464 | tf_op jit(solution)/shard_map/ppermute | solution.py:323
  42.6 2.4 %collective-permute-start.6 = (bf16[96,256]{1,0:T(8,128)(2,1)S(1)}, bf16[96,256]{1,0:T(8,128)(2,1)S(1)}, u32[]{:S(2)}, u32[]{:S(2)}) collective-permute-start(bf16[96,256]{1,0:T(8,128)(2,1)S(1)} %get-tuple-element.17.refs_0_), channel_id=1, source_target_pairs={{0,12},{2,14},{4,8},{6,10},{8,4},{10,6},{12,0},{14,2},{1,13},{3,15... | collective-permute-start | bytes 147464 | tf_op jit(solution)/shard_map/ppermute | solution.py:323
  45.0 0.0 collective-permute-start.5
  45.0 2.9 %collective-permute-start.4 = (bf16[96,256]{1,0:T(8,128)(2,1)S(1)}, bf16[96,256]{1,0:T(8,128)(2,1)S(1)}, u32[]{:S(2)}, u32[]{:S(2)}) collective-permute-start(bf16[96,256]{1,0:T(8,128)(2,1)S(1)} %get-tuple-element.17.refs_0_), channel_id=1, source_target_pairs={{0,8},{2,10},{4,12},{6,14},{8,0},{10,2},{12,4},{14,6},{1,9},{3,11}... | collective-permute-start | bytes 147464 | tf_op jit(solution)/shard_map/ppermute | solution.py:323
  47.9 0.0 collective-permute-start.3
  47.9 0.0 collective-permute-done.7.refs_7_
  47.9 2.9 %collective-permute-start.2 = (bf16[96,256]{1,0:T(8,128)(2,1)S(1)}, bf16[96,256]{1,0:T(8,128)(2,1)S(1)}, u32[]{:S(2)}, u32[]{:S(2)}) collective-permute-start(bf16[96,256]{1,0:T(8,128)(2,1)S(1)} %get-tuple-element.17.refs_0_), channel_id=1, source_target_pairs={{0,4},{2,6},{4,0},{6,2},{8,12},{10,14},{12,8},{14,10},{1,5},{3,7},... | collective-permute-start | bytes 147464 | tf_op jit(solution)/shard_map/ppermute | solution.py:323
  50.9 0.0 collective-permute-done.6.refs_6_
  50.9 0.6 %collective-permute-start.1 = (bf16[96,256]{1,0:T(8,128)(2,1)S(1)}, bf16[96,256]{1,0:T(8,128)(2,1)S(1)}, u32[]{:S(2)}, u32[]{:S(2)}) collective-permute-start(bf16[96,256]{1,0:T(8,128)(2,1)S(1)} %get-tuple-element.17.refs_0_), channel_id=1, source_target_pairs={{0,2},{2,0},{4,6},{6,4},{8,10},{10,8},{12,14},{14,12},{1,3},{3,1},... | collective-permute-start | bytes 147464 | tf_op jit(solution)/shard_map/ppermute | solution.py:323
  51.4 0.1 collective-permute-done.5.refs_5_
  51.5 0.9 %collective-permute-done.4.refs_4_ = bf16[96,256]{1,0:T(8,128)(2,1)S(1)} collective-permute-done((bf16[96,256]{1,0:T(8,128)(2,1)S(1)}, bf16[96,256]{1,0:T(8,128)(2,1)S(1)}, u32[]{:S(2)}, u32[]{:S(2)}) %collective-permute-start.4) | collective-permute-done | bytes 49184 | tf_op jit(solution)/shard_map/ppermute | solution.py:323
  52.4 0.8 %collective-permute-done.3.refs_3_ = bf16[96,256]{1,0:T(8,128)(2,1)S(1)} collective-permute-done((bf16[96,256]{1,0:T(8,128)(2,1)S(1)}, bf16[96,256]{1,0:T(8,128)(2,1)S(1)}, u32[]{:S(2)}, u32[]{:S(2)}) %collective-permute-start.3) | collective-permute-done | bytes 49184 | tf_op jit(solution)/shard_map/ppermute | solution.py:323
  53.2 0.7 %collective-permute-done.2.refs_2_ = bf16[96,256]{1,0:T(8,128)(2,1)S(1)} collective-permute-done((bf16[96,256]{1,0:T(8,128)(2,1)S(1)}, bf16[96,256]{1,0:T(8,128)(2,1)S(1)}, u32[]{:S(2)}, u32[]{:S(2)}) %collective-permute-start.2) | collective-permute-done | bytes 49184 | tf_op jit(solution)/shard_map/ppermute | solution.py:323
  53.9 1.0 %collective-permute-done.1.refs_1_ = bf16[96,256]{1,0:T(8,128)(2,1)S(1)} collective-permute-done((bf16[96,256]{1,0:T(8,128)(2,1)S(1)}, bf16[96,256]{1,0:T(8,128)(2,1)S(1)}, u32[]{:S(2)}, u32[]{:S(2)}) %collective-permute-start.1) | collective-permute-done | bytes 49184 | tf_op jit(solution)/shard_map/ppermute | solution.py:323
  55.0 0.0 copy-done.4
  55.0 0.8 %finish.1 = f32[32,768]{1,0:T(8,128)} custom-call(bf16[96,256]{1,0:T(8,128)(2,1)S(1)} %get-tuple-element.17.refs_0_, bf16[96,256]{1,0:T(8,128)(2,1)S(1)} %collective-permute-done.1.refs_1_, bf16[96,256]{1,0:T(8,128)(2,1)S(1)} %collective-permute-done.2.refs_2_, bf16[96,256]{1,0:T(8,128)(2,1)S(1)} %collective-permute-done.3.refs_3_, ...), custom_call_target="tpu_custom_call" | custom-call | tf_op jit(solution)/shard_map/finish/pallas_call | solution.py:325
Async XLA Ops:
  0.6 1.2 %copy-start = (bf16[512,1024]{1,0:T(8,128)(2,1)S(1)}, bf16[512,1024]{1,0:T(8,128)(2,1)}, u32[]{:S(2)}) copy-start(bf16[512,1024]{1,0:T(8,128)(2,1)} %constant.20.clone.table_ref) | copy-start | bytes 3145732
  1.9 0.9 %copy-start.1 = (bf16[32,8,512]{2,1,0:T(8,128)(2,1)S(1)}, bf16[32,8,512]{2,1,0:T(8,128)(2,1)}, u32[]{:S(2)}) copy-start(bf16[32,8,512]{2,1,0:T(8,128)(2,1)} %param.8) | copy-start | bytes 786436
  2.8 0.7 %copy-start.5 = (bf16[3,8,512]{2,1,0:T(8,128)(2,1)S(1)}, bf16[3,8,512]{2,1,0:T(8,128)(2,1)}, u32[]{:S(2)}) copy-start(bf16[3,8,512]{2,1,0:T(8,128)(2,1)} %param.9) | copy-start | bytes 73732
  3.5 9.9 %copy-start.2 = (f32[2,64,256]{2,1,0:T(8,128)S(1)}, f32[2,64,256]{2,1,0:T(8,128)}, u32[]{:S(2)}) copy-start(f32[2,64,256]{2,1,0:T(8,128)} %constant.22.clone.row_ref) | copy-start | bytes 393220
  3.5 24.6 %copy-start.3 = (bf16[256,256]{1,0:T(8,128)(2,1)S(1)}, bf16[256,256]{1,0:T(8,128)(2,1)}, u32[]{:S(2)}) copy-start(bf16[256,256]{1,0:T(8,128)(2,1)} %constant.23.clone.table_ref) | copy-start | bytes 393220
  5.3 22.9 %all-to-all-start = ((bf16[8,280,128]{2,1,0:T(8,128)(2,1)}), bf16[8,280,128]{2,1,0:T(8,128)(2,1)}, u32[]{:S(2)}, u32[]{:S(2)}) async-start(bf16[8,280,128]{2,1,0:T(8,128)(2,1)} %columns.1), calls=%async_computation | async-start | bytes 1146880 | tf_op jit(solution)/shard_map/all_to_all | solution.py:274
  31.3 1.3 %collective-permute-start = (bf16[256,128]{1,0:T(8,128)(2,1)S(1)}, bf16[256,128]{1,0:T(8,128)(2,1)S(1)}, u32[]{:S(2)}, u32[]{:S(2)}) collective-permute-start(bf16[256,128]{1,0:T(8,128)(2,1)S(1)} %get-tuple-element.14), channel_id=1, source_target_pairs={{0,1},{1,0},{2,3},{3,2},{4,5},{5,4},{6,7},{7,6},{8,9},{9,8},{10,11... | collective-permute-start | bytes 196616 | tf_op jit(solution)/shard_map/ppermute | solution.py:306
  32.6 22.3 %copy-start.4 = (f32[32,768]{1,0:T(8,128)S(1)}, f32[32,768]{1,0:T(8,128)}, u32[]{:S(2)}) copy-start(f32[32,768]{1,0:T(8,128)} %refs_8_.1) | copy-start | bytes 294916
  40.3 7.7 %collective-permute-start.7 = (bf16[96,256]{1,0:T(8,128)(2,1)S(1)}, bf16[96,256]{1,0:T(8,128)(2,1)S(1)}, u32[]{:S(2)}, u32[]{:S(2)}) collective-permute-start(bf16[96,256]{1,0:T(8,128)(2,1)S(1)} %get-tuple-element.17.refs_0_), channel_id=1, source_target_pairs={{0,14},{2,12},{4,10},{6,8},{8,6},{10,4},{12,2},{14,0},{1,15},{3,13... | collective-permute-start | bytes 147464 | tf_op jit(solution)/shard_map/ppermute | solution.py:323
  42.6 8.2 %collective-permute-start.6 = (bf16[96,256]{1,0:T(8,128)(2,1)S(1)}, bf16[96,256]{1,0:T(8,128)(2,1)S(1)}, u32[]{:S(2)}, u32[]{:S(2)}) collective-permute-start(bf16[96,256]{1,0:T(8,128)(2,1)S(1)} %get-tuple-element.17.refs_0_), channel_id=1, source_target_pairs={{0,12},{2,14},{4,8},{6,10},{8,4},{10,6},{12,0},{14,2},{1,13},{3,15... | collective-permute-start | bytes 147464 | tf_op jit(solution)/shard_map/ppermute | solution.py:323
  45.0 6.5 %collective-permute-start.5 = (bf16[96,256]{1,0:T(8,128)(2,1)S(1)}, bf16[96,256]{1,0:T(8,128)(2,1)S(1)}, u32[]{:S(2)}, u32[]{:S(2)}) collective-permute-start(bf16[96,256]{1,0:T(8,128)(2,1)S(1)} %get-tuple-element.17.refs_0_), channel_id=1, source_target_pairs={{0,10},{2,8},{4,14},{6,12},{8,2},{10,0},{12,6},{14,4},{1,11},{3,9}... | collective-permute-start | bytes 147464 | tf_op jit(solution)/shard_map/ppermute | solution.py:323
  45.0 7.4 %collective-permute-start.4 = (bf16[96,256]{1,0:T(8,128)(2,1)S(1)}, bf16[96,256]{1,0:T(8,128)(2,1)S(1)}, u32[]{:S(2)}, u32[]{:S(2)}) collective-permute-start(bf16[96,256]{1,0:T(8,128)(2,1)S(1)} %get-tuple-element.17.refs_0_), channel_id=1, source_target_pairs={{0,8},{2,10},{4,12},{6,14},{8,0},{10,2},{12,4},{14,6},{1,9},{3,11}... | collective-permute-start | bytes 147464 | tf_op jit(solution)/shard_map/ppermute | solution.py:323
  47.9 5.3 %collective-permute-start.3 = (bf16[96,256]{1,0:T(8,128)(2,1)S(1)}, bf16[96,256]{1,0:T(8,128)(2,1)S(1)}, u32[]{:S(2)}, u32[]{:S(2)}) collective-permute-start(bf16[96,256]{1,0:T(8,128)(2,1)S(1)} %get-tuple-element.17.refs_0_), channel_id=1, source_target_pairs={{0,6},{2,4},{4,2},{6,0},{8,14},{10,12},{12,10},{14,8},{1,7},{3,5},... | collective-permute-start | bytes 147464 | tf_op jit(solution)/shard_map/ppermute | solution.py:323
  47.9 6.0 %collective-permute-start.2 = (bf16[96,256]{1,0:T(8,128)(2,1)S(1)}, bf16[96,256]{1,0:T(8,128)(2,1)S(1)}, u32[]{:S(2)}, u32[]{:S(2)}) collective-permute-start(bf16[96,256]{1,0:T(8,128)(2,1)S(1)} %get-tuple-element.17.refs_0_), channel_id=1, source_target_pairs={{0,4},{2,6},{4,0},{6,2},{8,12},{10,14},{12,8},{14,10},{1,5},{3,7},... | collective-permute-start | bytes 147464 | tf_op jit(solution)/shard_map/ppermute | solution.py:323
  50.9 4.1 %collective-permute-start.1 = (bf16[96,256]{1,0:T(8,128)(2,1)S(1)}, bf16[96,256]{1,0:T(8,128)(2,1)S(1)}, u32[]{:S(2)}, u32[]{:S(2)}) collective-permute-start(bf16[96,256]{1,0:T(8,128)(2,1)S(1)} %get-tuple-element.17.refs_0_), channel_id=1, source_target_pairs={{0,2},{2,0},{4,6},{6,4},{8,10},{10,8},{12,14},{14,12},{1,3},{3,1},... | collective-permute-start | bytes 147464 | tf_op jit(solution)/shard_map/ppermute | solution.py:323

commit v2 on v1

--- a/solution.py
+++ b/solution.py
@@ -11,6 +11,8 @@
 K = 16
 LANES = 128
 HALF = 64
+GROUP = 4
+CHUNKS = 8
 
 penalty = 1.0
 
@@ -23,8 +25,8 @@
     angles = (ramp[:, None] * ramp[None, :] % length) * (2.0 * math.pi / length)
     factor = 1.0 / math.sqrt(length)
     table = np.stack([np.cos(angles) * factor, -np.sin(angles) * factor], axis=1)
-    table = table.reshape(length, 2, bands, length // bands).transpose(0, 2, 1, 3)
-    return table.reshape(length, 2 * length).astype(np.float32).astype(bf16)
+    table = table.reshape(length, 2, bands, length // bands).transpose(2, 0, 1, 3)
+    return table.reshape(bands, length, 2 * length // bands).astype(np.float32).astype(bf16)
 
 
 def row_table(height, band_rows):
@@ -42,32 +44,53 @@
     return table.reshape(4 * height, 4 * height).astype(np.float32).astype(bf16)
 
 
-def angle_tables(height, columns, width):
+def inverse_table(height, columns, width, group):
     reach = np.arange(width)
     rows = (np.arange(height)[:, None] * reach[None, :] % height) * (2.0 * math.pi / height)
-    rows = np.repeat(rows, width, axis=1)
-    cols = (np.arange(columns)[:, None] * reach[None, :] % columns) * (2.0 * math.pi / columns)
-    cols = np.tile(cols, (1, width))
+    cols = (np.arange(group)[:, None] * reach[None, :] % columns) * (2.0 * math.pi / columns)
+    turn = rows[None, :, :, None] + cols[:, None, None, :]
     factor = 1.0 / math.sqrt(height * columns)
-    row_pair = np.stack([np.cos(rows) * factor, np.sin(rows) * factor])
-    col_pair = np.stack([np.cos(cols), np.sin(cols)])
-    return row_pair.astype(np.float32), col_pair.astype(np.float32)
+    cos, sin = np.cos(turn) * factor, np.sin(turn) * factor
+    table = np.stack([np.stack([cos, -sin], axis=1), np.stack([-sin, -cos], axis=1)], axis=3)
+    return table.reshape(group * 2 * height, 2 * width * width).astype(np.float32).astype(bf16)
+
+
+def turn_table(columns, width, group):
+    reach = np.arange(width)
+    first = np.arange(0, columns, group)
+    turn = (first[:, None] * reach[None, :] % columns) * (2.0 * math.pi / columns)
+    turn = np.tile(turn, (1, width))
+    return np.concatenate([np.cos(turn), np.sin(turn)], axis=1).astype(np.float32)
 
 
 def low_lanes(shape):
     return lax.broadcasted_iota(jnp.int32, shape, len(shape) - 1) < HALF
 
 
-def columns_kernel(maps_ref, image_ref, table_ref, out_ref):
+def columns_kernel(
+    maps_ref, image_ref, table_ref, out_ref, maps_in, image_in, table_in, maps_sem, image_sem, table_sem
+):
     bands = out_ref.shape[0]
     rows = maps_ref.shape[0]
+    maps_copy = pltpu.make_async_copy(maps_ref, maps_in, maps_sem)
+    image_copy = pltpu.make_async_copy(image_ref, image_in, image_sem)
+    table_copies = [
+        pltpu.make_async_copy(table_ref.at[b], table_in.at[b], table_sem.at[b]) for b in range(bands)
+    ]
+    maps_copy.start()
+    image_copy.start()
+    for copy in table_copies:
+        copy.start()
+    maps_copy.wait()
+    image_copy.wait()
     for b in range(bands):
-        table = table_ref[:, b * LANES : (b + 1) * LANES]
-        out_ref[b, :rows] = jnp.dot(maps_ref[...], table, preferred_element_type=f32).astype(bf16)
-        out_ref[b, rows:] = jnp.dot(image_ref[...], table, preferred_element_type=f32).astype(bf16)
-
-
-def prepare_kernel(target_ref, row_ref, col_ref, packed_ref, inverse_ref):
+        table_copies[b].wait()
+        table = table_in[b]
+        out_ref[b, :rows] = jnp.dot(maps_in[...], table, preferred_element_type=f32).astype(bf16)
+        out_ref[b, rows:] = jnp.dot(image_in[...], table, preferred_element_type=f32).astype(bf16)
+
+
+def prepare_kernel(target_ref, packed_ref):
     freqs, _, channels, filters, height = target_ref.shape
 
     def step(q, carry):
@@ -75,12 +98,6 @@
             packed_ref[q, c] = jnp.concatenate(
                 [target_ref[q, 0, c].astype(f32), target_ref[q, 1, c].astype(f32)], axis=-1
             )
-        cos_col = col_ref[0, pl.ds(q, 1), :]
-        sin_col = col_ref[1, pl.ds(q, 1), :]
-        cos_row = row_ref[0]
-        sin_row = row_ref[1]
-        inverse_ref[q, :height] = (cos_row * cos_col - sin_row * sin_col).astype(bf16)
-        inverse_ref[q, height:] = (-(sin_row * cos_col) - cos_row * sin_col).astype(bf16)
         return carry
 
     lax.fori_loop(0, freqs, step, 0, unroll=2)
@@ -139,9 +156,24 @@
 
 
 def solve_kernel(
-    x_ref, packed_ref, image_ref, own_ref, peer_ref, inverse_ref, out_ref, rim_ref, re_ref, im_ref
+    x_ref,
+    packed_ref,
+    image_ref,
+    own_ref,
+    peer_ref,
+    inverse_ref,
+    turn_ref,
+    out_ref,
+    rim_ref,
+    re_ref,
+    im_ref,
+    held_ref,
+    sems,
 ):
     freqs, channels, filters, _ = packed_ref.shape
+    group = inverse_ref.shape[0] // LANES
+    area = rim_ref.shape[1]
+    lines = channels * filters
     top = channels * freqs
     total = own_ref[...] + peer_ref[...].astype(f32)
     denom = penalty + total[top:]
@@ -153,31 +185,46 @@
         re_ref[span] = jnp.where(low, coef, -turned)
         im_ref[span] = jnp.where(low, turned, coef)
 
+    chunk = freqs // CHUNKS
+
+    def written(i):
+        span = pl.ds(i * chunk, chunk)
+        return pltpu.make_async_copy(held_ref.at[span], out_ref.at[span], sems.at[i])
+
     def step(i, acc):
-        sides = []
-        for k in range(2):
-            q = 2 * i + k
-            x = x_ref[pl.ds(pl.multiple_of(q * filters, filters), filters), :]
-            y = pltpu.roll(x, HALF, 1)
-            parts = []
-            for c in range(channels):
-                d = (
-                    packed_ref[q, c]
-                    + x * re_ref[pl.ds(c * freqs + q, 1), :]
-                    + y * im_ref[pl.ds(c * freqs + q, 1), :]
-                )
-                d = d.astype(bf16)
-                out_ref[q, 0, c] = d[:, :HALF]
-                out_ref[q, 1, c] = d[:, HALF:]
-                parts.append(d)
-            sides.append(jnp.concatenate(parts, axis=0))
-        left = jnp.concatenate(sides, axis=1)
-        right = inverse_ref[pl.ds(2 * i, 2)].reshape(2 * LANES, inverse_ref.shape[2])
-        return acc + jnp.dot(left, right, preferred_element_type=f32)
-
-    acc = jnp.zeros(rim_ref.shape, f32)
-    acc = lax.fori_loop(0, freqs // 2, step, acc, unroll=2)
+        blocks = []
+        for j in range(chunk // group):
+            sides = []
+            for k in range(group):
+                q = i * chunk + j * group + k
+                x = x_ref[pl.ds(pl.multiple_of(q * filters, filters), filters), :]
+                y = pltpu.roll(x, HALF, 1)
+                parts = []
+                for c in range(channels):
+                    d = (
+                        packed_ref[q, c]
+                        + x * re_ref[pl.ds(c * freqs + q, 1), :]
+                        + y * im_ref[pl.ds(c * freqs + q, 1), :]
+                    )
+                    d = d.astype(bf16)
+                    held_ref[q, 0, c] = d[:, :HALF]
+                    held_ref[q, 1, c] = d[:, HALF:]
+                    parts.append(d)
+                sides.append(jnp.concatenate(parts, axis=0))
+            blocks.append(jnp.concatenate(sides, axis=1))
+        written(i).start()
+        left = jnp.concatenate(blocks, axis=0)
+        both = jnp.dot(left, inverse_ref[...], preferred_element_type=f32)
+        for j in range(chunk // group):
+            line = i * (chunk // group) + j
+            part = both[j * lines : (j + 1) * lines] * turn_ref[pl.ds(line, 1), :]
+            acc = acc + (part[:, :area] + part[:, area:])
+        return acc
+
+    acc = lax.fori_loop(0, CHUNKS, step, jnp.zeros(rim_ref.shape, f32))
     rim_ref[...] = acc.astype(bf16)
+    for i in range(CHUNKS):
+        written(i).wait()
 
 
 def finish_kernel(*refs):
@@ -199,8 +246,16 @@
         out_ref[:, c * area : (c + 1) * area] = joined[c] / scale
 
 
-def params():
-    return pltpu.CompilerParams(vmem_limit_bytes=48 * 1024 * 1024)
+def params(mib):
+    return pltpu.CompilerParams(vmem_limit_bytes=mib * 1024 * 1024)
+
+
+def far(array):
+    return pltpu.with_memory_space_constraint(array, pltpu.HBM)
+
+
+def add_kernel(a_ref, b_ref, out_ref):
+    out_ref[...] = (a_ref[...].astype(f32) + b_ref[...].astype(f32)).astype(bf16)
 
 
 def plain(coeff_maps, image, target, dual_rim):
@@ -209,9 +264,9 @@
     bands = lax.axis_size("band")
     height = band_rows * bands
     freqs = width_cols // bands
-    table = jnp.asarray(column_table(width_cols, bands)).reshape(width_cols, bands, 2 * freqs)
+    table = jnp.asarray(column_table(width_cols, bands))
     stacked = jnp.concatenate([coeff_maps, image], axis=0)
-    send = jnp.einsum("mrn,nbk->brmk", stacked, table, preferred_element_type=f32)
+    send = jnp.einsum("mrn,bnk->brmk", stacked, table, preferred_element_type=f32)
     got = lax.all_to_all(send.astype(bf16), "band", split_axis=0, concat_axis=0)
     got = got.reshape(height, filters + channels, 2, freqs)
     ramp = jnp.arange(height, dtype=jnp.int32)
@@ -264,27 +319,33 @@
     send = pl.pallas_call(
         columns_kernel,
         out_shape=jax.ShapeDtypeStruct((bands, rows, LANES), bf16),
-        compiler_params=params(),
+        in_specs=[pl.BlockSpec(memory_space=pltpu.HBM)] * 3,
+        scratch_shapes=[
+            pltpu.VMEM((filters * band_rows, width_cols), bf16),
+            pltpu.VMEM((channels * band_rows, width_cols), bf16),
+            pltpu.VMEM((bands, width_cols, LANES), bf16),
+            pltpu.SemaphoreType.DMA,
+            pltpu.SemaphoreType.DMA,
+            pltpu.SemaphoreType.DMA((bands,)),
+        ],
+        compiler_params=params(8),
         name="columns",
     )(
-        coeff_maps.reshape(filters * band_rows, width_cols),
-        image.reshape(channels * band_rows, width_cols),
-        jnp.asarray(column_table(width_cols, bands)),
+        far(coeff_maps.reshape(filters * band_rows, width_cols)),
+        far(image.reshape(channels * band_rows, width_cols)),
+        far(jnp.asarray(column_table(width_cols, bands))),
     )
     got = lax.all_to_all(send, "band", split_axis=0, concat_axis=0)
 
-    row_pair, col_pair = angle_tables(height, width_cols, K)
-    first = lax.axis_index("band") * freqs
-    col_mine = lax.dynamic_slice_in_dim(jnp.asarray(col_pair), first, freqs, axis=1)
-    packed, inverse = pl.pallas_call(
+    groups = freqs // GROUP
+    turns = jnp.asarray(turn_table(width_cols, K, GROUP))
+    turns = lax.dynamic_slice_in_dim(turns, lax.axis_index("band") * groups, groups, axis=0)
+    packed = pl.pallas_call(
         prepare_kernel,
-        out_shape=(
-            jax.ShapeDtypeStruct((freqs, channels, filters, LANES), f32),
-            jax.ShapeDtypeStruct((freqs, LANES, K * K), bf16),
-        ),
-        compiler_params=params(),
+        out_shape=jax.ShapeDtypeStruct((freqs, channels, filters, LANES), f32),
+        compiler_params=params(12),
         name="prepare",
-    )(target, jnp.asarray(row_pair), col_mine)
+    )(target)
 
     lines = (channels + 1) * freqs
     x, lit, own, sums = pl.pallas_call(
@@ -299,7 +360,7 @@
             pltpu.VMEM((lines, LANES), f32),
             pltpu.VMEM((channels * freqs, LANES), f32),
         ],
-        compiler_params=params(),
+        compiler_params=params(8),
         name="rows",
     )(got, jnp.asarray(row_table(height, band_rows)), packed)
 
@@ -311,21 +372,31 @@
             jax.ShapeDtypeStruct(target.shape, bf16),
             jax.ShapeDtypeStruct((channels * filters, K * K), bf16),
         ),
+        out_specs=(pl.BlockSpec(memory_space=pltpu.HBM), pl.BlockSpec(memory_space=pltpu.VMEM)),
         scratch_shapes=[
             pltpu.VMEM((channels * freqs, LANES), f32),
             pltpu.VMEM((channels * freqs, LANES), f32),
+            pltpu.VMEM(target.shape, bf16),
+            pltpu.SemaphoreType.DMA((CHUNKS,)),
         ],
-        compiler_params=params(),
+        compiler_params=params(16),
         name="solve",
-    )(x, packed, lit, own, peer, inverse)
-
-    parts = [rim] + [
-        lax.ppermute(rim, "band", [(i, i ^ k) for i in range(bands)]) for k in range(1, bands)
+    )(x, packed, lit, own, peer, jnp.asarray(inverse_table(height, width_cols, K, GROUP)), turns)
+
+    near = lax.ppermute(rim, "band", [(i, i ^ 1) for i in range(bands)])
+    pair = pl.pallas_call(
+        add_kernel,
+        out_shape=jax.ShapeDtypeStruct(rim.shape, bf16),
+        compiler_params=params(4),
+        name="add",
+    )(rim, near)
+    parts = [pair] + [
+        lax.ppermute(pair, "band", [(i, i ^ k) for i in range(bands)]) for k in range(2, bands, 2)
     ]
     dictionary = pl.pallas_call(
         finish_kernel,
         out_shape=jax.ShapeDtypeStruct(dual_rim.shape, f32),
-        compiler_params=params(),
+        compiler_params=params(4),
         name="finish",
     )(*parts, dual_rim)
     return (dict_spectra, dictionary)

time: 56.2 us -> 48.1 us (0.86)
  Pallas kernels: 21.1 us -> 14.2 us
  starting transfers between devices: 18.5 us -> 13.3 us
  waiting for transfers between devices: 11.7 us -> 16.9 us
  local copies, waits for them, and re-layouts: 3.83 us -> 2.67 us
    ppermute x7 -> x4, starting transfers between devices: 11.1 us -> 5.98 us  [the longest x3 4.45 us: body(): lax.ppermute(pair, 'band', [(i, i ^ k) for i in range(bands)])]
    pallas_call x1 -> x2, Pallas kernels: 7.76 us -> 2.69 us  [the longest x1 2.67 us: body(): pl.pallas_call(prepare_kernel, out_shape=jax.ShapeDtypeStruct((freqs, cha...]
    all_to_all x1, waiting for transfers between devices: 6.95 us -> 11.1 us  [body(): got = lax.all_to_all(send, 'band', split_axis=0, concat_axis=0)]
    pallas_call x1, Pallas kernels: 7.64 us -> 3.54 us  [body(): pl.pallas_call(solve_kernel, out_shape=(jax.ShapeDtypeStruct(target.shape...]
    pallas_call x1, Pallas kernels: 1.72 us -> 4.05 us  [body(): pl.pallas_call(columns_kernel, out_shape=jax.ShapeDtypeStruct((bands, row...]
    ppermute x7 -> x4, waiting for transfers between devices: 3.53 us -> 5.32 us  [the longest x3 2.69 us: body(): lax.ppermute(pair, 'band', [(i, i ^ k) for i in range(bands)])]
    unnamed x12 -> x8, local copies, waits for them, and re-layouts: 2.92 us -> 1.9 us
    ppermute x1, waiting for transfers between devices: 1.24 us -> 0.47 us  [body(): peer = lax.ppermute(sums, 'filt', [(0, 1), (1, 0)])]
  transfers between devices with their start and end apart: 9 -> 6, of which waited for: 7 -> 5; matrix products, arithmetic and copies ran while one was open for 2% -> 2% of each run, Pallas kernels for 14% -> 6%
where the time goes in v2:
time: 48.1 us; the launch traced here: 47.8 us
  waiting for transfers between devices  16.9 us (35%)
  Pallas kernels  14.2 us (30%)
  starting transfers between devices  13.3 us (28%)
  local copies, waits for them, and re-layouts  2.67 us (6%)
  between operations  0.69 us (1%)
    all_to_all x1, waiting for transfers between devices, body(): got = lax.all_to_all(send, 'band', split_axis=0, concat_axis=0)  11.1 us
    all_to_all x1, starting transfers between devices, body(): got = lax.all_to_all(send, 'band', split_axis=0, concat_axis=0)  7.27 us
    ppermute x3, starting transfers between devices, body(): lax.ppermute(pair, 'band', [(i, i ^ k) for i in range(bands)])  4.45 us
    pallas_call x1, Pallas kernels, body(): pl.pallas_call(columns_kernel, out_shape=jax.ShapeDtypeStruct((bands, row...  4.05 us
    pallas_call x1, Pallas kernels, body(): pl.pallas_call(solve_kernel, out_shape=(jax.ShapeDtypeStruct(target.shape...  3.54 us
    pallas_call x1, Pallas kernels, body(): pl.pallas_call(rows_kernel, out_shape=(jax.ShapeDtypeStruct((freqs * filt...  3.19 us
    ppermute x3, waiting for transfers between devices, body(): lax.ppermute(pair, 'band', [(i, i ^ k) for i in range(bands)])  2.69 us
    pallas_call x1, Pallas kernels, body(): pl.pallas_call(prepare_kernel, out_shape=jax.ShapeDtypeStruct((freqs, cha...  2.67 us
  transfers between devices with their start and end apart: 6, of which 5 were waited for; matrix products, arithmetic and copies ran while one was open for 2% of the time, Pallas kernels for 6%

profile of v2, /device:TPU:0, one launch (start us, length us, event | category | flops | bytes accessed | tf_op | source)
XLA Modules:
  0.0 47.8 jit_solution(12756486200112645061)
XLA Ops:
  0.6 4.0 %columns.1 = bf16[8,280,128]{2,1,0:T(8,128)(2,1)} custom-call(bf16[256,512]{1,0:T(8,128)(2,1)} %bitcast.2, bf16[24,512]{1,0:T(8,128)(2,1)} %bitcast.3, bf16[8,512,128]{2,1,0:T(8,128)(2,1)} %constant.20.clone.table_ref), custom_call_target="tpu_custom_call" | custom-call | tf_op jit(solution)/shard_map/columns/pallas_call | solution.py:319
  4.7 7.3 %all-to-all-start = ((bf16[8,280,128]{2,1,0:T(8,128)(2,1)}), bf16[8,280,128]{2,1,0:T(8,128)(2,1)}, u32[]{:S(2)}, u32[]{:S(2)}) async-start(bf16[8,280,128]{2,1,0:T(8,128)(2,1)} %columns.1), calls=%async_computation | async-start | bytes 1146880 | tf_op jit(solution)/shard_map/all_to_all | solution.py:338
  12.0 0.0 copy-start
  12.0 1.9 %copy-done = bf16[64,2,3,32,64]{4,3,2,1,0:T(8,128)(2,1)S(1)} copy-done((bf16[64,2,3,32,64]{4,3,2,1,0:T(8,128)(2,1)S(1)}, bf16[64,2,3,32,64]{4,3,2,1,0:T(8,128)(2,1)}, u32[]{:S(2)}) %copy-start) | copy-done | bytes 1572888
  13.8 0.0 copy-start.2
  13.8 2.7 %prepare.1.packed_ref = f32[64,3,32,128]{3,2,1,0:T(8,128)S(1)} custom-call(bf16[64,2,3,32,64]{4,3,2,1,0:T(8,128)(2,1)S(1)} %copy-done), custom_call_target="tpu_custom_call" | custom-call | tf_op jit(solution)/shard_map/prepare/pallas_call | solution.py:343
  16.5 11.1 %all-to-all-done.got_ref = bf16[8,280,128]{2,1,0:T(8,128)(2,1)} async-done(((bf16[8,280,128]{2,1,0:T(8,128)(2,1)}), bf16[8,280,128]{2,1,0:T(8,128)(2,1)}, u32[]{:S(2)}, u32[]{:S(2)}) %all-to-all-start) | async-done | bytes 573472 | tf_op jit(solution)/shard_map/all_to_all | solution.py:338
  27.6 0.0 copy-done.2
  27.6 0.0 copy-start.1
  27.6 3.2 %rows.1 = (f32[2048,128]{1,0:T(8,128)S(1)}, f32[192,128]{1,0:T(8,128)S(1)}, f32[256,128]{1,0:T(8,128)S(1)}, bf16[256,128]{1,0:T(8,128)(2,1)S(1)}) custom-call(bf16[8,280,128]{2,1,0:T(8,128)(2,1)} %all-to-all-done.got_ref, bf16[256,256]{1,0:T(8,128)(2,1)S(1)} %copy-done.2, f32[64,3,32,128]{3,2,1,0:T(8,128)S(1)} %prepare.1.packed_ref), custom_call_target="tpu_custom_call" | custom-call | tf_op jit(solution)/shard_map/rows/pallas_call | solution.py:351
  30.8 0.0 copy-start.3
  30.8 0.1 collective-permute-start
  30.9 0.8 %constant_dynamic-slice_fusion.turn_ref = f32[16,512]{1,0:T(8,128)S(1)} fusion(f32[128,512]{1,0:T(8,128)} %constant.21.clone, s32[]{:T(128)S(6)} %select_n.3), kind=kLoop, calls=%fused_computation | loop fusion | bytes 65540 | tf_op jit(solution)/shard_map/dynamic_slice | solution.py:342
  31.7 0.5 collective-permute-done.peer_ref
  32.1 0.0 copy-done.1
  32.1 3.5 %solve.1 = (bf16[64,2,3,32,64]{4,3,2,1,0:T(8,128)(2,1)}, bf16[96,256]{1,0:T(8,128)(2,1)S(1)}) custom-call(f32[2048,128]{1,0:T(8,128)S(1)} %get-tuple-element.8.x_ref, f32[64,3,32,128]{3,2,1,0:T(8,128)S(1)} %prepare.1.packed_ref, f32[192,128]{1,0:T(8,128)S(1)} %get-tuple-element.9.image_ref, f32[256,128]{1,0:T(8,128)S(1)} %get-tuple-element.10.own_ref, ...), custom_call_target="tpu_custom_call" | custom-call | tf_op jit(solution)/shard_map/solve/pallas_call | solution.py:369
  35.7 1.5 %collective-permute-start.1 = (bf16[96,256]{1,0:T(8,128)(2,1)S(1)}, bf16[96,256]{1,0:T(8,128)(2,1)S(1)}, u32[]{:S(2)}, u32[]{:S(2)}) collective-permute-start(bf16[96,256]{1,0:T(8,128)(2,1)S(1)} %get-tuple-element.13.a_ref), channel_id=1, source_target_pairs={{0,2},{2,0},{4,6},{6,4},{8,10},{10,8},{12,14},{14,12},{1,3},{3,1},... | collective-permute-start | bytes 147464 | tf_op jit(solution)/shard_map/ppermute | solution.py:386
  37.2 2.6 %collective-permute-done.1.b_ref = bf16[96,256]{1,0:T(8,128)(2,1)S(1)} collective-permute-done((bf16[96,256]{1,0:T(8,128)(2,1)S(1)}, bf16[96,256]{1,0:T(8,128)(2,1)S(1)}, u32[]{:S(2)}, u32[]{:S(2)}) %collective-permute-start.1) | collective-permute-done | bytes 49184 | tf_op jit(solution)/shard_map/ppermute | solution.py:386
  39.9 1.2 %collective-permute-start.4 = (bf16[96,256]{1,0:T(8,128)(2,1)S(1)}, bf16[96,256]{1,0:T(8,128)(2,1)S(1)}, u32[]{:S(2)}, u32[]{:S(2)}) collective-permute-start(bf16[96,256]{1,0:T(8,128)(2,1)S(1)} %add.5.refs_0_), channel_id=1, source_target_pairs={{0,12},{2,14},{4,8},{6,10},{8,4},{10,6},{12,0},{14,2},{1,13},{3,15... | collective-permute-start | bytes 147464 | tf_op jit(solution)/shard_map/ppermute | solution.py:394
  41.1 1.0 %collective-permute-start.3 = (bf16[96,256]{1,0:T(8,128)(2,1)S(1)}, bf16[96,256]{1,0:T(8,128)(2,1)S(1)}, u32[]{:S(2)}, u32[]{:S(2)}) collective-permute-start(bf16[96,256]{1,0:T(8,128)(2,1)S(1)} %add.5.refs_0_), channel_id=1, source_target_pairs={{0,8},{2,10},{4,12},{6,14},{8,0},{10,2},{12,4},{14,6},{1,9},{3,11}... | collective-permute-start | bytes 147464 | tf_op jit(solution)/shard_map/ppermute | solution.py:394
  42.1 2.2 %collective-permute-start.2 = (bf16[96,256]{1,0:T(8,128)(2,1)S(1)}, bf16[96,256]{1,0:T(8,128)(2,1)S(1)}, u32[]{:S(2)}, u32[]{:S(2)}) collective-permute-start(bf16[96,256]{1,0:T(8,128)(2,1)S(1)} %add.5.refs_0_), channel_id=1, source_target_pairs={{0,4},{2,6},{4,0},{6,2},{8,12},{10,14},{12,8},{14,10},{1,5},{3,7},... | collective-permute-start | bytes 147464 | tf_op jit(solution)/shard_map/ppermute | solution.py:394
  44.3 1.6 %collective-permute-done.4.refs_3_ = bf16[96,256]{1,0:T(8,128)(2,1)S(1)} collective-permute-done((bf16[96,256]{1,0:T(8,128)(2,1)S(1)}, bf16[96,256]{1,0:T(8,128)(2,1)S(1)}, u32[]{:S(2)}, u32[]{:S(2)}) %collective-permute-start.4) | collective-permute-done | bytes 49184 | tf_op jit(solution)/shard_map/ppermute | solution.py:394
  45.9 1.1 %collective-permute-done.3.refs_2_ = bf16[96,256]{1,0:T(8,128)(2,1)S(1)} collective-permute-done((bf16[96,256]{1,0:T(8,128)(2,1)S(1)}, bf16[96,256]{1,0:T(8,128)(2,1)S(1)}, u32[]{:S(2)}, u32[]{:S(2)}) %collective-permute-start.3) | collective-permute-done | bytes 49184 | tf_op jit(solution)/shard_map/ppermute | solution.py:394
  47.0 0.0 collective-permute-done.2.refs_1_
  47.0 0.0 copy-done.3
  47.0 0.8 %finish.1 = f32[32,768]{1,0:T(8,128)} custom-call(bf16[96,256]{1,0:T(8,128)(2,1)S(1)} %add.5.refs_0_, bf16[96,256]{1,0:T(8,128)(2,1)S(1)} %collective-permute-done.2.refs_1_, bf16[96,256]{1,0:T(8,128)(2,1)S(1)} %collective-permute-done.3.refs_2_, bf16[96,256]{1,0:T(8,128)(2,1)S(1)} %collective-permute-done.4.refs_3_, f32[32,768]{1,0:T(8,128)S(1)} %copy-done.3), custom_call_target="tpu_custom_call" | custom-call | tf_op jit(solution)/shard_map/finish/pallas_call | solution.py:396
  (1 shorter events, 0.0 us)
Async XLA Ops:
  4.7 22.9 %all-to-all-start = ((bf16[8,280,128]{2,1,0:T(8,128)(2,1)}), bf16[8,280,128]{2,1,0:T(8,128)(2,1)}, u32[]{:S(2)}, u32[]{:S(2)}) async-start(bf16[8,280,128]{2,1,0:T(8,128)(2,1)} %columns.1), calls=%async_computation | async-start | bytes 1146880 | tf_op jit(solution)/shard_map/all_to_all | solution.py:338
  12.0 1.9 %copy-start = (bf16[64,2,3,32,64]{4,3,2,1,0:T(8,128)(2,1)S(1)}, bf16[64,2,3,32,64]{4,3,2,1,0:T(8,128)(2,1)}, u32[]{:S(2)}) copy-start(bf16[64,2,3,32,64]{4,3,2,1,0:T(8,128)(2,1)} %target_ref.1) | copy-start | bytes 4718596
  13.8 13.8 %copy-start.2 = (bf16[256,256]{1,0:T(8,128)(2,1)S(1)}, bf16[256,256]{1,0:T(8,128)(2,1)}, u32[]{:S(2)}) copy-start(bf16[256,256]{1,0:T(8,128)(2,1)} %constant.22.clone.table_ref) | copy-start | bytes 393220
  27.6 4.5 %copy-start.1 = (bf16[512,512]{1,0:T(8,128)(2,1)S(1)}, bf16[512,512]{1,0:T(8,128)(2,1)}, u32[]{:S(2)}) copy-start(bf16[512,512]{1,0:T(8,128)(2,1)} %constant.23.clone.inverse_ref) | copy-start | bytes 1572868
  30.8 16.2 %copy-start.3 = (f32[32,768]{1,0:T(8,128)S(1)}, f32[32,768]{1,0:T(8,128)}, u32[]{:S(2)}) copy-start(f32[32,768]{1,0:T(8,128)} %refs_4_.1) | copy-start | bytes 294916
  30.8 1.3 %collective-permute-start = (bf16[256,128]{1,0:T(8,128)(2,1)S(1)}, bf16[256,128]{1,0:T(8,128)(2,1)S(1)}, u32[]{:S(2)}, u32[]{:S(2)}) collective-permute-start(bf16[256,128]{1,0:T(8,128)(2,1)S(1)} %get-tuple-element.11), channel_id=1, source_target_pairs={{0,1},{1,0},{2,3},{3,2},{4,5},{5,4},{6,7},{7,6},{8,9},{9,8},{10,11... | collective-permute-start | bytes 196616 | tf_op jit(solution)/shard_map/ppermute | solution.py:367
  35.7 4.2 %collective-permute-start.1 = (bf16[96,256]{1,0:T(8,128)(2,1)S(1)}, bf16[96,256]{1,0:T(8,128)(2,1)S(1)}, u32[]{:S(2)}, u32[]{:S(2)}) collective-permute-start(bf16[96,256]{1,0:T(8,128)(2,1)S(1)} %get-tuple-element.13.a_ref), channel_id=1, source_target_pairs={{0,2},{2,0},{4,6},{6,4},{8,10},{10,8},{12,14},{14,12},{1,3},{3,1},... | collective-permute-start | bytes 147464 | tf_op jit(solution)/shard_map/ppermute | solution.py:386
  39.9 6.1 %collective-permute-start.4 = (bf16[96,256]{1,0:T(8,128)(2,1)S(1)}, bf16[96,256]{1,0:T(8,128)(2,1)S(1)}, u32[]{:S(2)}, u32[]{:S(2)}) collective-permute-start(bf16[96,256]{1,0:T(8,128)(2,1)S(1)} %add.5.refs_0_), channel_id=1, source_target_pairs={{0,12},{2,14},{4,8},{6,10},{8,4},{10,6},{12,0},{14,2},{1,13},{3,15... | collective-permute-start | bytes 147464 | tf_op jit(solution)/shard_map/ppermute | solution.py:394
  41.1 5.9 %collective-permute-start.3 = (bf16[96,256]{1,0:T(8,128)(2,1)S(1)}, bf16[96,256]{1,0:T(8,128)(2,1)S(1)}, u32[]{:S(2)}, u32[]{:S(2)}) collective-permute-start(bf16[96,256]{1,0:T(8,128)(2,1)S(1)} %add.5.refs_0_), channel_id=1, source_target_pairs={{0,8},{2,10},{4,12},{6,14},{8,0},{10,2},{12,4},{14,6},{1,9},{3,11}... | collective-permute-start | bytes 147464 | tf_op jit(solution)/shard_map/ppermute | solution.py:394
  42.1 4.9 %collective-permute-start.2 = (bf16[96,256]{1,0:T(8,128)(2,1)S(1)}, bf16[96,256]{1,0:T(8,128)(2,1)S(1)}, u32[]{:S(2)}, u32[]{:S(2)}) collective-permute-start(bf16[96,256]{1,0:T(8,128)(2,1)S(1)} %add.5.refs_0_), channel_id=1, source_target_pairs={{0,4},{2,6},{4,0},{6,2},{8,12},{10,14},{12,8},{14,10},{1,5},{3,7},... | collective-permute-start | bytes 147464 | tf_op jit(solution)/shard_map/ppermute | solution.py:394

commit v3 on v2

--- a/solution.py
+++ b/solution.py
@@ -41,7 +41,8 @@
     table = np.zeros((2, height // band_rows, 2, band_rows, 2, 2 * height))
     table[:, :, 0, :, 0] = both
     table[:, :, 1, :, 1] = both
-    return table.reshape(4 * height, 4 * height).astype(np.float32).astype(bf16)
+    table = table.reshape(2, height // band_rows, 2 * band_rows, 4 * height)
+    return table.astype(np.float32).astype(bf16)
 
 
 def inverse_table(height, columns, width, group):
@@ -63,19 +64,31 @@
     return np.concatenate([np.cos(turn), np.sin(turn)], axis=1).astype(np.float32)
 
 
+def far_first(bands):
+    if bands == 8:
+        return [4, 2, 6, 5, 3, 7, 1, 0]
+    return list(range(bands - 1, -1, -1))
+
+
 def low_lanes(shape):
     return lax.broadcasted_iota(jnp.int32, shape, len(shape) - 1) < HALF
 
 
-def columns_kernel(
-    maps_ref, image_ref, table_ref, out_ref, maps_in, image_in, table_in, maps_sem, image_sem, table_sem
-):
-    bands = out_ref.shape[0]
+def columns_kernel(maps_ref, image_ref, table_ref, *refs):
+    out_refs = refs[:-4]
+    lines_in, table_in, line_sem, table_sem = refs[-4:]
+    bands = len(out_refs)
     rows = maps_ref.shape[0]
-    maps_copy = pltpu.make_async_copy(maps_ref, maps_in, maps_sem)
-    image_copy = pltpu.make_async_copy(image_ref, image_in, image_sem)
+    mine = lax.axis_index("band")
+    maps_copy = pltpu.make_async_copy(maps_ref, lines_in.at[:rows], line_sem.at[0])
+    image_copy = pltpu.make_async_copy(image_ref, lines_in.at[rows:], line_sem.at[1])
     table_copies = [
-        pltpu.make_async_copy(table_ref.at[b], table_in.at[b], table_sem.at[b]) for b in range(bands)
+        pltpu.make_async_copy(
+            table_ref.at[mine ^ k],
+            table_in.at[i // 2, :, i % 2 * LANES : (i % 2 + 1) * LANES],
+            table_sem.at[i],
+        )
+        for i, k in enumerate(far_first(bands))
     ]
     maps_copy.start()
     image_copy.start()
@@ -83,35 +96,50 @@
         copy.start()
     maps_copy.wait()
     image_copy.wait()
-    for b in range(bands):
-        table_copies[b].wait()
-        table = table_in[b]
-        out_ref[b, :rows] = jnp.dot(maps_in[...], table, preferred_element_type=f32).astype(bf16)
-        out_ref[b, rows:] = jnp.dot(image_in[...], table, preferred_element_type=f32).astype(bf16)
-
-
-def prepare_kernel(target_ref, packed_ref):
+    for i in range(0, bands, 2):
+        table_copies[i].wait()
+        table_copies[i + 1].wait()
+        both = jnp.dot(lines_in[...], table_in[i // 2], preferred_element_type=f32).astype(bf16)
+        out_refs[i][...] = both[:, :LANES]
+        out_refs[i + 1][...] = both[:, LANES:]
+
+
+def prepare_kernel(target_ref, packed_ref, target_in, sems):
     freqs, _, channels, filters, height = target_ref.shape
-
-    def step(q, carry):
-        for c in range(channels):
-            packed_ref[q, c] = jnp.concatenate(
-                [target_ref[q, 0, c].astype(f32), target_ref[q, 1, c].astype(f32)], axis=-1
-            )
+    chunk = freqs // CHUNKS
+
+    def fetched(i):
+        span = pl.ds(i * chunk, chunk)
+        return pltpu.make_async_copy(target_ref.at[span], target_in.at[span], sems.at[i])
+
+    for i in range(CHUNKS):
+        fetched(i).start()
+
+    def step(i, carry):
+        fetched(i).wait()
+        for j in range(chunk):
+            q = i * chunk + j
+            for c in range(channels):
+                packed_ref[q, c] = jnp.concatenate(
+                    [target_in[q, 0, c].astype(f32), target_in[q, 1, c].astype(f32)], axis=-1
+                )
         return carry
 
-    lax.fori_loop(0, freqs, step, 0, unroll=2)
-
-
-def rows_kernel(got_ref, table_ref, packed_ref, x_ref, image_ref, own_ref, send_ref, one_ref, two_ref):
+    lax.fori_loop(0, CHUNKS, step, 0)
+
+
+def rows_kernel(*refs):
+    got_refs = refs[:-8]
+    table_ref, packed_ref, x_ref, image_ref, own_ref, send_ref, one_ref, two_ref = refs[-8:]
     freqs, channels, filters, _ = packed_ref.shape
-    sources, rows, _ = got_ref.shape
-    band_rows = rows // (filters + channels)
+    sources = len(got_refs)
+    band_rows = got_refs[0].shape[0] // (filters + channels)
     pair = 2 * band_rows
-    table = table_ref[...]
+    mine = lax.axis_index("band")
+    table = jnp.concatenate([table_ref[p, mine ^ k] for p in range(2) for k in far_first(sources)], axis=0)
 
     def transform(start):
-        block = got_ref[:, start : start + pair, :].reshape(sources * pair, LANES)
+        block = jnp.concatenate([ref[start : start + pair, :] for ref in got_refs], axis=0)
         turned = block.T
         left = jnp.concatenate([turned[:freqs], turned[freqs:]], axis=1)
         return jnp.dot(left, table, preferred_element_type=f32)
@@ -186,6 +214,7 @@
         im_ref[span] = jnp.where(low, turned, coef)
 
     chunk = freqs // CHUNKS
+    mine = lax.axis_index("band")
 
     def written(i):
         span = pl.ds(i * chunk, chunk)
@@ -217,7 +246,7 @@
         both = jnp.dot(left, inverse_ref[...], preferred_element_type=f32)
         for j in range(chunk // group):
             line = i * (chunk // group) + j
-            part = both[j * lines : (j + 1) * lines] * turn_ref[pl.ds(line, 1), :]
+            part = both[j * lines : (j + 1) * lines] * turn_ref[mine, pl.ds(line, 1), :]
             acc = acc + (part[:, :area] + part[:, area:])
         return acc
 
@@ -316,16 +345,17 @@
     if (2 * freqs, 2 * height, 16 % band_rows, filters % 2, bands & (bands - 1)) != (LANES, LANES, 0, 0, 0):
         return plain(coeff_maps, image, target, dual_rim)
 
-    send = pl.pallas_call(
+    def swap(array, k):
+        return lax.ppermute(array, "band", [(i, i ^ k) for i in range(bands)])
+
+    chunks = pl.pallas_call(
         columns_kernel,
-        out_shape=jax.ShapeDtypeStruct((bands, rows, LANES), bf16),
+        out_shape=(jax.ShapeDtypeStruct((rows, LANES), bf16),) * bands,
         in_specs=[pl.BlockSpec(memory_space=pltpu.HBM)] * 3,
         scratch_shapes=[
-            pltpu.VMEM((filters * band_rows, width_cols), bf16),
-            pltpu.VMEM((channels * band_rows, width_cols), bf16),
-            pltpu.VMEM((bands, width_cols, LANES), bf16),
-            pltpu.SemaphoreType.DMA,
-            pltpu.SemaphoreType.DMA,
+            pltpu.VMEM((rows, width_cols), bf16),
+            pltpu.VMEM((bands // 2, width_cols, 2 * LANES), bf16),
+            pltpu.SemaphoreType.DMA((2,)),
             pltpu.SemaphoreType.DMA((bands,)),
         ],
         compiler_params=params(8),
@@ -335,17 +365,17 @@
         far(image.reshape(channels * band_rows, width_cols)),
         far(jnp.asarray(column_table(width_cols, bands))),
     )
-    got = lax.all_to_all(send, "band", split_axis=0, concat_axis=0)
-
-    groups = freqs // GROUP
-    turns = jnp.asarray(turn_table(width_cols, K, GROUP))
-    turns = lax.dynamic_slice_in_dim(turns, lax.axis_index("band") * groups, groups, axis=0)
+    got = [swap(chunk, k) if k else chunk for k, chunk in zip(far_first(bands), chunks)]
+
+    turns = turn_table(width_cols, K, GROUP).reshape(bands, freqs // GROUP, 2 * K * K)
     packed = pl.pallas_call(
         prepare_kernel,
         out_shape=jax.ShapeDtypeStruct((freqs, channels, filters, LANES), f32),
+        in_specs=[pl.BlockSpec(memory_space=pltpu.HBM)],
+        scratch_shapes=[pltpu.VMEM(target.shape, bf16), pltpu.SemaphoreType.DMA((CHUNKS,))],
         compiler_params=params(12),
         name="prepare",
-    )(target)
+    )(far(target))
 
     lines = (channels + 1) * freqs
     x, lit, own, sums = pl.pallas_call(
@@ -362,7 +392,7 @@
         ],
         compiler_params=params(8),
         name="rows",
-    )(got, jnp.asarray(row_table(height, band_rows)), packed)
+    )(*got, jnp.asarray(row_table(height, band_rows)), packed)
 
     peer = lax.ppermute(sums, "filt", [(0, 1), (1, 0)])
 
@@ -381,18 +411,16 @@
         ],
         compiler_params=params(16),
         name="solve",
-    )(x, packed, lit, own, peer, jnp.asarray(inverse_table(height, width_cols, K, GROUP)), turns)
-
-    near = lax.ppermute(rim, "band", [(i, i ^ 1) for i in range(bands)])
+    )(x, packed, lit, own, peer, jnp.asarray(inverse_table(height, width_cols, K, GROUP)), jnp.asarray(turns))
+
+    near = swap(rim, 1)
     pair = pl.pallas_call(
         add_kernel,
         out_shape=jax.ShapeDtypeStruct(rim.shape, bf16),
         compiler_params=params(4),
         name="add",
     )(rim, near)
-    parts = [pair] + [
-        lax.ppermute(pair, "band", [(i, i ^ k) for i in range(bands)]) for k in range(2, bands, 2)
-    ]
+    parts = [pair] + [swap(pair, k) for k in range(2, bands, 2)]
     dictionary = pl.pallas_call(
         finish_kernel,
         out_shape=jax.ShapeDtypeStruct(dual_rim.shape, f32),

time: 48.1 us -> 42.2 us (0.88)
  starting transfers between devices: 13.3 us -> 21 us
  waiting for transfers between devices: 16.9 us -> 9.2 us
  Pallas kernels: 14.2 us -> 11.1 us
  local copies, waits for them, and re-layouts: 2.67 us -> 0.02 us
    ppermute x4 -> x11, starting transfers between devices: 5.98 us -> 21 us  [swap(): return lax.ppermute(array, 'band', [(i, i ^ k) for i in range(bands)])]
    all_to_all x1 -> x0, waiting for transfers between devices: 11.1 us -> none  [body(): got = lax.all_to_all(send, 'band', split_axis=0, concat_axis=0)]
    all_to_all x1 -> x0, starting transfers between devices: 7.27 us -> none  [body(): got = lax.all_to_all(send, 'band', split_axis=0, concat_axis=0)]
    ppermute x4 -> x11, waiting for transfers between devices: 5.32 us -> 7.96 us  [swap(): return lax.ppermute(array, 'band', [(i, i ^ k) for i in range(bands)])]
    unnamed x8, local copies, waits for them, and re-layouts: 1.9 us -> 0.02 us
    pallas_call x1, Pallas kernels: 4.05 us -> 2.6 us  [body(): pl.pallas_call(columns_kernel, out_shape=(jax.ShapeDtypeStruct((rows, LAN...]
    pallas_call x1, Pallas kernels: 3.19 us -> 2.07 us  [body(): pl.pallas_call(rows_kernel, out_shape=(jax.ShapeDtypeStruct((freqs * filt...]
    ppermute x1, waiting for transfers between devices: 0.47 us -> 1.24 us  [body(): peer = lax.ppermute(sums, 'filt', [(0, 1), (1, 0)])]
  transfers between devices with their start and end apart: 6 -> 12, of which waited for: 5 -> 6; matrix products, arithmetic and copies ran while one was open for 2% -> 0% of each run, Pallas kernels for 6% -> 5%
where the time goes in v3:
time: 42.2 us; the launch traced here: 42 us
  starting transfers between devices  21 us (50%)
  Pallas kernels  11.1 us (26%)
  waiting for transfers between devices  9.2 us (22%)
  between operations  0.73 us (2%)
    ppermute x11, starting transfers between devices, swap(): return lax.ppermute(array, 'band', [(i, i ^ k) for i in range(bands)])  21 us
    ppermute x11, waiting for transfers between devices, swap(): return lax.ppermute(array, 'band', [(i, i ^ k) for i in range(bands)])  7.96 us
    pallas_call x1, Pallas kernels, body(): pl.pallas_call(solve_kernel, out_shape=(jax.ShapeDtypeStruct(target.shape...  3.55 us
    pallas_call x1, Pallas kernels, body(): pl.pallas_call(columns_kernel, out_shape=(jax.ShapeDtypeStruct((rows, LAN...  2.6 us
    pallas_call x1, Pallas kernels, body(): pl.pallas_call(rows_kernel, out_shape=(jax.ShapeDtypeStruct((freqs * filt...  2.07 us
    pallas_call x1, Pallas kernels, body(): pl.pallas_call(prepare_kernel, out_shape=jax.ShapeDtypeStruct((freqs, cha...  2.05 us
    ppermute x1, waiting for transfers between devices, body(): peer = lax.ppermute(sums, 'filt', [(0, 1), (1, 0)])  1.24 us
  transfers between devices with their start and end apart: 12, of which 6 were waited for; matrix products, arithmetic and copies ran while one was open for 0% of the time, Pallas kernels for 5%

profile of v3, /device:TPU:0, one launch (start us, length us, event | category | flops | bytes accessed | tf_op | source)
XLA Modules:
  0.0 42.0 jit_solution(7555621108889949621)
XLA Ops:
  0.6 2.6 %columns.1 = (bf16[280,128]{1,0:T(8,128)(2,1)S(1)}, bf16[280,128]{1,0:T(8,128)(2,1)S(1)}, bf16[280,128]{1,0:T(8,128)(2,1)S(1)}, bf16[280,128]{1,0:T(8,128)(2,1)S...) custom-call(bf16[256,512]{1,0:T(8,128)(2,1)} %bitcast.2, ...), custom_call_target="tpu_custom_call" | custom-call | tf_op jit(solution)/shard_map/columns/pallas_call | solution.py:351
  3.2 4.1 %collective-permute-start = (bf16[280,128]{1,0:T(8,128)(2,1)S(1)}, bf16[280,128]{1,0:T(8,128)(2,1)S(1)}, u32[]{:S(2)}, u32[]{:S(2)}) collective-permute-start(bf16[280,128]{1,0:T(8,128)(2,1)S(1)} %get-tuple-element.16), channel_id=1, source_target_pairs={{0,8},{2,10},{4,12},{6,14},{8,0},{10,2},{12,4},{14,6},{1,9},{3,11}... | collective-permute-start | bytes 215048 | tf_op jit(solution)/shard_map/ppermute | solution.py:349
  7.3 1.6 %collective-permute-start.1 = (bf16[280,128]{1,0:T(8,128)(2,1)S(1)}, bf16[280,128]{1,0:T(8,128)(2,1)S(1)}, u32[]{:S(2)}, u32[]{:S(2)}) collective-permute-start(bf16[280,128]{1,0:T(8,128)(2,1)S(1)} %get-tuple-element.17), channel_id=1, source_target_pairs={{0,4},{2,6},{4,0},{6,2},{8,12},{10,14},{12,8},{14,10},{1,5},{3,7},... | collective-permute-start | bytes 215048 | tf_op jit(solution)/shard_map/ppermute | solution.py:349
  8.9 0.0 collective-permute-start.2
  8.9 2.8 %collective-permute-start.3 = (bf16[280,128]{1,0:T(8,128)(2,1)S(1)}, bf16[280,128]{1,0:T(8,128)(2,1)S(1)}, u32[]{:S(2)}, u32[]{:S(2)}) collective-permute-start(bf16[280,128]{1,0:T(8,128)(2,1)S(1)} %get-tuple-element.19), channel_id=1, source_target_pairs={{0,10},{2,8},{4,14},{6,12},{8,2},{10,0},{12,6},{14,4},{1,11},{3,9}... | collective-permute-start | bytes 215048 | tf_op jit(solution)/shard_map/ppermute | solution.py:349
  11.8 2.4 %collective-permute-start.4 = (bf16[280,128]{1,0:T(8,128)(2,1)S(1)}, bf16[280,128]{1,0:T(8,128)(2,1)S(1)}, u32[]{:S(2)}, u32[]{:S(2)}) collective-permute-start(bf16[280,128]{1,0:T(8,128)(2,1)S(1)} %get-tuple-element.20), channel_id=1, source_target_pairs={{0,6},{2,4},{4,2},{6,0},{8,14},{10,12},{12,10},{14,8},{1,7},{3,5},... | collective-permute-start | bytes 215048 | tf_op jit(solution)/shard_map/ppermute | solution.py:349
  14.2 0.0 collective-permute-done.refs_0_
  14.2 4.1 %collective-permute-start.5 = (bf16[280,128]{1,0:T(8,128)(2,1)S(1)}, bf16[280,128]{1,0:T(8,128)(2,1)S(1)}, u32[]{:S(2)}, u32[]{:S(2)}) collective-permute-start(bf16[280,128]{1,0:T(8,128)(2,1)S(1)} %get-tuple-element.21), channel_id=1, source_target_pairs={{0,14},{2,12},{4,10},{6,8},{8,6},{10,4},{12,2},{14,0},{1,15},{3,13... | collective-permute-start | bytes 215048 | tf_op jit(solution)/shard_map/ppermute | solution.py:349
  18.3 0.0 collective-permute-done.1.refs_1_
  18.3 0.0 copy-start.2
  18.3 0.5 %collective-permute-start.6 = (bf16[280,128]{1,0:T(8,128)(2,1)S(1)}, bf16[280,128]{1,0:T(8,128)(2,1)S(1)}, u32[]{:S(2)}, u32[]{:S(2)}) collective-permute-start(bf16[280,128]{1,0:T(8,128)(2,1)S(1)} %get-tuple-element.22), channel_id=1, source_target_pairs={{0,2},{2,0},{4,6},{6,4},{8,10},{10,8},{12,14},{14,12},{1,3},{3,1},... | collective-permute-start | bytes 215048 | tf_op jit(solution)/shard_map/ppermute | solution.py:349
  18.9 2.0 %prepare.1.refs_9_.packed_ref = f32[64,3,32,128]{3,2,1,0:T(8,128)S(1)} custom-call(bf16[64,2,3,32,64]{4,3,2,1,0:T(8,128)(2,1)} %target_ref.1), custom_call_target="tpu_custom_call" | custom-call | tf_op jit(solution)/shard_map/prepare/pallas_call | solution.py:371
  20.9 0.0 copy-start
  20.9 0.0 copy-start.1
  20.9 0.0 collective-permute-done.2.refs_2_
  21.0 0.0 collective-permute-done.3.refs_3_
  21.0 0.0 collective-permute-done.4.refs_4_
  21.0 0.4 collective-permute-done.5.refs_5_
  21.3 1.3 %collective-permute-done.6.refs_6_ = bf16[280,128]{1,0:T(8,128)(2,1)S(1)} collective-permute-done((bf16[280,128]{1,0:T(8,128)(2,1)S(1)}, bf16[280,128]{1,0:T(8,128)(2,1)S(1)}, u32[]{:S(2)}, u32[]{:S(2)}) %collective-permute-start.6) | collective-permute-done | bytes 71712 | tf_op jit(solution)/shard_map/ppermute | solution.py:349
  22.7 0.0 copy-done.2
  22.7 2.1 %rows.1 = (f32[2048,128]{1,0:T(8,128)S(1)}, f32[192,128]{1,0:T(8,128)S(1)}, f32[256,128]{1,0:T(8,128)S(1)}, bf16[256,128]{1,0:T(8,128)(2,1)S(1)}) custom-call(bf16[280,128]{1,0:T(8,128)(2,1)S(1)} %collective-permute-done.refs_0_, bf16[280,128]{1,0:T(8,128)(2,1)S(1)} %collective-permute-done.1.refs_1_, bf16[280,128]{1,0:T(8,128)(2,1)S(1)} %collective-permute-done.2.refs_2_, ...), custom_call_target="tpu_custom_call" | custom-call | tf_op jit(solution)/shard_map/rows/pallas_call | solution.py:381
  24.8 0.0 copy-start.3
  24.8 0.1 collective-permute-start.7
  24.8 1.2 %collective-permute-done.7.peer_ref = bf16[256,128]{1,0:T(8,128)(2,1)S(1)} collective-permute-done((bf16[256,128]{1,0:T(8,128)(2,1)S(1)}, bf16[256,128]{1,0:T(8,128)(2,1)S(1)}, u32[]{:S(2)}, u32[]{:S(2)}) %collective-permute-start.7) | collective-permute-done | bytes 65568 | tf_op jit(solution)/shard_map/ppermute | solution.py:397
  26.1 0.0 copy-done
  26.1 0.0 copy-done.1
  26.1 3.6 %solve.1 = (bf16[64,2,3,32,64]{4,3,2,1,0:T(8,128)(2,1)}, bf16[96,256]{1,0:T(8,128)(2,1)S(1)}) custom-call(f32[2048,128]{1,0:T(8,128)S(1)} %get-tuple-element.24.x_ref, f32[64,3,32,128]{3,2,1,0:T(8,128)S(1)} %prepare.1.refs_9_.packed_ref, f32[192,128]{1,0:T(8,128)S(1)} %get-tuple-element.25.image_ref, f32[256,128]{1,0:T(8,128)S(1)} %get-tuple-element.26.own_ref, ...), custom_call_target="tpu_custom_call" | custom-call | tf_op jit(solution)/shard_map/solve/pallas_call | solution.py:399
  29.6 0.9 %collective-permute-start.8 = (bf16[96,256]{1,0:T(8,128)(2,1)S(1)}, bf16[96,256]{1,0:T(8,128)(2,1)S(1)}, u32[]{:S(2)}, u32[]{:S(2)}) collective-permute-start(bf16[96,256]{1,0:T(8,128)(2,1)S(1)} %get-tuple-element.29.a_ref), channel_id=1, source_target_pairs={{0,2},{2,0},{4,6},{6,4},{8,10},{10,8},{12,14},{14,12},{1,3},{3,1},... | collective-permute-start | bytes 147464 | tf_op jit(solution)/shard_map/ppermute | solution.py:349
  30.5 3.3 %collective-permute-done.8.b_ref = bf16[96,256]{1,0:T(8,128)(2,1)S(1)} collective-permute-done((bf16[96,256]{1,0:T(8,128)(2,1)S(1)}, bf16[96,256]{1,0:T(8,128)(2,1)S(1)}, u32[]{:S(2)}, u32[]{:S(2)}) %collective-permute-start.8) | collective-permute-done | bytes 49184 | tf_op jit(solution)/shard_map/ppermute | solution.py:349
  33.8 1.9 %collective-permute-start.11 = (bf16[96,256]{1,0:T(8,128)(2,1)S(1)}, bf16[96,256]{1,0:T(8,128)(2,1)S(1)}, u32[]{:S(2)}, u32[]{:S(2)}) collective-permute-start(bf16[96,256]{1,0:T(8,128)(2,1)S(1)} %add.1.refs_0_), channel_id=1, source_target_pairs={{0,12},{2,14},{4,8},{6,10},{8,4},{10,6},{12,0},{14,2},{1,13},{3,15... | collective-permute-start | bytes 147464 | tf_op jit(solution)/shard_map/ppermute | solution.py:349
  35.8 0.0 collective-permute-start.10
  35.8 2.5 %collective-permute-start.9 = (bf16[96,256]{1,0:T(8,128)(2,1)S(1)}, bf16[96,256]{1,0:T(8,128)(2,1)S(1)}, u32[]{:S(2)}, u32[]{:S(2)}) collective-permute-start(bf16[96,256]{1,0:T(8,128)(2,1)S(1)} %add.1.refs_0_), channel_id=1, source_target_pairs={{0,4},{2,6},{4,0},{6,2},{8,12},{10,14},{12,8},{14,10},{1,5},{3,7},... | collective-permute-start | bytes 147464 | tf_op jit(solution)/shard_map/ppermute | solution.py:349
  38.3 1.9 %collective-permute-done.11.refs_3_ = bf16[96,256]{1,0:T(8,128)(2,1)S(1)} collective-permute-done((bf16[96,256]{1,0:T(8,128)(2,1)S(1)}, bf16[96,256]{1,0:T(8,128)(2,1)S(1)}, u32[]{:S(2)}, u32[]{:S(2)}) %collective-permute-start.11) | collective-permute-done | bytes 49184 | tf_op jit(solution)/shard_map/ppermute | solution.py:349
  40.2 1.0 %collective-permute-done.10.refs_2_ = bf16[96,256]{1,0:T(8,128)(2,1)S(1)} collective-permute-done((bf16[96,256]{1,0:T(8,128)(2,1)S(1)}, bf16[96,256]{1,0:T(8,128)(2,1)S(1)}, u32[]{:S(2)}, u32[]{:S(2)}) %collective-permute-start.10) | collective-permute-done | bytes 49184 | tf_op jit(solution)/shard_map/ppermute | solution.py:349
  41.3 0.0 collective-permute-done.9.refs_1_
  41.3 0.0 copy-done.3
  41.3 0.8 %finish.1 = f32[32,768]{1,0:T(8,128)} custom-call(bf16[96,256]{1,0:T(8,128)(2,1)S(1)} %add.1.refs_0_, bf16[96,256]{1,0:T(8,128)(2,1)S(1)} %collective-permute-done.9.refs_1_, bf16[96,256]{1,0:T(8,128)(2,1)S(1)} %collective-permute-done.10.refs_2_, bf16[96,256]{1,0:T(8,128)(2,1)S(1)} %collective-permute-done.11.refs_3_, f32[32,768]{1,0:T(8,128)S(1)} %copy-done.3), custom_call_target="tpu_custom_call" | custom-call | tf_op jit(solution)/shard_map/finish/pallas_call | solution.py:424
  (1 shorter events, 0.0 us)
Async XLA Ops:
  3.2 11.0 %collective-permute-start = (bf16[280,128]{1,0:T(8,128)(2,1)S(1)}, bf16[280,128]{1,0:T(8,128)(2,1)S(1)}, u32[]{:S(2)}, u32[]{:S(2)}) collective-permute-start(bf16[280,128]{1,0:T(8,128)(2,1)S(1)} %get-tuple-element.16), channel_id=1, source_target_pairs={{0,8},{2,10},{4,12},{6,14},{8,0},{10,2},{12,4},{14,6},{1,9},{3,11}... | collective-permute-start | bytes 215048 | tf_op jit(solution)/shard_map/ppermute | solution.py:349
  7.3 11.0 %collective-permute-start.1 = (bf16[280,128]{1,0:T(8,128)(2,1)S(1)}, bf16[280,128]{1,0:T(8,128)(2,1)S(1)}, u32[]{:S(2)}, u32[]{:S(2)}) collective-permute-start(bf16[280,128]{1,0:T(8,128)(2,1)S(1)} %get-tuple-element.17), channel_id=1, source_target_pairs={{0,4},{2,6},{4,0},{6,2},{8,12},{10,14},{12,8},{14,10},{1,5},{3,7},... | collective-permute-start | bytes 215048 | tf_op jit(solution)/shard_map/ppermute | solution.py:349
  8.9 12.0 %collective-permute-start.2 = (bf16[280,128]{1,0:T(8,128)(2,1)S(1)}, bf16[280,128]{1,0:T(8,128)(2,1)S(1)}, u32[]{:S(2)}, u32[]{:S(2)}) collective-permute-start(bf16[280,128]{1,0:T(8,128)(2,1)S(1)} %get-tuple-element.18), channel_id=1, source_target_pairs={{0,12},{2,14},{4,8},{6,10},{8,4},{10,6},{12,0},{14,2},{1,13},{3,15... | collective-permute-start | bytes 215048 | tf_op jit(solution)/shard_map/ppermute | solution.py:349
  8.9 12.0 %collective-permute-start.3 = (bf16[280,128]{1,0:T(8,128)(2,1)S(1)}, bf16[280,128]{1,0:T(8,128)(2,1)S(1)}, u32[]{:S(2)}, u32[]{:S(2)}) collective-permute-start(bf16[280,128]{1,0:T(8,128)(2,1)S(1)} %get-tuple-element.19), channel_id=1, source_target_pairs={{0,10},{2,8},{4,14},{6,12},{8,2},{10,0},{12,6},{14,4},{1,11},{3,9}... | collective-permute-start | bytes 215048 | tf_op jit(solution)/shard_map/ppermute | solution.py:349
  11.8 9.2 %collective-permute-start.4 = (bf16[280,128]{1,0:T(8,128)(2,1)S(1)}, bf16[280,128]{1,0:T(8,128)(2,1)S(1)}, u32[]{:S(2)}, u32[]{:S(2)}) collective-permute-start(bf16[280,128]{1,0:T(8,128)(2,1)S(1)} %get-tuple-element.20), channel_id=1, source_target_pairs={{0,6},{2,4},{4,2},{6,0},{8,14},{10,12},{12,10},{14,8},{1,7},{3,5},... | collective-permute-start | bytes 215048 | tf_op jit(solution)/shard_map/ppermute | solution.py:349
  14.2 7.1 %collective-permute-start.5 = (bf16[280,128]{1,0:T(8,128)(2,1)S(1)}, bf16[280,128]{1,0:T(8,128)(2,1)S(1)}, u32[]{:S(2)}, u32[]{:S(2)}) collective-permute-start(bf16[280,128]{1,0:T(8,128)(2,1)S(1)} %get-tuple-element.21), channel_id=1, source_target_pairs={{0,14},{2,12},{4,10},{6,8},{8,6},{10,4},{12,2},{14,0},{1,15},{3,13... | collective-permute-start | bytes 215048 | tf_op jit(solution)/shard_map/ppermute | solution.py:349
  18.3 4.3 %copy-start.2 = (bf16[2,8,16,256]{3,2,1,0:T(8,128)(2,1)S(1)}, bf16[2,8,16,256]{3,2,1,0:T(8,128)(2,1)}, u32[]{:S(2)}) copy-start(bf16[2,8,16,256]{3,2,1,0:T(8,128)(2,1)} %constant.9.clone.refs_8_) | copy-start | bytes 393220
  18.3 4.3 %collective-permute-start.6 = (bf16[280,128]{1,0:T(8,128)(2,1)S(1)}, bf16[280,128]{1,0:T(8,128)(2,1)S(1)}, u32[]{:S(2)}, u32[]{:S(2)}) collective-permute-start(bf16[280,128]{1,0:T(8,128)(2,1)S(1)} %get-tuple-element.22), channel_id=1, source_target_pairs={{0,2},{2,0},{4,6},{6,4},{8,10},{10,8},{12,14},{14,12},{1,3},{3,1},... | collective-permute-start | bytes 215048 | tf_op jit(solution)/shard_map/ppermute | solution.py:349
  20.9 5.2 %copy-start = (bf16[512,512]{1,0:T(8,128)(2,1)S(1)}, bf16[512,512]{1,0:T(8,128)(2,1)}, u32[]{:S(2)}) copy-start(bf16[512,512]{1,0:T(8,128)(2,1)} %constant.10.clone.inverse_ref) | copy-start | bytes 1572868
  20.9 5.2 %copy-start.1 = (f32[8,16,512]{2,1,0:T(8,128)S(1)}, f32[8,16,512]{2,1,0:T(8,128)}, u32[]{:S(2)}) copy-start(f32[8,16,512]{2,1,0:T(8,128)} %constant.11.clone.turn_ref) | copy-start | bytes 786436
  24.8 16.5 %copy-start.3 = (f32[32,768]{1,0:T(8,128)S(1)}, f32[32,768]{1,0:T(8,128)}, u32[]{:S(2)}) copy-start(f32[32,768]{1,0:T(8,128)} %refs_4_.1) | copy-start | bytes 294916
  24.8 1.3 %collective-permute-start.7 = (bf16[256,128]{1,0:T(8,128)(2,1)S(1)}, bf16[256,128]{1,0:T(8,128)(2,1)S(1)}, u32[]{:S(2)}, u32[]{:S(2)}) collective-permute-start(bf16[256,128]{1,0:T(8,128)(2,1)S(1)} %get-tuple-element.27), channel_id=1, source_target_pairs={{0,1},{1,0},{2,3},{3,2},{4,5},{5,4},{6,7},{7,6},{8,9},{9,8},{10,11... | collective-permute-start | bytes 196616 | tf_op jit(solution)/shard_map/ppermute | solution.py:397
  29.6 4.2 %collective-permute-start.8 = (bf16[96,256]{1,0:T(8,128)(2,1)S(1)}, bf16[96,256]{1,0:T(8,128)(2,1)S(1)}, u32[]{:S(2)}, u32[]{:S(2)}) collective-permute-start(bf16[96,256]{1,0:T(8,128)(2,1)S(1)} %get-tuple-element.29.a_ref), channel_id=1, source_target_pairs={{0,2},{2,0},{4,6},{6,4},{8,10},{10,8},{12,14},{14,12},{1,3},{3,1},... | collective-permute-start | bytes 147464 | tf_op jit(solution)/shard_map/ppermute | solution.py:349
  33.8 6.4 %collective-permute-start.11 = (bf16[96,256]{1,0:T(8,128)(2,1)S(1)}, bf16[96,256]{1,0:T(8,128)(2,1)S(1)}, u32[]{:S(2)}, u32[]{:S(2)}) collective-permute-start(bf16[96,256]{1,0:T(8,128)(2,1)S(1)} %add.1.refs_0_), channel_id=1, source_target_pairs={{0,12},{2,14},{4,8},{6,10},{8,4},{10,6},{12,0},{14,2},{1,13},{3,15... | collective-permute-start | bytes 147464 | tf_op jit(solution)/shard_map/ppermute | solution.py:349
  35.8 5.5 %collective-permute-start.10 = (bf16[96,256]{1,0:T(8,128)(2,1)S(1)}, bf16[96,256]{1,0:T(8,128)(2,1)S(1)}, u32[]{:S(2)}, u32[]{:S(2)}) collective-permute-start(bf16[96,256]{1,0:T(8,128)(2,1)S(1)} %add.1.refs_0_), channel_id=1, source_target_pairs={{0,8},{2,10},{4,12},{6,14},{8,0},{10,2},{12,4},{14,6},{1,9},{3,11}... | collective-permute-start | bytes 147464 | tf_op jit(solution)/shard_map/ppermute | solution.py:349
  35.8 5.5 %collective-permute-start.9 = (bf16[96,256]{1,0:T(8,128)(2,1)S(1)}, bf16[96,256]{1,0:T(8,128)(2,1)S(1)}, u32[]{:S(2)}, u32[]{:S(2)}) collective-permute-start(bf16[96,256]{1,0:T(8,128)(2,1)S(1)} %add.1.refs_0_), channel_id=1, source_target_pairs={{0,4},{2,6},{4,0},{6,2},{8,12},{10,14},{12,8},{14,10},{1,5},{3,7},... | collective-permute-start | bytes 147464 | tf_op jit(solution)/shard_map/ppermute | solution.py:349

commit v4 on v3

--- a/solution.py
+++ b/solution.py
@@ -66,7 +66,7 @@
 
 def far_first(bands):
     if bands == 8:
-        return [4, 2, 6, 5, 3, 7, 1, 0]
+        return [7, 1, 5, 2, 3, 4, 6, 0]
     return list(range(bands - 1, -1, -1))
 
 
@@ -75,33 +75,42 @@
 
 
 def columns_kernel(maps_ref, image_ref, table_ref, *refs):
-    out_refs = refs[:-4]
-    lines_in, table_in, line_sem, table_sem = refs[-4:]
-    bands = len(out_refs)
+    out_refs = refs[:-5]
+    lines_in, both_in, table_in, line_sem, table_sem = refs[-5:]
+    half = len(out_refs) // 2
     rows = maps_ref.shape[0]
+    lines = lines_in.shape[0]
     mine = lax.axis_index("band")
     maps_copy = pltpu.make_async_copy(maps_ref, lines_in.at[:rows], line_sem.at[0])
     image_copy = pltpu.make_async_copy(image_ref, lines_in.at[rows:], line_sem.at[1])
     table_copies = [
         pltpu.make_async_copy(
-            table_ref.at[mine ^ k],
-            table_in.at[i // 2, :, i % 2 * LANES : (i % 2 + 1) * LANES],
-            table_sem.at[i],
+            table_ref.at[(mine ^ k) % half],
+            table_in.at[k // 2, :, k % 2 * LANES : (k % 2 + 1) * LANES],
+            table_sem.at[k],
         )
-        for i, k in enumerate(far_first(bands))
+        for k in range(half)
     ]
     maps_copy.start()
     image_copy.start()
     for copy in table_copies:
         copy.start()
+    odd = lax.broadcasted_iota(jnp.int32, (1, lines_in.shape[1]), 1) % 2
+    upper = (mine >= half).astype(jnp.int32)
+    near_sign = (1 - 2 * odd * upper).astype(f32).astype(bf16)
+    far_sign = (1 - 2 * odd * (1 - upper)).astype(f32).astype(bf16)
     maps_copy.wait()
     image_copy.wait()
-    for i in range(0, bands, 2):
-        table_copies[i].wait()
-        table_copies[i + 1].wait()
-        both = jnp.dot(lines_in[...], table_in[i // 2], preferred_element_type=f32).astype(bf16)
-        out_refs[i][...] = both[:, :LANES]
-        out_refs[i + 1][...] = both[:, LANES:]
+    both_in[:lines] = lines_in[...] * near_sign
+    both_in[lines:] = lines_in[...] * far_sign
+    for k in range(0, half, 2):
+        table_copies[k].wait()
+        table_copies[k + 1].wait()
+        both = jnp.dot(both_in[...], table_in[k // 2], preferred_element_type=f32).astype(bf16)
+        out_refs[k][...] = both[:lines, :LANES]
+        out_refs[k + 1][...] = both[:lines, LANES:]
+        out_refs[half + k][...] = both[lines:, :LANES]
+        out_refs[half + k + 1][...] = both[lines:, LANES:]
 
 
 def prepare_kernel(target_ref, packed_ref, target_in, sems):
@@ -195,8 +204,6 @@
     rim_ref,
     re_ref,
     im_ref,
-    held_ref,
-    sems,
 ):
     freqs, channels, filters, _ = packed_ref.shape
     group = inverse_ref.shape[0] // LANES
@@ -215,10 +222,6 @@
 
     chunk = freqs // CHUNKS
     mine = lax.axis_index("band")
-
-    def written(i):
-        span = pl.ds(i * chunk, chunk)
-        return pltpu.make_async_copy(held_ref.at[span], out_ref.at[span], sems.at[i])
 
     def step(i, acc):
         blocks = []
@@ -236,12 +239,11 @@
                         + y * im_ref[pl.ds(c * freqs + q, 1), :]
                     )
                     d = d.astype(bf16)
-                    held_ref[q, 0, c] = d[:, :HALF]
-                    held_ref[q, 1, c] = d[:, HALF:]
+                    out_ref[q, 0, c] = d[:, :HALF]
+                    out_ref[q, 1, c] = d[:, HALF:]
                     parts.append(d)
                 sides.append(jnp.concatenate(parts, axis=0))
             blocks.append(jnp.concatenate(sides, axis=1))
-        written(i).start()
         left = jnp.concatenate(blocks, axis=0)
         both = jnp.dot(left, inverse_ref[...], preferred_element_type=f32)
         for j in range(chunk // group):
@@ -252,8 +254,12 @@
 
     acc = lax.fori_loop(0, CHUNKS, step, jnp.zeros(rim_ref.shape, f32))
     rim_ref[...] = acc.astype(bf16)
-    for i in range(CHUNKS):
-        written(i).wait()
+
+
+def write_kernel(held_ref, out_ref, sem):
+    copy = pltpu.make_async_copy(held_ref, out_ref, sem)
+    copy.start()
+    copy.wait()
 
 
 def finish_kernel(*refs):
@@ -354,18 +360,19 @@
         in_specs=[pl.BlockSpec(memory_space=pltpu.HBM)] * 3,
         scratch_shapes=[
             pltpu.VMEM((rows, width_cols), bf16),
-            pltpu.VMEM((bands // 2, width_cols, 2 * LANES), bf16),
+            pltpu.VMEM((2 * rows, width_cols), bf16),
+            pltpu.VMEM((bands // 4, width_cols, 2 * LANES), bf16),
             pltpu.SemaphoreType.DMA((2,)),
-            pltpu.SemaphoreType.DMA((bands,)),
+            pltpu.SemaphoreType.DMA((bands // 2,)),
         ],
         compiler_params=params(8),
         name="columns",
     )(
         far(coeff_maps.reshape(filters * band_rows, width_cols)),
         far(image.reshape(channels * band_rows, width_cols)),
-        far(jnp.asarray(column_table(width_cols, bands))),
+        far(jnp.asarray(column_table(width_cols, bands)[: bands // 2])),
     )
-    got = [swap(chunk, k) if k else chunk for k, chunk in zip(far_first(bands), chunks)]
+    got = [swap(chunks[k], k) if k else chunks[k] for k in far_first(bands)]
 
     turns = turn_table(width_cols, K, GROUP).reshape(bands, freqs // GROUP, 2 * K * K)
     packed = pl.pallas_call(
@@ -396,22 +403,29 @@
 
     peer = lax.ppermute(sums, "filt", [(0, 1), (1, 0)])
 
-    dict_spectra, rim = pl.pallas_call(
+    held, rim = pl.pallas_call(
         solve_kernel,
         out_shape=(
             jax.ShapeDtypeStruct(target.shape, bf16),
             jax.ShapeDtypeStruct((channels * filters, K * K), bf16),
         ),
-        out_specs=(pl.BlockSpec(memory_space=pltpu.HBM), pl.BlockSpec(memory_space=pltpu.VMEM)),
         scratch_shapes=[
             pltpu.VMEM((channels * freqs, LANES), f32),
             pltpu.VMEM((channels * freqs, LANES), f32),
-            pltpu.VMEM(target.shape, bf16),
-            pltpu.SemaphoreType.DMA((CHUNKS,)),
         ],
         compiler_params=params(16),
         name="solve",
     )(x, packed, lit, own, peer, jnp.asarray(inverse_table(height, width_cols, K, GROUP)), jnp.asarray(turns))
+
+    dict_spectra = pl.pallas_call(
+        write_kernel,
+        out_shape=jax.ShapeDtypeStruct(target.shape, bf16),
+        in_specs=[pl.BlockSpec(memory_space=pltpu.VMEM)],
+        out_specs=pl.BlockSpec(memory_space=pltpu.HBM),
+        scratch_shapes=[pltpu.SemaphoreType.DMA],
+        compiler_params=params(4),
+        name="write",
+    )(held)
 
     near = swap(rim, 1)
     pair = pl.pallas_call(
@@ -420,7 +434,7 @@
         compiler_params=params(4),
         name="add",
     )(rim, near)
-    parts = [pair] + [swap(pair, k) for k in range(2, bands, 2)]
+    parts = [pair] + [swap(pair, k) for k in (4, 2, 6)]
     dictionary = pl.pallas_call(
         finish_kernel,
         out_shape=jax.ShapeDtypeStruct(dual_rim.shape, f32),

time: 42.2 us -> 39.6 us (0.938)
  starting transfers between devices: 21 us -> 18.9 us
  waiting for transfers between devices: 9.2 us -> 8.54 us
    ppermute x11, starting transfers between devices: 21 us -> 18.8 us  [swap(): return lax.ppermute(array, 'band', [(i, i ^ k) for i in range(bands)])]
    pallas_call x0 -> x1, Pallas kernels: none -> 1.67 us  [body(): pl.pallas_call(write_kernel, out_shape=jax.ShapeDtypeStruct(target.shape,...]
    pallas_call x1, Pallas kernels: 3.55 us -> 2.73 us  [body(): pl.pallas_call(solve_kernel, out_shape=(jax.ShapeDtypeStruct(target.shape...]
    ppermute x11, waiting for transfers between devices: 7.96 us -> 7.3 us  [swap(): return lax.ppermute(array, 'band', [(i, i ^ k) for i in range(bands)])]
    pallas_call x1, Pallas kernels: 2.6 us -> 2.02 us  [body(): pl.pallas_call(columns_kernel, out_shape=(jax.ShapeDtypeStruct((rows, LAN...]
  transfers between devices with their start and end apart: 12 -> 12, of which waited for: 6 -> 6; matrix products, arithmetic and copies ran while one was open for 0% -> 0% of each run, Pallas kernels for 5% -> 9%
where the time goes in v4:
time: 39.6 us; the launch traced here: 39.5 us
  starting transfers between devices  18.9 us (48%)
  Pallas kernels  11.3 us (29%)
  waiting for transfers between devices  8.54 us (22%)
  between operations  0.73 us (2%)
    ppermute x11, starting transfers between devices, swap(): return lax.ppermute(array, 'band', [(i, i ^ k) for i in range(bands)])  18.8 us
    ppermute x11, waiting for transfers between devices, swap(): return lax.ppermute(array, 'band', [(i, i ^ k) for i in range(bands)])  7.3 us
    pallas_call x1, Pallas kernels, body(): pl.pallas_call(solve_kernel, out_shape=(jax.ShapeDtypeStruct(target.shape...  2.73 us
    pallas_call x1, Pallas kernels, body(): pl.pallas_call(rows_kernel, out_shape=(jax.ShapeDtypeStruct((freqs * filt...  2.07 us
    pallas_call x1, Pallas kernels, body(): pl.pallas_call(prepare_kernel, out_shape=jax.ShapeDtypeStruct((freqs, cha...  2.05 us
    pallas_call x1, Pallas kernels, body(): pl.pallas_call(columns_kernel, out_shape=(jax.ShapeDtypeStruct((rows, LAN...  2.02 us
    pallas_call x1, Pallas kernels, body(): pl.pallas_call(write_kernel, out_shape=jax.ShapeDtypeStruct(target.shape,...  1.67 us
    ppermute x1, waiting for transfers between devices, body(): peer = lax.ppermute(sums, 'filt', [(0, 1), (1, 0)])  1.24 us
  transfers between devices with their start and end apart: 12, of which 6 were waited for; matrix products, arithmetic and copies ran while one was open for 0% of the time, Pallas kernels for 9%

profile of v4, /device:TPU:0, one launch (start us, length us, event | category | flops | bytes accessed | tf_op | source)
XLA Modules:
  0.0 39.5 jit_solution(13076661454223907120)
XLA Ops:
  0.6 2.0 %columns.1 = (bf16[280,128]{1,0:T(8,128)(2,1)S(1)}, bf16[280,128]{1,0:T(8,128)(2,1)S(1)}, bf16[280,128]{1,0:T(8,128)(2,1)S(1)}, bf16[280,128]{1,0:T(8,128)(2,1)S...) custom-call(bf16[256,512]{1,0:T(8,128)(2,1)} %bitcast.2, ...), custom_call_target="tpu_custom_call" | custom-call | tf_op jit(solution)/shard_map/columns/pallas_call | solution.py:357
  2.7 6.0 %collective-permute-start = (bf16[280,128]{1,0:T(8,128)(2,1)S(1)}, bf16[280,128]{1,0:T(8,128)(2,1)S(1)}, u32[]{:S(2)}, u32[]{:S(2)}) collective-permute-start(bf16[280,128]{1,0:T(8,128)(2,1)S(1)} %get-tuple-element.16), channel_id=1, source_target_pairs={{0,14},{2,12},{4,10},{6,8},{8,6},{10,4},{12,2},{14,0},{1,15},{3,13... | collective-permute-start | bytes 215048 | tf_op jit(solution)/shard_map/ppermute | solution.py:355
  8.7 0.5 %collective-permute-start.1 = (bf16[280,128]{1,0:T(8,128)(2,1)S(1)}, bf16[280,128]{1,0:T(8,128)(2,1)S(1)}, u32[]{:S(2)}, u32[]{:S(2)}) collective-permute-start(bf16[280,128]{1,0:T(8,128)(2,1)S(1)} %get-tuple-element.17), channel_id=1, source_target_pairs={{0,2},{2,0},{4,6},{6,4},{8,10},{10,8},{12,14},{14,12},{1,3},{3,1},... | collective-permute-start | bytes 215048 | tf_op jit(solution)/shard_map/ppermute | solution.py:355
  9.2 0.4 collective-permute-start.2
  9.6 1.3 %collective-permute-start.3 = (bf16[280,128]{1,0:T(8,128)(2,1)S(1)}, bf16[280,128]{1,0:T(8,128)(2,1)S(1)}, u32[]{:S(2)}, u32[]{:S(2)}) collective-permute-start(bf16[280,128]{1,0:T(8,128)(2,1)S(1)} %get-tuple-element.19), channel_id=1, source_target_pairs={{0,4},{2,6},{4,0},{6,2},{8,12},{10,14},{12,8},{14,10},{1,5},{3,7},... | collective-permute-start | bytes 215048 | tf_op jit(solution)/shard_map/ppermute | solution.py:355
  10.9 1.2 %collective-permute-start.4 = (bf16[280,128]{1,0:T(8,128)(2,1)S(1)}, bf16[280,128]{1,0:T(8,128)(2,1)S(1)}, u32[]{:S(2)}, u32[]{:S(2)}) collective-permute-start(bf16[280,128]{1,0:T(8,128)(2,1)S(1)} %get-tuple-element.20), channel_id=1, source_target_pairs={{0,6},{2,4},{4,2},{6,0},{8,14},{10,12},{12,10},{14,8},{1,7},{3,5},... | collective-permute-start | bytes 215048 | tf_op jit(solution)/shard_map/ppermute | solution.py:355
  12.2 0.0 collective-permute-done.refs_0_
  12.2 2.9 %collective-permute-start.5 = (bf16[280,128]{1,0:T(8,128)(2,1)S(1)}, bf16[280,128]{1,0:T(8,128)(2,1)S(1)}, u32[]{:S(2)}, u32[]{:S(2)}) collective-permute-start(bf16[280,128]{1,0:T(8,128)(2,1)S(1)} %get-tuple-element.21), channel_id=1, source_target_pairs={{0,8},{2,10},{4,12},{6,14},{8,0},{10,2},{12,4},{14,6},{1,9},{3,11}... | collective-permute-start | bytes 215048 | tf_op jit(solution)/shard_map/ppermute | solution.py:355
  15.1 0.0 collective-permute-done.1.refs_1_
  15.1 0.0 copy-start.2
  15.1 0.5 %collective-permute-start.6 = (bf16[280,128]{1,0:T(8,128)(2,1)S(1)}, bf16[280,128]{1,0:T(8,128)(2,1)S(1)}, u32[]{:S(2)}, u32[]{:S(2)}) collective-permute-start(bf16[280,128]{1,0:T(8,128)(2,1)S(1)} %get-tuple-element.22), channel_id=1, source_target_pairs={{0,12},{2,14},{4,8},{6,10},{8,4},{10,6},{12,0},{14,2},{1,13},{3,15... | collective-permute-start | bytes 215048 | tf_op jit(solution)/shard_map/ppermute | solution.py:355
  15.6 2.0 %prepare.1.refs_9_.packed_ref = f32[64,3,32,128]{3,2,1,0:T(8,128)S(1)} custom-call(bf16[64,2,3,32,64]{4,3,2,1,0:T(8,128)(2,1)} %target_ref.1), custom_call_target="tpu_custom_call" | custom-call | tf_op jit(solution)/shard_map/prepare/pallas_call | solution.py:378
  17.6 0.0 copy-start
  17.6 0.0 copy-start.1
  17.6 0.0 collective-permute-done.2.refs_2_
  17.7 0.0 collective-permute-done.3.refs_3_
  17.7 0.0 collective-permute-done.4.refs_4_
  17.7 2.3 %collective-permute-done.5.refs_5_ = bf16[280,128]{1,0:T(8,128)(2,1)S(1)} collective-permute-done((bf16[280,128]{1,0:T(8,128)(2,1)S(1)}, bf16[280,128]{1,0:T(8,128)(2,1)S(1)}, u32[]{:S(2)}, u32[]{:S(2)}) %collective-permute-start.5) | collective-permute-done | bytes 71712 | tf_op jit(solution)/shard_map/ppermute | solution.py:355
  20.0 1.4 %collective-permute-done.6.refs_6_ = bf16[280,128]{1,0:T(8,128)(2,1)S(1)} collective-permute-done((bf16[280,128]{1,0:T(8,128)(2,1)S(1)}, bf16[280,128]{1,0:T(8,128)(2,1)S(1)}, u32[]{:S(2)}, u32[]{:S(2)}) %collective-permute-start.6) | collective-permute-done | bytes 71712 | tf_op jit(solution)/shard_map/ppermute | solution.py:355
  21.3 0.0 copy-done.2
  21.3 2.1 %rows.1 = (f32[2048,128]{1,0:T(8,128)S(1)}, f32[192,128]{1,0:T(8,128)S(1)}, f32[256,128]{1,0:T(8,128)S(1)}, bf16[256,128]{1,0:T(8,128)(2,1)S(1)}) custom-call(bf16[280,128]{1,0:T(8,128)(2,1)S(1)} %collective-permute-done.refs_0_, bf16[280,128]{1,0:T(8,128)(2,1)S(1)} %collective-permute-done.1.refs_1_, bf16[280,128]{1,0:T(8,128)(2,1)S(1)} %collective-permute-done.2.refs_2_, ...), custom_call_target="tpu_custom_call" | custom-call | tf_op jit(solution)/shard_map/rows/pallas_call | solution.py:388
  23.4 0.1 collective-permute-start.7
  23.5 1.2 %collective-permute-done.7.peer_ref = bf16[256,128]{1,0:T(8,128)(2,1)S(1)} collective-permute-done((bf16[256,128]{1,0:T(8,128)(2,1)S(1)}, bf16[256,128]{1,0:T(8,128)(2,1)S(1)}, u32[]{:S(2)}, u32[]{:S(2)}) %collective-permute-start.7) | collective-permute-done | bytes 65568 | tf_op jit(solution)/shard_map/ppermute | solution.py:404
  24.7 0.0 copy-done
  24.7 0.0 copy-done.1
  24.7 2.7 %solve.1 = (bf16[64,2,3,32,64]{4,3,2,1,0:T(8,128)(2,1)S(1)}, bf16[96,256]{1,0:T(8,128)(2,1)S(1)}) custom-call(f32[2048,128]{1,0:T(8,128)S(1)} %get-tuple-element.24.x_ref, f32[64,3,32,128]{3,2,1,0:T(8,128)S(1)} %prepare.1.refs_9_.packed_ref, f32[192,128]{1,0:T(8,128)S(1)} %get-tuple-element.25.image_ref, f32[256,128]{1,0:T(8,128)S(1)} %get-tuple-element.26.own_ref, ...), custom_call_target="tpu_custom_call" | custom-call | tf_op jit(solution)/shard_map/solve/pallas_call | solution.py:406
  27.5 1.4 %collective-permute-start.8 = (bf16[96,256]{1,0:T(8,128)(2,1)S(1)}, bf16[96,256]{1,0:T(8,128)(2,1)S(1)}, u32[]{:S(2)}, u32[]{:S(2)}) collective-permute-start(bf16[96,256]{1,0:T(8,128)(2,1)S(1)} %get-tuple-element.29.a_ref), channel_id=1, source_target_pairs={{0,2},{2,0},{4,6},{6,4},{8,10},{10,8},{12,14},{14,12},{1,3},{3,1},... | collective-permute-start | bytes 147464 | tf_op jit(solution)/shard_map/ppermute | solution.py:355
  28.9 2.7 %collective-permute-done.8.b_ref = bf16[96,256]{1,0:T(8,128)(2,1)S(1)} collective-permute-done((bf16[96,256]{1,0:T(8,128)(2,1)S(1)}, bf16[96,256]{1,0:T(8,128)(2,1)S(1)}, u32[]{:S(2)}, u32[]{:S(2)}) %collective-permute-start.8) | collective-permute-done | bytes 49184 | tf_op jit(solution)/shard_map/ppermute | solution.py:355
  31.7 1.6 %collective-permute-start.11 = (bf16[96,256]{1,0:T(8,128)(2,1)S(1)}, bf16[96,256]{1,0:T(8,128)(2,1)S(1)}, u32[]{:S(2)}, u32[]{:S(2)}) collective-permute-start(bf16[96,256]{1,0:T(8,128)(2,1)S(1)} %add.1.refs_0_), channel_id=1, source_target_pairs={{0,12},{2,14},{4,8},{6,10},{8,4},{10,6},{12,0},{14,2},{1,13},{3,15... | collective-permute-start | bytes 147464 | tf_op jit(solution)/shard_map/ppermute | solution.py:355
  33.3 0.4 %collective-permute-start.10 = (bf16[96,256]{1,0:T(8,128)(2,1)S(1)}, bf16[96,256]{1,0:T(8,128)(2,1)S(1)}, u32[]{:S(2)}, u32[]{:S(2)}) collective-permute-start(bf16[96,256]{1,0:T(8,128)(2,1)S(1)} %add.1.refs_0_), channel_id=1, source_target_pairs={{0,4},{2,6},{4,0},{6,2},{8,12},{10,14},{12,8},{14,10},{1,5},{3,7},... | collective-permute-start | bytes 147464 | tf_op jit(solution)/shard_map/ppermute | solution.py:355
  33.7 2.4 %collective-permute-start.9 = (bf16[96,256]{1,0:T(8,128)(2,1)S(1)}, bf16[96,256]{1,0:T(8,128)(2,1)S(1)}, u32[]{:S(2)}, u32[]{:S(2)}) collective-permute-start(bf16[96,256]{1,0:T(8,128)(2,1)S(1)} %add.1.refs_0_), channel_id=1, source_target_pairs={{0,8},{2,10},{4,12},{6,14},{8,0},{10,2},{12,4},{14,6},{1,9},{3,11}... | collective-permute-start | bytes 147464 | tf_op jit(solution)/shard_map/ppermute | solution.py:355
  36.1 0.0 copy-start.3
  36.1 1.7 %write.1 = bf16[64,2,3,32,64]{4,3,2,1,0:T(8,128)(2,1)} custom-call(bf16[64,2,3,32,64]{4,3,2,1,0:T(8,128)(2,1)S(1)} %get-tuple-element.28.held_ref), custom_call_target="tpu_custom_call" | custom-call | tf_op jit(solution)/shard_map/write/pallas_call | solution.py:420
  37.8 0.0 collective-permute-done.11.refs_3_
  37.8 0.1 collective-permute-done.10.refs_2_
  37.9 0.8 %collective-permute-done.9.refs_1_ = bf16[96,256]{1,0:T(8,128)(2,1)S(1)} collective-permute-done((bf16[96,256]{1,0:T(8,128)(2,1)S(1)}, bf16[96,256]{1,0:T(8,128)(2,1)S(1)}, u32[]{:S(2)}, u32[]{:S(2)}) %collective-permute-start.9) | collective-permute-done | bytes 49184 | tf_op jit(solution)/shard_map/ppermute | solution.py:355
  38.7 0.0 copy-done.3
  38.7 0.8 %finish.1 = f32[32,768]{1,0:T(8,128)} custom-call(bf16[96,256]{1,0:T(8,128)(2,1)S(1)} %add.1.refs_0_, bf16[96,256]{1,0:T(8,128)(2,1)S(1)} %collective-permute-done.9.refs_1_, bf16[96,256]{1,0:T(8,128)(2,1)S(1)} %collective-permute-done.10.refs_2_, bf16[96,256]{1,0:T(8,128)(2,1)S(1)} %collective-permute-done.11.refs_3_, f32[32,768]{1,0:T(8,128)S(1)} %copy-done.3), custom_call_target="tpu_custom_call" | custom-call | tf_op jit(solution)/shard_map/finish/pallas_call | solution.py:438
  (1 shorter events, 0.0 us)
Async XLA Ops:
  2.7 9.5 %collective-permute-start = (bf16[280,128]{1,0:T(8,128)(2,1)S(1)}, bf16[280,128]{1,0:T(8,128)(2,1)S(1)}, u32[]{:S(2)}, u32[]{:S(2)}) collective-permute-start(bf16[280,128]{1,0:T(8,128)(2,1)S(1)} %get-tuple-element.16), channel_id=1, source_target_pairs={{0,14},{2,12},{4,10},{6,8},{8,6},{10,4},{12,2},{14,0},{1,15},{3,13... | collective-permute-start | bytes 215048 | tf_op jit(solution)/shard_map/ppermute | solution.py:355
  8.7 6.4 %collective-permute-start.1 = (bf16[280,128]{1,0:T(8,128)(2,1)S(1)}, bf16[280,128]{1,0:T(8,128)(2,1)S(1)}, u32[]{:S(2)}, u32[]{:S(2)}) collective-permute-start(bf16[280,128]{1,0:T(8,128)(2,1)S(1)} %get-tuple-element.17), channel_id=1, source_target_pairs={{0,2},{2,0},{4,6},{6,4},{8,10},{10,8},{12,14},{14,12},{1,3},{3,1},... | collective-permute-start | bytes 215048 | tf_op jit(solution)/shard_map/ppermute | solution.py:355
  9.2 8.4 %collective-permute-start.2 = (bf16[280,128]{1,0:T(8,128)(2,1)S(1)}, bf16[280,128]{1,0:T(8,128)(2,1)S(1)}, u32[]{:S(2)}, u32[]{:S(2)}) collective-permute-start(bf16[280,128]{1,0:T(8,128)(2,1)S(1)} %get-tuple-element.18), channel_id=1, source_target_pairs={{0,10},{2,8},{4,14},{6,12},{8,2},{10,0},{12,6},{14,4},{1,11},{3,9}... | collective-permute-start | bytes 215048 | tf_op jit(solution)/shard_map/ppermute | solution.py:355
  9.6 8.1 %collective-permute-start.3 = (bf16[280,128]{1,0:T(8,128)(2,1)S(1)}, bf16[280,128]{1,0:T(8,128)(2,1)S(1)}, u32[]{:S(2)}, u32[]{:S(2)}) collective-permute-start(bf16[280,128]{1,0:T(8,128)(2,1)S(1)} %get-tuple-element.19), channel_id=1, source_target_pairs={{0,4},{2,6},{4,0},{6,2},{8,12},{10,14},{12,8},{14,10},{1,5},{3,7},... | collective-permute-start | bytes 215048 | tf_op jit(solution)/shard_map/ppermute | solution.py:355
  10.9 6.7 %collective-permute-start.4 = (bf16[280,128]{1,0:T(8,128)(2,1)S(1)}, bf16[280,128]{1,0:T(8,128)(2,1)S(1)}, u32[]{:S(2)}, u32[]{:S(2)}) collective-permute-start(bf16[280,128]{1,0:T(8,128)(2,1)S(1)} %get-tuple-element.20), channel_id=1, source_target_pairs={{0,6},{2,4},{4,2},{6,0},{8,14},{10,12},{12,10},{14,8},{1,7},{3,5},... | collective-permute-start | bytes 215048 | tf_op jit(solution)/shard_map/ppermute | solution.py:355
  12.2 7.8 %collective-permute-start.5 = (bf16[280,128]{1,0:T(8,128)(2,1)S(1)}, bf16[280,128]{1,0:T(8,128)(2,1)S(1)}, u32[]{:S(2)}, u32[]{:S(2)}) collective-permute-start(bf16[280,128]{1,0:T(8,128)(2,1)S(1)} %get-tuple-element.21), channel_id=1, source_target_pairs={{0,8},{2,10},{4,12},{6,14},{8,0},{10,2},{12,4},{14,6},{1,9},{3,11}... | collective-permute-start | bytes 215048 | tf_op jit(solution)/shard_map/ppermute | solution.py:355
  15.1 6.2 %copy-start.2 = (bf16[2,8,16,256]{3,2,1,0:T(8,128)(2,1)S(1)}, bf16[2,8,16,256]{3,2,1,0:T(8,128)(2,1)}, u32[]{:S(2)}) copy-start(bf16[2,8,16,256]{3,2,1,0:T(8,128)(2,1)} %constant.9.clone.refs_8_) | copy-start | bytes 393220
  15.1 6.2 %collective-permute-start.6 = (bf16[280,128]{1,0:T(8,128)(2,1)S(1)}, bf16[280,128]{1,0:T(8,128)(2,1)S(1)}, u32[]{:S(2)}, u32[]{:S(2)}) collective-permute-start(bf16[280,128]{1,0:T(8,128)(2,1)S(1)} %get-tuple-element.22), channel_id=1, source_target_pairs={{0,12},{2,14},{4,8},{6,10},{8,4},{10,6},{12,0},{14,2},{1,13},{3,15... | collective-permute-start | bytes 215048 | tf_op jit(solution)/shard_map/ppermute | solution.py:355
  17.6 7.1 %copy-start = (bf16[512,512]{1,0:T(8,128)(2,1)S(1)}, bf16[512,512]{1,0:T(8,128)(2,1)}, u32[]{:S(2)}) copy-start(bf16[512,512]{1,0:T(8,128)(2,1)} %constant.10.clone.inverse_ref) | copy-start | bytes 1572868
  17.6 7.1 %copy-start.1 = (f32[8,16,512]{2,1,0:T(8,128)S(1)}, f32[8,16,512]{2,1,0:T(8,128)}, u32[]{:S(2)}) copy-start(f32[8,16,512]{2,1,0:T(8,128)} %constant.11.clone.turn_ref) | copy-start | bytes 786436
  23.4 1.3 %collective-permute-start.7 = (bf16[256,128]{1,0:T(8,128)(2,1)S(1)}, bf16[256,128]{1,0:T(8,128)(2,1)S(1)}, u32[]{:S(2)}, u32[]{:S(2)}) collective-permute-start(bf16[256,128]{1,0:T(8,128)(2,1)S(1)} %get-tuple-element.27), channel_id=1, source_target_pairs={{0,1},{1,0},{2,3},{3,2},{4,5},{5,4},{6,7},{7,6},{8,9},{9,8},{10,11... | collective-permute-start | bytes 196616 | tf_op jit(solution)/shard_map/ppermute | solution.py:404
  27.5 4.2 %collective-permute-start.8 = (bf16[96,256]{1,0:T(8,128)(2,1)S(1)}, bf16[96,256]{1,0:T(8,128)(2,1)S(1)}, u32[]{:S(2)}, u32[]{:S(2)}) collective-permute-start(bf16[96,256]{1,0:T(8,128)(2,1)S(1)} %get-tuple-element.29.a_ref), channel_id=1, source_target_pairs={{0,2},{2,0},{4,6},{6,4},{8,10},{10,8},{12,14},{14,12},{1,3},{3,1},... | collective-permute-start | bytes 147464 | tf_op jit(solution)/shard_map/ppermute | solution.py:355
  31.7 6.1 %collective-permute-start.11 = (bf16[96,256]{1,0:T(8,128)(2,1)S(1)}, bf16[96,256]{1,0:T(8,128)(2,1)S(1)}, u32[]{:S(2)}, u32[]{:S(2)}) collective-permute-start(bf16[96,256]{1,0:T(8,128)(2,1)S(1)} %add.1.refs_0_), channel_id=1, source_target_pairs={{0,12},{2,14},{4,8},{6,10},{8,4},{10,6},{12,0},{14,2},{1,13},{3,15... | collective-permute-start | bytes 147464 | tf_op jit(solution)/shard_map/ppermute | solution.py:355
  33.3 4.6 %collective-permute-start.10 = (bf16[96,256]{1,0:T(8,128)(2,1)S(1)}, bf16[96,256]{1,0:T(8,128)(2,1)S(1)}, u32[]{:S(2)}, u32[]{:S(2)}) collective-permute-start(bf16[96,256]{1,0:T(8,128)(2,1)S(1)} %add.1.refs_0_), channel_id=1, source_target_pairs={{0,4},{2,6},{4,0},{6,2},{8,12},{10,14},{12,8},{14,10},{1,5},{3,7},... | collective-permute-start | bytes 147464 | tf_op jit(solution)/shard_map/ppermute | solution.py:355
  33.7 5.0 %collective-permute-start.9 = (bf16[96,256]{1,0:T(8,128)(2,1)S(1)}, bf16[96,256]{1,0:T(8,128)(2,1)S(1)}, u32[]{:S(2)}, u32[]{:S(2)}) collective-permute-start(bf16[96,256]{1,0:T(8,128)(2,1)S(1)} %add.1.refs_0_), channel_id=1, source_target_pairs={{0,8},{2,10},{4,12},{6,14},{8,0},{10,2},{12,4},{14,6},{1,9},{3,11}... | collective-permute-start | bytes 147464 | tf_op jit(solution)/shard_map/ppermute | solution.py:355
  36.1 2.6 %copy-start.3 = (f32[32,768]{1,0:T(8,128)S(1)}, f32[32,768]{1,0:T(8,128)}, u32[]{:S(2)}) copy-start(f32[32,768]{1,0:T(8,128)} %refs_4_.1) | copy-start | bytes 294916

commit v5 on v4

--- a/solution.py
+++ b/solution.py
@@ -13,6 +13,8 @@
 HALF = 64
 GROUP = 4
 CHUNKS = 8
+BLOCKS = 4
+BLOCK = 4
 
 penalty = 1.0
 
@@ -74,43 +76,36 @@
     return lax.broadcasted_iota(jnp.int32, shape, len(shape) - 1) < HALF
 
 
-def columns_kernel(maps_ref, image_ref, table_ref, *refs):
-    out_refs = refs[:-5]
-    lines_in, both_in, table_in, line_sem, table_sem = refs[-5:]
+def fetch_kernel(maps_ref, image_ref, table_ref, lines_ref, table_in, line_sem, table_sem):
+    rows = maps_ref.shape[0]
+    half = table_ref.shape[0]
+    mine = lax.axis_index("band")
+    copies = [
+        pltpu.make_async_copy(maps_ref, lines_ref.at[:rows], line_sem.at[0]),
+        pltpu.make_async_copy(image_ref, lines_ref.at[rows:], line_sem.at[1]),
+    ]
+    for k in range(half):
+        here = table_in.at[:, k * LANES : (k + 1) * LANES]
+        copies.append(pltpu.make_async_copy(table_ref.at[(mine ^ k) % half], here, table_sem.at[k]))
+    for copy in copies:
+        copy.start()
+    for copy in copies:
+        copy.wait()
+
+
+def columns_kernel(lines_ref, table_ref, *out_refs):
     half = len(out_refs) // 2
-    rows = maps_ref.shape[0]
-    lines = lines_in.shape[0]
-    mine = lax.axis_index("band")
-    maps_copy = pltpu.make_async_copy(maps_ref, lines_in.at[:rows], line_sem.at[0])
-    image_copy = pltpu.make_async_copy(image_ref, lines_in.at[rows:], line_sem.at[1])
-    table_copies = [
-        pltpu.make_async_copy(
-            table_ref.at[(mine ^ k) % half],
-            table_in.at[k // 2, :, k % 2 * LANES : (k % 2 + 1) * LANES],
-            table_sem.at[k],
-        )
-        for k in range(half)
-    ]
-    maps_copy.start()
-    image_copy.start()
-    for copy in table_copies:
-        copy.start()
-    odd = lax.broadcasted_iota(jnp.int32, (1, lines_in.shape[1]), 1) % 2
-    upper = (mine >= half).astype(jnp.int32)
+    odd = lax.broadcasted_iota(jnp.int32, (1, lines_ref.shape[1]), 1) % 2
+    upper = (lax.axis_index("band") >= half).astype(jnp.int32)
     near_sign = (1 - 2 * odd * upper).astype(f32).astype(bf16)
     far_sign = (1 - 2 * odd * (1 - upper)).astype(f32).astype(bf16)
-    maps_copy.wait()
-    image_copy.wait()
-    both_in[:lines] = lines_in[...] * near_sign
-    both_in[lines:] = lines_in[...] * far_sign
-    for k in range(0, half, 2):
-        table_copies[k].wait()
-        table_copies[k + 1].wait()
-        both = jnp.dot(both_in[...], table_in[k // 2], preferred_element_type=f32).astype(bf16)
-        out_refs[k][...] = both[:lines, :LANES]
-        out_refs[k + 1][...] = both[:lines, LANES:]
-        out_refs[half + k][...] = both[lines:, :LANES]
-        out_refs[half + k + 1][...] = both[lines:, LANES:]
+    for first, sign in ((0, near_sign), (half, far_sign)):
+        lines = lines_ref[...] * sign
+        for k in range(0, half, 2):
+            table = table_ref[:, k * LANES : (k + 2) * LANES]
+            both = jnp.dot(lines, table, preferred_element_type=f32).astype(bf16)
+            out_refs[first + k][...] = both[:, :LANES]
+            out_refs[first + k + 1][...] = both[:, LANES:]
 
 
 def prepare_kernel(target_ref, packed_ref, target_in, sems):
@@ -138,8 +133,8 @@
 
 
 def rows_kernel(*refs):
-    got_refs = refs[:-8]
-    table_ref, packed_ref, x_ref, image_ref, own_ref, send_ref, one_ref, two_ref = refs[-8:]
+    got_refs = refs[:-9]
+    table_ref, packed_ref, x_ref, image_ref, own_ref, send_ref, one_ref, two_ref, left_ref = refs[-9:]
     freqs, channels, filters, _ = packed_ref.shape
     sources = len(got_refs)
     band_rows = got_refs[0].shape[0] // (filters + channels)
@@ -147,23 +142,30 @@
     mine = lax.axis_index("band")
     table = jnp.concatenate([table_ref[p, mine ^ k] for p in range(2) for k in far_first(sources)], axis=0)
 
-    def transform(start):
+    starts = [j * pair for j in range(filters // 2)]
+    starts += [(filters + c) * band_rows for c in range(channels - 1)]
+    for i, start in enumerate(starts):
         block = jnp.concatenate([ref[start : start + pair, :] for ref in got_refs], axis=0)
         turned = block.T
-        left = jnp.concatenate([turned[:freqs], turned[freqs:]], axis=1)
-        return jnp.dot(left, table, preferred_element_type=f32)
-
-    for j in range(filters // 2):
-        both = transform(j * pair)
-        x_ref[pl.ds(2 * j, freqs, stride=filters), :] = both[:, :LANES]
-        x_ref[pl.ds(2 * j + 1, freqs, stride=filters), :] = both[:, LANES:]
+        left_ref[i * freqs : (i + 1) * freqs, :LANES] = turned[:freqs]
+        left_ref[i * freqs : (i + 1) * freqs, LANES:] = turned[freqs:]
+    for i in range(0, filters // 2, BLOCK):
+        many = jnp.dot(
+            left_ref[i * freqs : (i + BLOCK) * freqs, :], table, preferred_element_type=f32
+        )
+        for j in range(BLOCK):
+            both = many[j * freqs : (j + 1) * freqs]
+            x_ref[pl.ds(2 * (i + j), freqs, stride=filters), :] = both[:, :LANES]
+            x_ref[pl.ds(2 * (i + j) + 1, freqs, stride=filters), :] = both[:, LANES:]
+    many = jnp.dot(left_ref[filters // 2 * freqs :, :], table, preferred_element_type=f32)
     for c in range(channels):
         first = min(c, channels - 2)
-        both = transform((filters + first) * band_rows)
         part = (c - first) * LANES
-        image_ref[c * freqs : (c + 1) * freqs, :] = both[:, part : part + LANES]
-
-    group = 8
+        image_ref[c * freqs : (c + 1) * freqs, :] = many[
+            first * freqs : (first + 1) * freqs, part : part + LANES
+        ]
+
+    group = 16
 
     def step(i, carry):
         q0 = pl.multiple_of(i * group, group)
@@ -220,7 +222,7 @@
         re_ref[span] = jnp.where(low, coef, -turned)
         im_ref[span] = jnp.where(low, turned, coef)
 
-    chunk = freqs // CHUNKS
+    chunk = freqs // BLOCKS
     mine = lax.axis_index("band")
 
     def step(i, acc):
@@ -252,7 +254,7 @@
             acc = acc + (part[:, :area] + part[:, area:])
         return acc
 
-    acc = lax.fori_loop(0, CHUNKS, step, jnp.zeros(rim_ref.shape, f32))
+    acc = lax.fori_loop(0, BLOCKS, step, jnp.zeros(rim_ref.shape, f32))
     rim_ref[...] = acc.astype(bf16)
 
 
@@ -354,24 +356,27 @@
     def swap(array, k):
         return lax.ppermute(array, "band", [(i, i ^ k) for i in range(bands)])
 
-    chunks = pl.pallas_call(
-        columns_kernel,
-        out_shape=(jax.ShapeDtypeStruct((rows, LANES), bf16),) * bands,
+    lines, table = pl.pallas_call(
+        fetch_kernel,
+        out_shape=(
+            jax.ShapeDtypeStruct((rows, width_cols), bf16),
+            jax.ShapeDtypeStruct((width_cols, bands // 2 * LANES), bf16),
+        ),
         in_specs=[pl.BlockSpec(memory_space=pltpu.HBM)] * 3,
-        scratch_shapes=[
-            pltpu.VMEM((rows, width_cols), bf16),
-            pltpu.VMEM((2 * rows, width_cols), bf16),
-            pltpu.VMEM((bands // 4, width_cols, 2 * LANES), bf16),
-            pltpu.SemaphoreType.DMA((2,)),
-            pltpu.SemaphoreType.DMA((bands // 2,)),
-        ],
+        scratch_shapes=[pltpu.SemaphoreType.DMA((2,)), pltpu.SemaphoreType.DMA((bands // 2,))],
         compiler_params=params(8),
-        name="columns",
+        name="fetch",
     )(
         far(coeff_maps.reshape(filters * band_rows, width_cols)),
         far(image.reshape(channels * band_rows, width_cols)),
         far(jnp.asarray(column_table(width_cols, bands)[: bands // 2])),
     )
+    chunks = pl.pallas_call(
+        columns_kernel,
+        out_shape=(jax.ShapeDtypeStruct((rows, LANES), bf16),) * bands,
+        compiler_params=params(8),
+        name="columns",
+    )(lines, table)
     got = [swap(chunks[k], k) if k else chunks[k] for k in far_first(bands)]
 
     turns = turn_table(width_cols, K, GROUP).reshape(bands, freqs // GROUP, 2 * K * K)
@@ -396,6 +401,7 @@
         scratch_shapes=[
             pltpu.VMEM((lines, LANES), f32),
             pltpu.VMEM((channels * freqs, LANES), f32),
+            pltpu.VMEM(((filters // 2 + channels - 1) * freqs, 2 * LANES), bf16),
         ],
         compiler_params=params(8),
         name="rows",

time: 39.6 us -> 38.6 us (0.975)
  Pallas kernels: 11.3 us -> 10.2 us
    pallas_call x1, Pallas kernels: 2.02 us -> 0.47 us  [body(): pl.pallas_call(columns_kernel, out_shape=(jax.ShapeDtypeStruct((rows, LAN...]
    pallas_call x0 -> x1, Pallas kernels: none -> 1.23 us  [body(): pl.pallas_call(fetch_kernel, out_shape=(jax.ShapeDtypeStruct((rows, width...]
    pallas_call x1, Pallas kernels: 2.73 us -> 2.14 us  [body(): pl.pallas_call(solve_kernel, out_shape=(jax.ShapeDtypeStruct(target.shape...]
  transfers between devices with their start and end apart: 12 -> 12, of which waited for: 6 -> 6; matrix products, arithmetic and copies ran while one was open for 0% -> 0% of each run, Pallas kernels for 9% -> 10%
where the time goes in v5:
time: 38.6 us; the launch traced here: 38.4 us
  starting transfers between devices  18.9 us (49%)
  Pallas kernels  10.2 us (26%)
  waiting for transfers between devices  8.54 us (22%)
  between operations  0.75 us (2%)
    ppermute x11, starting transfers between devices, swap(): return lax.ppermute(array, 'band', [(i, i ^ k) for i in range(bands)])  18.8 us
    ppermute x11, waiting for transfers between devices, swap(): return lax.ppermute(array, 'band', [(i, i ^ k) for i in range(bands)])  7.3 us
    pallas_call x1, Pallas kernels, body(): pl.pallas_call(solve_kernel, out_shape=(jax.ShapeDtypeStruct(target.shape...  2.14 us
    pallas_call x1, Pallas kernels, body(): pl.pallas_call(prepare_kernel, out_shape=jax.ShapeDtypeStruct((freqs, cha...  2.05 us
    pallas_call x1, Pallas kernels, body(): pl.pallas_call(rows_kernel, out_shape=(jax.ShapeDtypeStruct((freqs * filt...  1.88 us
    pallas_call x1, Pallas kernels, body(): pl.pallas_call(write_kernel, out_shape=jax.ShapeDtypeStruct(target.shape,...  1.67 us
    ppermute x1, waiting for transfers between devices, body(): peer = lax.ppermute(sums, 'filt', [(0, 1), (1, 0)])  1.24 us
    pallas_call x1, Pallas kernels, body(): pl.pallas_call(fetch_kernel, out_shape=(jax.ShapeDtypeStruct((rows, width...  1.23 us
  transfers between devices with their start and end apart: 12, of which 6 were waited for; matrix products, arithmetic and copies ran while one was open for 0% of the time, Pallas kernels for 10%

profile of v5, /device:TPU:0, one launch (start us, length us, event | category | flops | bytes accessed | tf_op | source)
XLA Modules:
  0.0 38.4 jit_solution(18215137894893904443)
XLA Ops:
  0.6 1.2 %fetch.1 = (bf16[280,512]{1,0:T(8,128)(2,1)S(1)}, bf16[512,512]{1,0:T(8,128)(2,1)S(1)}) custom-call(bf16[256,512]{1,0:T(8,128)(2,1)} %bitcast.2, bf16[24,512]{1,0:T(8,128)(2,1)} %bitcast.3, bf16[4,512,128]{2,1,0:T(8,128)(2,1)} %constant.8.clone.table_ref), custom_call_target="tpu_custom_call" | custom-call | tf_op jit(solution)/shard_map/fetch/pallas_call | solution.py:359
  1.9 0.5 %columns.1 = (bf16[280,128]{1,0:T(8,128)(2,1)S(1)}, bf16[280,128]{1,0:T(8,128)(2,1)S(1)}, bf16[280,128]{1,0:T(8,128)(2,1)S(1)}, bf16[280,128]{1,0:T(8,128)(2,1)S...) custom-call(bf16[280,512]{1,0:T(8,128)(2,1)S(1)} %get-tuple-element., ...), custom_call_target="tpu_custom_call" | custom-call | tf_op jit(solution)/shard_map/columns/pallas_call | solution.py:374
  2.3 6.0 %collective-permute-start = (bf16[280,128]{1,0:T(8,128)(2,1)S(1)}, bf16[280,128]{1,0:T(8,128)(2,1)S(1)}, u32[]{:S(2)}, u32[]{:S(2)}) collective-permute-start(bf16[280,128]{1,0:T(8,128)(2,1)S(1)} %get-tuple-element.20), channel_id=1, source_target_pairs={{0,14},{2,12},{4,10},{6,8},{8,6},{10,4},{12,2},{14,0},{1,15},{3,13... | collective-permute-start | bytes 215048 | tf_op jit(solution)/shard_map/ppermute | solution.py:357
  8.4 0.5 %collective-permute-start.1 = (bf16[280,128]{1,0:T(8,128)(2,1)S(1)}, bf16[280,128]{1,0:T(8,128)(2,1)S(1)}, u32[]{:S(2)}, u32[]{:S(2)}) collective-permute-start(bf16[280,128]{1,0:T(8,128)(2,1)S(1)} %get-tuple-element.21), channel_id=1, source_target_pairs={{0,2},{2,0},{4,6},{6,4},{8,10},{10,8},{12,14},{14,12},{1,3},{3,1},... | collective-permute-start | bytes 215048 | tf_op jit(solution)/shard_map/ppermute | solution.py:357
  8.9 0.4 collective-permute-start.2
  9.3 1.3 %collective-permute-start.3 = (bf16[280,128]{1,0:T(8,128)(2,1)S(1)}, bf16[280,128]{1,0:T(8,128)(2,1)S(1)}, u32[]{:S(2)}, u32[]{:S(2)}) collective-permute-start(bf16[280,128]{1,0:T(8,128)(2,1)S(1)} %get-tuple-element.23), channel_id=1, source_target_pairs={{0,4},{2,6},{4,0},{6,2},{8,12},{10,14},{12,8},{14,10},{1,5},{3,7},... | collective-permute-start | bytes 215048 | tf_op jit(solution)/shard_map/ppermute | solution.py:357
  10.6 1.2 %collective-permute-start.4 = (bf16[280,128]{1,0:T(8,128)(2,1)S(1)}, bf16[280,128]{1,0:T(8,128)(2,1)S(1)}, u32[]{:S(2)}, u32[]{:S(2)}) collective-permute-start(bf16[280,128]{1,0:T(8,128)(2,1)S(1)} %get-tuple-element.24), channel_id=1, source_target_pairs={{0,6},{2,4},{4,2},{6,0},{8,14},{10,12},{12,10},{14,8},{1,7},{3,5},... | collective-permute-start | bytes 215048 | tf_op jit(solution)/shard_map/ppermute | solution.py:357
  11.9 0.0 collective-permute-done.refs_0_
  11.9 2.9 %collective-permute-start.5 = (bf16[280,128]{1,0:T(8,128)(2,1)S(1)}, bf16[280,128]{1,0:T(8,128)(2,1)S(1)}, u32[]{:S(2)}, u32[]{:S(2)}) collective-permute-start(bf16[280,128]{1,0:T(8,128)(2,1)S(1)} %get-tuple-element.25), channel_id=1, source_target_pairs={{0,8},{2,10},{4,12},{6,14},{8,0},{10,2},{12,4},{14,6},{1,9},{3,11}... | collective-permute-start | bytes 215048 | tf_op jit(solution)/shard_map/ppermute | solution.py:357
  14.8 0.0 collective-permute-done.1.refs_1_
  14.8 0.0 copy-start.2
  14.8 0.5 %collective-permute-start.6 = (bf16[280,128]{1,0:T(8,128)(2,1)S(1)}, bf16[280,128]{1,0:T(8,128)(2,1)S(1)}, u32[]{:S(2)}, u32[]{:S(2)}) collective-permute-start(bf16[280,128]{1,0:T(8,128)(2,1)S(1)} %get-tuple-element.26), channel_id=1, source_target_pairs={{0,12},{2,14},{4,8},{6,10},{8,4},{10,6},{12,0},{14,2},{1,13},{3,15... | collective-permute-start | bytes 215048 | tf_op jit(solution)/shard_map/ppermute | solution.py:357
  15.2 2.0 %prepare.1.refs_9_.packed_ref = f32[64,3,32,128]{3,2,1,0:T(8,128)S(1)} custom-call(bf16[64,2,3,32,64]{4,3,2,1,0:T(8,128)(2,1)} %target_ref.1), custom_call_target="tpu_custom_call" | custom-call | tf_op jit(solution)/shard_map/prepare/pallas_call | solution.py:383
  17.3 0.0 copy-start
  17.3 0.0 copy-start.1
  17.3 0.0 collective-permute-done.2.refs_2_
  17.3 0.0 collective-permute-done.3.refs_3_
  17.3 0.0 collective-permute-done.4.refs_4_
  17.4 2.3 %collective-permute-done.5.refs_5_ = bf16[280,128]{1,0:T(8,128)(2,1)S(1)} collective-permute-done((bf16[280,128]{1,0:T(8,128)(2,1)S(1)}, bf16[280,128]{1,0:T(8,128)(2,1)S(1)}, u32[]{:S(2)}, u32[]{:S(2)}) %collective-permute-start.5) | collective-permute-done | bytes 71712 | tf_op jit(solution)/shard_map/ppermute | solution.py:357
  19.7 1.3 %collective-permute-done.6.refs_6_ = bf16[280,128]{1,0:T(8,128)(2,1)S(1)} collective-permute-done((bf16[280,128]{1,0:T(8,128)(2,1)S(1)}, bf16[280,128]{1,0:T(8,128)(2,1)S(1)}, u32[]{:S(2)}, u32[]{:S(2)}) %collective-permute-start.6) | collective-permute-done | bytes 71712 | tf_op jit(solution)/shard_map/ppermute | solution.py:357
  21.0 0.0 copy-done.2
  21.0 1.9 %rows.1 = (f32[2048,128]{1,0:T(8,128)S(1)}, f32[192,128]{1,0:T(8,128)S(1)}, f32[256,128]{1,0:T(8,128)S(1)}, bf16[256,128]{1,0:T(8,128)(2,1)S(1)}) custom-call(bf16[280,128]{1,0:T(8,128)(2,1)S(1)} %collective-permute-done.refs_0_, bf16[280,128]{1,0:T(8,128)(2,1)S(1)} %collective-permute-done.1.refs_1_, bf16[280,128]{1,0:T(8,128)(2,1)S(1)} %collective-permute-done.2.refs_2_, ...), custom_call_target="tpu_custom_call" | custom-call | tf_op jit(solution)/shard_map/rows/pallas_call | solution.py:393
  22.9 0.1 collective-permute-start.7
  23.0 1.2 %collective-permute-done.7.peer_ref = bf16[256,128]{1,0:T(8,128)(2,1)S(1)} collective-permute-done((bf16[256,128]{1,0:T(8,128)(2,1)S(1)}, bf16[256,128]{1,0:T(8,128)(2,1)S(1)}, u32[]{:S(2)}, u32[]{:S(2)}) %collective-permute-start.7) | collective-permute-done | bytes 65568 | tf_op jit(solution)/shard_map/ppermute | solution.py:410
  24.2 0.0 copy-done
  24.2 0.0 copy-done.1
  24.2 2.1 %solve.1 = (bf16[64,2,3,32,64]{4,3,2,1,0:T(8,128)(2,1)S(1)}, bf16[96,256]{1,0:T(8,128)(2,1)S(1)}) custom-call(f32[2048,128]{1,0:T(8,128)S(1)} %get-tuple-element.28.x_ref, f32[64,3,32,128]{3,2,1,0:T(8,128)S(1)} %prepare.1.refs_9_.packed_ref, f32[192,128]{1,0:T(8,128)S(1)} %get-tuple-element.29.image_ref, f32[256,128]{1,0:T(8,128)S(1)} %get-tuple-element.30.own_ref, ...), custom_call_target="tpu_custom_call" | custom-call | tf_op jit(solution)/shard_map/solve/pallas_call | solution.py:412
  26.4 1.4 %collective-permute-start.8 = (bf16[96,256]{1,0:T(8,128)(2,1)S(1)}, bf16[96,256]{1,0:T(8,128)(2,1)S(1)}, u32[]{:S(2)}, u32[]{:S(2)}) collective-permute-start(bf16[96,256]{1,0:T(8,128)(2,1)S(1)} %get-tuple-element.33.a_ref), channel_id=1, source_target_pairs={{0,2},{2,0},{4,6},{6,4},{8,10},{10,8},{12,14},{14,12},{1,3},{3,1},... | collective-permute-start | bytes 147464 | tf_op jit(solution)/shard_map/ppermute | solution.py:357
  27.8 2.7 %collective-permute-done.8.b_ref = bf16[96,256]{1,0:T(8,128)(2,1)S(1)} collective-permute-done((bf16[96,256]{1,0:T(8,128)(2,1)S(1)}, bf16[96,256]{1,0:T(8,128)(2,1)S(1)}, u32[]{:S(2)}, u32[]{:S(2)}) %collective-permute-start.8) | collective-permute-done | bytes 49184 | tf_op jit(solution)/shard_map/ppermute | solution.py:357
  30.6 1.6 %collective-permute-start.11 = (bf16[96,256]{1,0:T(8,128)(2,1)S(1)}, bf16[96,256]{1,0:T(8,128)(2,1)S(1)}, u32[]{:S(2)}, u32[]{:S(2)}) collective-permute-start(bf16[96,256]{1,0:T(8,128)(2,1)S(1)} %add.1.refs_0_), channel_id=1, source_target_pairs={{0,12},{2,14},{4,8},{6,10},{8,4},{10,6},{12,0},{14,2},{1,13},{3,15... | collective-permute-start | bytes 147464 | tf_op jit(solution)/shard_map/ppermute | solution.py:357
  32.2 0.4 %collective-permute-start.10 = (bf16[96,256]{1,0:T(8,128)(2,1)S(1)}, bf16[96,256]{1,0:T(8,128)(2,1)S(1)}, u32[]{:S(2)}, u32[]{:S(2)}) collective-permute-start(bf16[96,256]{1,0:T(8,128)(2,1)S(1)} %add.1.refs_0_), channel_id=1, source_target_pairs={{0,4},{2,6},{4,0},{6,2},{8,12},{10,14},{12,8},{14,10},{1,5},{3,7},... | collective-permute-start | bytes 147464 | tf_op jit(solution)/shard_map/ppermute | solution.py:357
  32.6 2.4 %collective-permute-start.9 = (bf16[96,256]{1,0:T(8,128)(2,1)S(1)}, bf16[96,256]{1,0:T(8,128)(2,1)S(1)}, u32[]{:S(2)}, u32[]{:S(2)}) collective-permute-start(bf16[96,256]{1,0:T(8,128)(2,1)S(1)} %add.1.refs_0_), channel_id=1, source_target_pairs={{0,8},{2,10},{4,12},{6,14},{8,0},{10,2},{12,4},{14,6},{1,9},{3,11}... | collective-permute-start | bytes 147464 | tf_op jit(solution)/shard_map/ppermute | solution.py:357
  35.0 0.0 copy-start.3
  35.0 1.7 %write.1 = bf16[64,2,3,32,64]{4,3,2,1,0:T(8,128)(2,1)} custom-call(bf16[64,2,3,32,64]{4,3,2,1,0:T(8,128)(2,1)S(1)} %get-tuple-element.32.held_ref), custom_call_target="tpu_custom_call" | custom-call | tf_op jit(solution)/shard_map/write/pallas_call | solution.py:426
  36.7 0.0 collective-permute-done.11.refs_3_
  36.7 0.1 collective-permute-done.10.refs_2_
  36.8 0.8 %collective-permute-done.9.refs_1_ = bf16[96,256]{1,0:T(8,128)(2,1)S(1)} collective-permute-done((bf16[96,256]{1,0:T(8,128)(2,1)S(1)}, bf16[96,256]{1,0:T(8,128)(2,1)S(1)}, u32[]{:S(2)}, u32[]{:S(2)}) %collective-permute-start.9) | collective-permute-done | bytes 49184 | tf_op jit(solution)/shard_map/ppermute | solution.py:357
  37.6 0.0 copy-done.3
  37.6 0.8 %finish.1 = f32[32,768]{1,0:T(8,128)} custom-call(bf16[96,256]{1,0:T(8,128)(2,1)S(1)} %add.1.refs_0_, bf16[96,256]{1,0:T(8,128)(2,1)S(1)} %collective-permute-done.9.refs_1_, bf16[96,256]{1,0:T(8,128)(2,1)S(1)} %collective-permute-done.10.refs_2_, bf16[96,256]{1,0:T(8,128)(2,1)S(1)} %collective-permute-done.11.refs_3_, f32[32,768]{1,0:T(8,128)S(1)} %copy-done.3), custom_call_target="tpu_custom_call" | custom-call | tf_op jit(solution)/shard_map/finish/pallas_call | solution.py:444
  (1 shorter events, 0.0 us)
Async XLA Ops:
  2.3 9.5 %collective-permute-start = (bf16[280,128]{1,0:T(8,128)(2,1)S(1)}, bf16[280,128]{1,0:T(8,128)(2,1)S(1)}, u32[]{:S(2)}, u32[]{:S(2)}) collective-permute-start(bf16[280,128]{1,0:T(8,128)(2,1)S(1)} %get-tuple-element.20), channel_id=1, source_target_pairs={{0,14},{2,12},{4,10},{6,8},{8,6},{10,4},{12,2},{14,0},{1,15},{3,13... | collective-permute-start | bytes 215048 | tf_op jit(solution)/shard_map/ppermute | solution.py:357
  8.4 6.4 %collective-permute-start.1 = (bf16[280,128]{1,0:T(8,128)(2,1)S(1)}, bf16[280,128]{1,0:T(8,128)(2,1)S(1)}, u32[]{:S(2)}, u32[]{:S(2)}) collective-permute-start(bf16[280,128]{1,0:T(8,128)(2,1)S(1)} %get-tuple-element.21), channel_id=1, source_target_pairs={{0,2},{2,0},{4,6},{6,4},{8,10},{10,8},{12,14},{14,12},{1,3},{3,1},... | collective-permute-start | bytes 215048 | tf_op jit(solution)/shard_map/ppermute | solution.py:357
  8.9 8.4 %collective-permute-start.2 = (bf16[280,128]{1,0:T(8,128)(2,1)S(1)}, bf16[280,128]{1,0:T(8,128)(2,1)S(1)}, u32[]{:S(2)}, u32[]{:S(2)}) collective-permute-start(bf16[280,128]{1,0:T(8,128)(2,1)S(1)} %get-tuple-element.22), channel_id=1, source_target_pairs={{0,10},{2,8},{4,14},{6,12},{8,2},{10,0},{12,6},{14,4},{1,11},{3,9}... | collective-permute-start | bytes 215048 | tf_op jit(solution)/shard_map/ppermute | solution.py:357
  9.3 8.1 %collective-permute-start.3 = (bf16[280,128]{1,0:T(8,128)(2,1)S(1)}, bf16[280,128]{1,0:T(8,128)(2,1)S(1)}, u32[]{:S(2)}, u32[]{:S(2)}) collective-permute-start(bf16[280,128]{1,0:T(8,128)(2,1)S(1)} %get-tuple-element.23), channel_id=1, source_target_pairs={{0,4},{2,6},{4,0},{6,2},{8,12},{10,14},{12,8},{14,10},{1,5},{3,7},... | collective-permute-start | bytes 215048 | tf_op jit(solution)/shard_map/ppermute | solution.py:357
  10.6 6.7 %collective-permute-start.4 = (bf16[280,128]{1,0:T(8,128)(2,1)S(1)}, bf16[280,128]{1,0:T(8,128)(2,1)S(1)}, u32[]{:S(2)}, u32[]{:S(2)}) collective-permute-start(bf16[280,128]{1,0:T(8,128)(2,1)S(1)} %get-tuple-element.24), channel_id=1, source_target_pairs={{0,6},{2,4},{4,2},{6,0},{8,14},{10,12},{12,10},{14,8},{1,7},{3,5},... | collective-permute-start | bytes 215048 | tf_op jit(solution)/shard_map/ppermute | solution.py:357
  11.9 7.8 %collective-permute-start.5 = (bf16[280,128]{1,0:T(8,128)(2,1)S(1)}, bf16[280,128]{1,0:T(8,128)(2,1)S(1)}, u32[]{:S(2)}, u32[]{:S(2)}) collective-permute-start(bf16[280,128]{1,0:T(8,128)(2,1)S(1)} %get-tuple-element.25), channel_id=1, source_target_pairs={{0,8},{2,10},{4,12},{6,14},{8,0},{10,2},{12,4},{14,6},{1,9},{3,11}... | collective-permute-start | bytes 215048 | tf_op jit(solution)/shard_map/ppermute | solution.py:357
  14.8 6.2 %copy-start.2 = (bf16[2,8,16,256]{3,2,1,0:T(8,128)(2,1)S(1)}, bf16[2,8,16,256]{3,2,1,0:T(8,128)(2,1)}, u32[]{:S(2)}) copy-start(bf16[2,8,16,256]{3,2,1,0:T(8,128)(2,1)} %constant.9.clone.refs_8_) | copy-start | bytes 393220
  14.8 6.2 %collective-permute-start.6 = (bf16[280,128]{1,0:T(8,128)(2,1)S(1)}, bf16[280,128]{1,0:T(8,128)(2,1)S(1)}, u32[]{:S(2)}, u32[]{:S(2)}) collective-permute-start(bf16[280,128]{1,0:T(8,128)(2,1)S(1)} %get-tuple-element.26), channel_id=1, source_target_pairs={{0,12},{2,14},{4,8},{6,10},{8,4},{10,6},{12,0},{14,2},{1,13},{3,15... | collective-permute-start | bytes 215048 | tf_op jit(solution)/shard_map/ppermute | solution.py:357
  17.3 6.9 %copy-start = (bf16[512,512]{1,0:T(8,128)(2,1)S(1)}, bf16[512,512]{1,0:T(8,128)(2,1)}, u32[]{:S(2)}) copy-start(bf16[512,512]{1,0:T(8,128)(2,1)} %constant.10.clone.inverse_ref) | copy-start | bytes 1572868
  17.3 6.9 %copy-start.1 = (f32[8,16,512]{2,1,0:T(8,128)S(1)}, f32[8,16,512]{2,1,0:T(8,128)}, u32[]{:S(2)}) copy-start(f32[8,16,512]{2,1,0:T(8,128)} %constant.11.clone.turn_ref) | copy-start | bytes 786436
  22.9 1.3 %collective-permute-start.7 = (bf16[256,128]{1,0:T(8,128)(2,1)S(1)}, bf16[256,128]{1,0:T(8,128)(2,1)S(1)}, u32[]{:S(2)}, u32[]{:S(2)}) collective-permute-start(bf16[256,128]{1,0:T(8,128)(2,1)S(1)} %get-tuple-element.31), channel_id=1, source_target_pairs={{0,1},{1,0},{2,3},{3,2},{4,5},{5,4},{6,7},{7,6},{8,9},{9,8},{10,11... | collective-permute-start | bytes 196616 | tf_op jit(solution)/shard_map/ppermute | solution.py:410
  26.4 4.2 %collective-permute-start.8 = (bf16[96,256]{1,0:T(8,128)(2,1)S(1)}, bf16[96,256]{1,0:T(8,128)(2,1)S(1)}, u32[]{:S(2)}, u32[]{:S(2)}) collective-permute-start(bf16[96,256]{1,0:T(8,128)(2,1)S(1)} %get-tuple-element.33.a_ref), channel_id=1, source_target_pairs={{0,2},{2,0},{4,6},{6,4},{8,10},{10,8},{12,14},{14,12},{1,3},{3,1},... | collective-permute-start | bytes 147464 | tf_op jit(solution)/shard_map/ppermute | solution.py:357
  30.6 6.1 %collective-permute-start.11 = (bf16[96,256]{1,0:T(8,128)(2,1)S(1)}, bf16[96,256]{1,0:T(8,128)(2,1)S(1)}, u32[]{:S(2)}, u32[]{:S(2)}) collective-permute-start(bf16[96,256]{1,0:T(8,128)(2,1)S(1)} %add.1.refs_0_), channel_id=1, source_target_pairs={{0,12},{2,14},{4,8},{6,10},{8,4},{10,6},{12,0},{14,2},{1,13},{3,15... | collective-permute-start | bytes 147464 | tf_op jit(solution)/shard_map/ppermute | solution.py:357
  32.2 4.6 %collective-permute-start.10 = (bf16[96,256]{1,0:T(8,128)(2,1)S(1)}, bf16[96,256]{1,0:T(8,128)(2,1)S(1)}, u32[]{:S(2)}, u32[]{:S(2)}) collective-permute-start(bf16[96,256]{1,0:T(8,128)(2,1)S(1)} %add.1.refs_0_), channel_id=1, source_target_pairs={{0,4},{2,6},{4,0},{6,2},{8,12},{10,14},{12,8},{14,10},{1,5},{3,7},... | collective-permute-start | bytes 147464 | tf_op jit(solution)/shard_map/ppermute | solution.py:357
  32.6 5.0 %collective-permute-start.9 = (bf16[96,256]{1,0:T(8,128)(2,1)S(1)}, bf16[96,256]{1,0:T(8,128)(2,1)S(1)}, u32[]{:S(2)}, u32[]{:S(2)}) collective-permute-start(bf16[96,256]{1,0:T(8,128)(2,1)S(1)} %add.1.refs_0_), channel_id=1, source_target_pairs={{0,8},{2,10},{4,12},{6,14},{8,0},{10,2},{12,4},{14,6},{1,9},{3,11}... | collective-permute-start | bytes 147464 | tf_op jit(solution)/shard_map/ppermute | solution.py:357
  35.0 2.6 %copy-start.3 = (f32[32,768]{1,0:T(8,128)S(1)}, f32[32,768]{1,0:T(8,128)}, u32[]{:S(2)}) copy-start(f32[32,768]{1,0:T(8,128)} %refs_4_.1) | copy-start | bytes 294916

commit v6 on v5

--- a/solution.py
+++ b/solution.py
@@ -78,11 +78,16 @@
 
 def fetch_kernel(maps_ref, image_ref, table_ref, lines_ref, table_in, line_sem, table_sem):
     rows = maps_ref.shape[0]
+    first = lax.axis_index("filt") * (rows + image_ref.shape[0] - lines_ref.shape[0])
     half = table_ref.shape[0]
     mine = lax.axis_index("band")
     copies = [
         pltpu.make_async_copy(maps_ref, lines_ref.at[:rows], line_sem.at[0]),
-        pltpu.make_async_copy(image_ref, lines_ref.at[rows:], line_sem.at[1]),
+        pltpu.make_async_copy(
+            image_ref.at[pl.ds(pl.multiple_of(first, 8), lines_ref.shape[0] - rows)],
+            lines_ref.at[rows:],
+            line_sem.at[1],
+        ),
     ]
     for k in range(half):
         here = table_in.at[:, k * LANES : (k + 1) * LANES]
@@ -134,16 +139,16 @@
 
 def rows_kernel(*refs):
     got_refs = refs[:-9]
-    table_ref, packed_ref, x_ref, image_ref, own_ref, send_ref, one_ref, two_ref, left_ref = refs[-9:]
+    table_ref, packed_ref, x_ref, own_ref, send_ref, one_ref, two_ref, lit_ref, left_ref = refs[-9:]
     freqs, channels, filters, _ = packed_ref.shape
     sources = len(got_refs)
-    band_rows = got_refs[0].shape[0] // (filters + channels)
+    band_rows = got_refs[0].shape[0] // (filters + channels - 1)
     pair = 2 * band_rows
     mine = lax.axis_index("band")
     table = jnp.concatenate([table_ref[p, mine ^ k] for p in range(2) for k in far_first(sources)], axis=0)
 
     starts = [j * pair for j in range(filters // 2)]
-    starts += [(filters + c) * band_rows for c in range(channels - 1)]
+    starts += [(filters + c) * band_rows for c in range(channels - 2)]
     for i, start in enumerate(starts):
         block = jnp.concatenate([ref[start : start + pair, :] for ref in got_refs], axis=0)
         turned = block.T
@@ -158,12 +163,18 @@
             x_ref[pl.ds(2 * (i + j), freqs, stride=filters), :] = both[:, :LANES]
             x_ref[pl.ds(2 * (i + j) + 1, freqs, stride=filters), :] = both[:, LANES:]
     many = jnp.dot(left_ref[filters // 2 * freqs :, :], table, preferred_element_type=f32)
+    held = [many[:freqs, :LANES]]
+    for c in range(channels - 2):
+        held.append(many[c * freqs : (c + 1) * freqs, LANES:])
+    core = lax.axis_index("filt").astype(f32)
     for c in range(channels):
-        first = min(c, channels - 2)
-        part = (c - first) * LANES
-        image_ref[c * freqs : (c + 1) * freqs, :] = many[
-            first * freqs : (first + 1) * freqs, part : part + LANES
-        ]
+        share = 1.0 if c in (0, channels - 1) else 0.5
+        lit = jnp.zeros((freqs, LANES), f32)
+        if c < channels - 1:
+            lit = lit + held[c] * (share * (1.0 - core))
+        if c > 0:
+            lit = lit + held[c - 1] * (share * core)
+        lit_ref[c * freqs : (c + 1) * freqs, :] = lit
 
     group = 16
 
@@ -186,6 +197,7 @@
     two = two_ref[...]
     low = low_lanes(one.shape)
     cross = jnp.where(low, one - pltpu.roll(one, HALF, 1), two + pltpu.roll(two, HALF, 1))
+    cross = lit_ref[...] - cross
     energy = one_ref[top:]
     energy = energy + pltpu.roll(energy, HALF, 1)
     own_ref[:top] = cross
@@ -197,7 +209,6 @@
 def solve_kernel(
     x_ref,
     packed_ref,
-    image_ref,
     own_ref,
     peer_ref,
     inverse_ref,
@@ -217,7 +228,7 @@
     low = low_lanes(denom.shape)
     for c in range(channels):
         span = slice(c * freqs, (c + 1) * freqs)
-        coef = (image_ref[span] - total[span]) / denom
+        coef = total[span] / denom
         turned = pltpu.roll(coef, HALF, 1)
         re_ref[span] = jnp.where(low, coef, -turned)
         im_ref[span] = jnp.where(low, turned, coef)
@@ -349,8 +360,10 @@
     bands = lax.axis_size("band")
     height = band_rows * bands
     freqs = width_cols // bands
-    rows = (filters + channels) * band_rows
-    if (2 * freqs, 2 * height, 16 % band_rows, filters % 2, bands & (bands - 1)) != (LANES, LANES, 0, 0, 0):
+    rows = (filters + channels - 1) * band_rows
+    cores = lax.axis_size("filt")
+    fits = (2 * freqs, 2 * height, band_rows, channels, filters % 2, bands & (bands - 1), cores)
+    if fits != (LANES, LANES, 8, 3, 0, 0, 2):
         return plain(coeff_maps, image, target, dual_rim)
 
     def swap(array, k):
@@ -390,18 +403,18 @@
     )(far(target))
 
     lines = (channels + 1) * freqs
-    x, lit, own, sums = pl.pallas_call(
+    x, own, sums = pl.pallas_call(
         rows_kernel,
         out_shape=(
             jax.ShapeDtypeStruct((freqs * filters, LANES), f32),
-            jax.ShapeDtypeStruct((channels * freqs, LANES), f32),
             jax.ShapeDtypeStruct((lines, LANES), f32),
             jax.ShapeDtypeStruct((lines, LANES), bf16),
         ),
         scratch_shapes=[
             pltpu.VMEM((lines, LANES), f32),
             pltpu.VMEM((channels * freqs, LANES), f32),
-            pltpu.VMEM(((filters // 2 + channels - 1) * freqs, 2 * LANES), bf16),
+            pltpu.VMEM((channels * freqs, LANES), f32),
+            pltpu.VMEM(((filters // 2 + channels - 2) * freqs, 2 * LANES), bf16),
         ],
         compiler_params=params(8),
         name="rows",
@@ -421,7 +434,7 @@
         ],
         compiler_params=params(16),
         name="solve",
-    )(x, packed, lit, own, peer, jnp.asarray(inverse_table(height, width_cols, K, GROUP)), jnp.asarray(turns))
+    )(x, packed, own, peer, jnp.asarray(inverse_table(height, width_cols, K, GROUP)), jnp.asarray(turns))
 
     dict_spectra = pl.pallas_call(
         write_kernel,

time: 38.6 us -> 38.2 us (0.990)
  transfers between devices with their start and end apart: 12 -> 12, of which waited for: 6 -> 5; matrix products, arithmetic and copies ran while one was open for 0% -> 0% of each run, Pallas kernels for 10% -> 10%
where the time goes in v6:
time: 38.2 us; the launch traced here: 38.1 us
  starting transfers between devices  18.8 us (49%)
  Pallas kernels  10.2 us (27%)
  waiting for transfers between devices  8.27 us (22%)
  between operations  0.75 us (2%)
    ppermute x11, starting transfers between devices, swap(): return lax.ppermute(array, 'band', [(i, i ^ k) for i in range(bands)])  18.8 us
    ppermute x11, waiting for transfers between devices, swap(): return lax.ppermute(array, 'band', [(i, i ^ k) for i in range(bands)])  7.03 us
    pallas_call x1, Pallas kernels, body(): pl.pallas_call(solve_kernel, out_shape=(jax.ShapeDtypeStruct(target.shape...  2.14 us
    pallas_call x1, Pallas kernels, body(): pl.pallas_call(prepare_kernel, out_shape=jax.ShapeDtypeStruct((freqs, cha...  2.05 us
    pallas_call x1, Pallas kernels, body(): pl.pallas_call(rows_kernel, out_shape=(jax.ShapeDtypeStruct((freqs * filt...  1.9 us
    pallas_call x1, Pallas kernels, body(): pl.pallas_call(write_kernel, out_shape=jax.ShapeDtypeStruct(target.shape,...  1.67 us
    ppermute x1, waiting for transfers between devices, body(): peer = lax.ppermute(sums, 'filt', [(0, 1), (1, 0)])  1.24 us
    pallas_call x1, Pallas kernels, body(): pl.pallas_call(fetch_kernel, out_shape=(jax.ShapeDtypeStruct((rows, width...  1.23 us
  transfers between devices with their start and end apart: 12, of which 5 were waited for; matrix products, arithmetic and copies ran while one was open for 0% of the time, Pallas kernels for 10%

profile of v6, /device:TPU:0, one launch (start us, length us, event | category | flops | bytes accessed | tf_op | source)
XLA Modules:
  0.0 38.1 jit_solution(16079932695216761923)
XLA Ops:
  0.6 1.2 %fetch.1 = (bf16[272,512]{1,0:T(8,128)(2,1)S(1)}, bf16[512,512]{1,0:T(8,128)(2,1)S(1)}) custom-call(bf16[256,512]{1,0:T(8,128)(2,1)} %bitcast.2, bf16[24,512]{1,0:T(8,128)(2,1)} %bitcast.3, bf16[4,512,128]{2,1,0:T(8,128)(2,1)} %constant.8.clone.table_ref), custom_call_target="tpu_custom_call" | custom-call | tf_op jit(solution)/shard_map/fetch/pallas_call | solution.py:372
  1.9 0.5 %columns.1 = (bf16[272,128]{1,0:T(8,128)(2,1)S(1)}, bf16[272,128]{1,0:T(8,128)(2,1)S(1)}, bf16[272,128]{1,0:T(8,128)(2,1)S(1)}, bf16[272,128]{1,0:T(8,128)(2,1)S...) custom-call(bf16[272,512]{1,0:T(8,128)(2,1)S(1)} %get-tuple-element., ...), custom_call_target="tpu_custom_call" | custom-call | tf_op jit(solution)/shard_map/columns/pallas_call | solution.py:387
  2.3 6.0 %collective-permute-start = (bf16[272,128]{1,0:T(8,128)(2,1)S(1)}, bf16[272,128]{1,0:T(8,128)(2,1)S(1)}, u32[]{:S(2)}, u32[]{:S(2)}) collective-permute-start(bf16[272,128]{1,0:T(8,128)(2,1)S(1)} %get-tuple-element.19), channel_id=1, source_target_pairs={{0,14},{2,12},{4,10},{6,8},{8,6},{10,4},{12,2},{14,0},{1,15},{3,13... | collective-permute-start | bytes 208904 | tf_op jit(solution)/shard_map/ppermute | solution.py:370
  8.4 0.5 %collective-permute-start.1 = (bf16[272,128]{1,0:T(8,128)(2,1)S(1)}, bf16[272,128]{1,0:T(8,128)(2,1)S(1)}, u32[]{:S(2)}, u32[]{:S(2)}) collective-permute-start(bf16[272,128]{1,0:T(8,128)(2,1)S(1)} %get-tuple-element.20), channel_id=1, source_target_pairs={{0,2},{2,0},{4,6},{6,4},{8,10},{10,8},{12,14},{14,12},{1,3},{3,1},... | collective-permute-start | bytes 208904 | tf_op jit(solution)/shard_map/ppermute | solution.py:370
  8.9 0.4 collective-permute-start.2
  9.3 1.3 %collective-permute-start.3 = (bf16[272,128]{1,0:T(8,128)(2,1)S(1)}, bf16[272,128]{1,0:T(8,128)(2,1)S(1)}, u32[]{:S(2)}, u32[]{:S(2)}) collective-permute-start(bf16[272,128]{1,0:T(8,128)(2,1)S(1)} %get-tuple-element.22), channel_id=1, source_target_pairs={{0,4},{2,6},{4,0},{6,2},{8,12},{10,14},{12,8},{14,10},{1,5},{3,7},... | collective-permute-start | bytes 208904 | tf_op jit(solution)/shard_map/ppermute | solution.py:370
  10.6 1.2 %collective-permute-start.4 = (bf16[272,128]{1,0:T(8,128)(2,1)S(1)}, bf16[272,128]{1,0:T(8,128)(2,1)S(1)}, u32[]{:S(2)}, u32[]{:S(2)}) collective-permute-start(bf16[272,128]{1,0:T(8,128)(2,1)S(1)} %get-tuple-element.23), channel_id=1, source_target_pairs={{0,6},{2,4},{4,2},{6,0},{8,14},{10,12},{12,10},{14,8},{1,7},{3,5},... | collective-permute-start | bytes 208904 | tf_op jit(solution)/shard_map/ppermute | solution.py:370
  11.9 0.0 collective-permute-done.refs_0_
  11.9 2.9 %collective-permute-start.5 = (bf16[272,128]{1,0:T(8,128)(2,1)S(1)}, bf16[272,128]{1,0:T(8,128)(2,1)S(1)}, u32[]{:S(2)}, u32[]{:S(2)}) collective-permute-start(bf16[272,128]{1,0:T(8,128)(2,1)S(1)} %get-tuple-element.24), channel_id=1, source_target_pairs={{0,8},{2,10},{4,12},{6,14},{8,0},{10,2},{12,4},{14,6},{1,9},{3,11}... | collective-permute-start | bytes 208904 | tf_op jit(solution)/shard_map/ppermute | solution.py:370
  14.8 0.0 collective-permute-done.1.refs_1_
  14.8 0.0 copy-start.2
  14.8 0.4 %collective-permute-start.6 = (bf16[272,128]{1,0:T(8,128)(2,1)S(1)}, bf16[272,128]{1,0:T(8,128)(2,1)S(1)}, u32[]{:S(2)}, u32[]{:S(2)}) collective-permute-start(bf16[272,128]{1,0:T(8,128)(2,1)S(1)} %get-tuple-element.25), channel_id=1, source_target_pairs={{0,12},{2,14},{4,8},{6,10},{8,4},{10,6},{12,0},{14,2},{1,13},{3,15... | collective-permute-start | bytes 208904 | tf_op jit(solution)/shard_map/ppermute | solution.py:370
  15.2 2.0 %prepare.1.refs_9_.packed_ref = f32[64,3,32,128]{3,2,1,0:T(8,128)S(1)} custom-call(bf16[64,2,3,32,64]{4,3,2,1,0:T(8,128)(2,1)} %target_ref.1), custom_call_target="tpu_custom_call" | custom-call | tf_op jit(solution)/shard_map/prepare/pallas_call | solution.py:396
  17.2 0.0 copy-start
  17.3 0.0 copy-start.1
  17.3 0.0 collective-permute-done.2.refs_2_
  17.3 0.0 collective-permute-done.3.refs_3_
  17.3 0.0 collective-permute-done.4.refs_4_
  17.3 2.2 %collective-permute-done.5.refs_5_ = bf16[272,128]{1,0:T(8,128)(2,1)S(1)} collective-permute-done((bf16[272,128]{1,0:T(8,128)(2,1)S(1)}, bf16[272,128]{1,0:T(8,128)(2,1)S(1)}, u32[]{:S(2)}, u32[]{:S(2)}) %collective-permute-start.5) | collective-permute-done | bytes 69664 | tf_op jit(solution)/shard_map/ppermute | solution.py:370
  19.5 1.5 %collective-permute-done.6.refs_6_ = bf16[272,128]{1,0:T(8,128)(2,1)S(1)} collective-permute-done((bf16[272,128]{1,0:T(8,128)(2,1)S(1)}, bf16[272,128]{1,0:T(8,128)(2,1)S(1)}, u32[]{:S(2)}, u32[]{:S(2)}) %collective-permute-start.6) | collective-permute-done | bytes 69664 | tf_op jit(solution)/shard_map/ppermute | solution.py:370
  21.0 0.0 copy-done.2
  21.0 1.9 %rows.1 = (f32[2048,128]{1,0:T(8,128)S(1)}, f32[256,128]{1,0:T(8,128)S(1)}, bf16[256,128]{1,0:T(8,128)(2,1)S(1)}) custom-call(bf16[272,128]{1,0:T(8,128)(2,1)S(1)} %collective-permute-done.refs_0_, bf16[272,128]{1,0:T(8,128)(2,1)S(1)} %collective-permute-done.1.refs_1_, bf16[272,128]{1,0:T(8,128)(2,1)S(1)} %collective-permute-done.2.refs_2_, ...), custom_call_target="tpu_custom_call" | custom-call | tf_op jit(solution)/shard_map/rows/pallas_call | solution.py:406
  22.9 0.1 collective-permute-start.7
  22.9 1.2 %collective-permute-done.7.peer_ref = bf16[256,128]{1,0:T(8,128)(2,1)S(1)} collective-permute-done((bf16[256,128]{1,0:T(8,128)(2,1)S(1)}, bf16[256,128]{1,0:T(8,128)(2,1)S(1)}, u32[]{:S(2)}, u32[]{:S(2)}) %collective-permute-start.7) | collective-permute-done | bytes 65568 | tf_op jit(solution)/shard_map/ppermute | solution.py:423
  24.2 0.0 copy-done
  24.2 0.0 copy-done.1
  24.2 2.1 %solve.1 = (bf16[64,2,3,32,64]{4,3,2,1,0:T(8,128)(2,1)S(1)}, bf16[96,256]{1,0:T(8,128)(2,1)S(1)}) custom-call(f32[2048,128]{1,0:T(8,128)S(1)} %get-tuple-element.27.x_ref, f32[64,3,32,128]{3,2,1,0:T(8,128)S(1)} %prepare.1.refs_9_.packed_ref, f32[256,128]{1,0:T(8,128)S(1)} %get-tuple-element.28.own_ref, bf16[256,128]{1,0:T(8,128)(2,1)S(1)} %collective-permute-done.7.peer_ref, ...), custom_call_target="tpu_custom_call" | custom-call | tf_op jit(solution)/shard_map/solve/pallas_call | solution.py:425
  26.3 1.5 %collective-permute-start.8 = (bf16[96,256]{1,0:T(8,128)(2,1)S(1)}, bf16[96,256]{1,0:T(8,128)(2,1)S(1)}, u32[]{:S(2)}, u32[]{:S(2)}) collective-permute-start(bf16[96,256]{1,0:T(8,128)(2,1)S(1)} %get-tuple-element.31.a_ref), channel_id=1, source_target_pairs={{0,2},{2,0},{4,6},{6,4},{8,10},{10,8},{12,14},{14,12},{1,3},{3,1},... | collective-permute-start | bytes 147464 | tf_op jit(solution)/shard_map/ppermute | solution.py:370
  27.8 2.7 %collective-permute-done.8.b_ref = bf16[96,256]{1,0:T(8,128)(2,1)S(1)} collective-permute-done((bf16[96,256]{1,0:T(8,128)(2,1)S(1)}, bf16[96,256]{1,0:T(8,128)(2,1)S(1)}, u32[]{:S(2)}, u32[]{:S(2)}) %collective-permute-start.8) | collective-permute-done | bytes 49184 | tf_op jit(solution)/shard_map/ppermute | solution.py:370
  30.5 1.4 %collective-permute-start.11 = (bf16[96,256]{1,0:T(8,128)(2,1)S(1)}, bf16[96,256]{1,0:T(8,128)(2,1)S(1)}, u32[]{:S(2)}, u32[]{:S(2)}) collective-permute-start(bf16[96,256]{1,0:T(8,128)(2,1)S(1)} %add.1.refs_0_), channel_id=1, source_target_pairs={{0,12},{2,14},{4,8},{6,10},{8,4},{10,6},{12,0},{14,2},{1,13},{3,15... | collective-permute-start | bytes 147464 | tf_op jit(solution)/shard_map/ppermute | solution.py:370
  31.9 0.4 %collective-permute-start.10 = (bf16[96,256]{1,0:T(8,128)(2,1)S(1)}, bf16[96,256]{1,0:T(8,128)(2,1)S(1)}, u32[]{:S(2)}, u32[]{:S(2)}) collective-permute-start(bf16[96,256]{1,0:T(8,128)(2,1)S(1)} %add.1.refs_0_), channel_id=1, source_target_pairs={{0,4},{2,6},{4,0},{6,2},{8,12},{10,14},{12,8},{14,10},{1,5},{3,7},... | collective-permute-start | bytes 147464 | tf_op jit(solution)/shard_map/ppermute | solution.py:370
  32.3 2.6 %collective-permute-start.9 = (bf16[96,256]{1,0:T(8,128)(2,1)S(1)}, bf16[96,256]{1,0:T(8,128)(2,1)S(1)}, u32[]{:S(2)}, u32[]{:S(2)}) collective-permute-start(bf16[96,256]{1,0:T(8,128)(2,1)S(1)} %add.1.refs_0_), channel_id=1, source_target_pairs={{0,8},{2,10},{4,12},{6,14},{8,0},{10,2},{12,4},{14,6},{1,9},{3,11}... | collective-permute-start | bytes 147464 | tf_op jit(solution)/shard_map/ppermute | solution.py:370
  35.0 0.0 copy-start.3
  35.0 1.7 %write.1 = bf16[64,2,3,32,64]{4,3,2,1,0:T(8,128)(2,1)} custom-call(bf16[64,2,3,32,64]{4,3,2,1,0:T(8,128)(2,1)S(1)} %get-tuple-element.30.held_ref), custom_call_target="tpu_custom_call" | custom-call | tf_op jit(solution)/shard_map/write/pallas_call | solution.py:439
  36.7 0.0 collective-permute-done.11.refs_3_
  36.7 0.0 collective-permute-done.10.refs_2_
  36.7 0.6 %collective-permute-done.9.refs_1_ = bf16[96,256]{1,0:T(8,128)(2,1)S(1)} collective-permute-done((bf16[96,256]{1,0:T(8,128)(2,1)S(1)}, bf16[96,256]{1,0:T(8,128)(2,1)S(1)}, u32[]{:S(2)}, u32[]{:S(2)}) %collective-permute-start.9) | collective-permute-done | bytes 49184 | tf_op jit(solution)/shard_map/ppermute | solution.py:370
  37.3 0.0 copy-done.3
  37.3 0.8 %finish.1 = f32[32,768]{1,0:T(8,128)} custom-call(bf16[96,256]{1,0:T(8,128)(2,1)S(1)} %add.1.refs_0_, bf16[96,256]{1,0:T(8,128)(2,1)S(1)} %collective-permute-done.9.refs_1_, bf16[96,256]{1,0:T(8,128)(2,1)S(1)} %collective-permute-done.10.refs_2_, bf16[96,256]{1,0:T(8,128)(2,1)S(1)} %collective-permute-done.11.refs_3_, f32[32,768]{1,0:T(8,128)S(1)} %copy-done.3), custom_call_target="tpu_custom_call" | custom-call | tf_op jit(solution)/shard_map/finish/pallas_call | solution.py:457
  (1 shorter events, 0.0 us)
Async XLA Ops:
  2.3 9.5 %collective-permute-start = (bf16[272,128]{1,0:T(8,128)(2,1)S(1)}, bf16[272,128]{1,0:T(8,128)(2,1)S(1)}, u32[]{:S(2)}, u32[]{:S(2)}) collective-permute-start(bf16[272,128]{1,0:T(8,128)(2,1)S(1)} %get-tuple-element.19), channel_id=1, source_target_pairs={{0,14},{2,12},{4,10},{6,8},{8,6},{10,4},{12,2},{14,0},{1,15},{3,13... | collective-permute-start | bytes 208904 | tf_op jit(solution)/shard_map/ppermute | solution.py:370
  8.4 6.4 %collective-permute-start.1 = (bf16[272,128]{1,0:T(8,128)(2,1)S(1)}, bf16[272,128]{1,0:T(8,128)(2,1)S(1)}, u32[]{:S(2)}, u32[]{:S(2)}) collective-permute-start(bf16[272,128]{1,0:T(8,128)(2,1)S(1)} %get-tuple-element.20), channel_id=1, source_target_pairs={{0,2},{2,0},{4,6},{6,4},{8,10},{10,8},{12,14},{14,12},{1,3},{3,1},... | collective-permute-start | bytes 208904 | tf_op jit(solution)/shard_map/ppermute | solution.py:370
  8.9 8.4 %collective-permute-start.2 = (bf16[272,128]{1,0:T(8,128)(2,1)S(1)}, bf16[272,128]{1,0:T(8,128)(2,1)S(1)}, u32[]{:S(2)}, u32[]{:S(2)}) collective-permute-start(bf16[272,128]{1,0:T(8,128)(2,1)S(1)} %get-tuple-element.21), channel_id=1, source_target_pairs={{0,10},{2,8},{4,14},{6,12},{8,2},{10,0},{12,6},{14,4},{1,11},{3,9}... | collective-permute-start | bytes 208904 | tf_op jit(solution)/shard_map/ppermute | solution.py:370
  9.3 8.0 %collective-permute-start.3 = (bf16[272,128]{1,0:T(8,128)(2,1)S(1)}, bf16[272,128]{1,0:T(8,128)(2,1)S(1)}, u32[]{:S(2)}, u32[]{:S(2)}) collective-permute-start(bf16[272,128]{1,0:T(8,128)(2,1)S(1)} %get-tuple-element.22), channel_id=1, source_target_pairs={{0,4},{2,6},{4,0},{6,2},{8,12},{10,14},{12,8},{14,10},{1,5},{3,7},... | collective-permute-start | bytes 208904 | tf_op jit(solution)/shard_map/ppermute | solution.py:370
  10.6 6.7 %collective-permute-start.4 = (bf16[272,128]{1,0:T(8,128)(2,1)S(1)}, bf16[272,128]{1,0:T(8,128)(2,1)S(1)}, u32[]{:S(2)}, u32[]{:S(2)}) collective-permute-start(bf16[272,128]{1,0:T(8,128)(2,1)S(1)} %get-tuple-element.23), channel_id=1, source_target_pairs={{0,6},{2,4},{4,2},{6,0},{8,14},{10,12},{12,10},{14,8},{1,7},{3,5},... | collective-permute-start | bytes 208904 | tf_op jit(solution)/shard_map/ppermute | solution.py:370
  11.9 7.6 %collective-permute-start.5 = (bf16[272,128]{1,0:T(8,128)(2,1)S(1)}, bf16[272,128]{1,0:T(8,128)(2,1)S(1)}, u32[]{:S(2)}, u32[]{:S(2)}) collective-permute-start(bf16[272,128]{1,0:T(8,128)(2,1)S(1)} %get-tuple-element.24), channel_id=1, source_target_pairs={{0,8},{2,10},{4,12},{6,14},{8,0},{10,2},{12,4},{14,6},{1,9},{3,11}... | collective-permute-start | bytes 208904 | tf_op jit(solution)/shard_map/ppermute | solution.py:370
  14.8 6.2 %copy-start.2 = (bf16[2,8,16,256]{3,2,1,0:T(8,128)(2,1)S(1)}, bf16[2,8,16,256]{3,2,1,0:T(8,128)(2,1)}, u32[]{:S(2)}) copy-start(bf16[2,8,16,256]{3,2,1,0:T(8,128)(2,1)} %constant.9.clone.refs_8_) | copy-start | bytes 393220
  14.8 6.2 %collective-permute-start.6 = (bf16[272,128]{1,0:T(8,128)(2,1)S(1)}, bf16[272,128]{1,0:T(8,128)(2,1)S(1)}, u32[]{:S(2)}, u32[]{:S(2)}) collective-permute-start(bf16[272,128]{1,0:T(8,128)(2,1)S(1)} %get-tuple-element.25), channel_id=1, source_target_pairs={{0,12},{2,14},{4,8},{6,10},{8,4},{10,6},{12,0},{14,2},{1,13},{3,15... | collective-permute-start | bytes 208904 | tf_op jit(solution)/shard_map/ppermute | solution.py:370
  17.2 7.0 %copy-start = (bf16[512,512]{1,0:T(8,128)(2,1)S(1)}, bf16[512,512]{1,0:T(8,128)(2,1)}, u32[]{:S(2)}) copy-start(bf16[512,512]{1,0:T(8,128)(2,1)} %constant.10.clone.inverse_ref) | copy-start | bytes 1572868
  17.3 6.9 %copy-start.1 = (f32[8,16,512]{2,1,0:T(8,128)S(1)}, f32[8,16,512]{2,1,0:T(8,128)}, u32[]{:S(2)}) copy-start(f32[8,16,512]{2,1,0:T(8,128)} %constant.11.clone.turn_ref) | copy-start | bytes 786436
  22.9 1.3 %collective-permute-start.7 = (bf16[256,128]{1,0:T(8,128)(2,1)S(1)}, bf16[256,128]{1,0:T(8,128)(2,1)S(1)}, u32[]{:S(2)}, u32[]{:S(2)}) collective-permute-start(bf16[256,128]{1,0:T(8,128)(2,1)S(1)} %get-tuple-element.29), channel_id=1, source_target_pairs={{0,1},{1,0},{2,3},{3,2},{4,5},{5,4},{6,7},{7,6},{8,9},{9,8},{10,11... | collective-permute-start | bytes 196616 | tf_op jit(solution)/shard_map/ppermute | solution.py:423
  26.3 4.2 %collective-permute-start.8 = (bf16[96,256]{1,0:T(8,128)(2,1)S(1)}, bf16[96,256]{1,0:T(8,128)(2,1)S(1)}, u32[]{:S(2)}, u32[]{:S(2)}) collective-permute-start(bf16[96,256]{1,0:T(8,128)(2,1)S(1)} %get-tuple-element.31.a_ref), channel_id=1, source_target_pairs={{0,2},{2,0},{4,6},{6,4},{8,10},{10,8},{12,14},{14,12},{1,3},{3,1},... | collective-permute-start | bytes 147464 | tf_op jit(solution)/shard_map/ppermute | solution.py:370
  30.5 6.1 %collective-permute-start.11 = (bf16[96,256]{1,0:T(8,128)(2,1)S(1)}, bf16[96,256]{1,0:T(8,128)(2,1)S(1)}, u32[]{:S(2)}, u32[]{:S(2)}) collective-permute-start(bf16[96,256]{1,0:T(8,128)(2,1)S(1)} %add.1.refs_0_), channel_id=1, source_target_pairs={{0,12},{2,14},{4,8},{6,10},{8,4},{10,6},{12,0},{14,2},{1,13},{3,15... | collective-permute-start | bytes 147464 | tf_op jit(solution)/shard_map/ppermute | solution.py:370
  31.9 4.7 %collective-permute-start.10 = (bf16[96,256]{1,0:T(8,128)(2,1)S(1)}, bf16[96,256]{1,0:T(8,128)(2,1)S(1)}, u32[]{:S(2)}, u32[]{:S(2)}) collective-permute-start(bf16[96,256]{1,0:T(8,128)(2,1)S(1)} %add.1.refs_0_), channel_id=1, source_target_pairs={{0,4},{2,6},{4,0},{6,2},{8,12},{10,14},{12,8},{14,10},{1,5},{3,7},... | collective-permute-start | bytes 147464 | tf_op jit(solution)/shard_map/ppermute | solution.py:370
  32.3 5.0 %collective-permute-start.9 = (bf16[96,256]{1,0:T(8,128)(2,1)S(1)}, bf16[96,256]{1,0:T(8,128)(2,1)S(1)}, u32[]{:S(2)}, u32[]{:S(2)}) collective-permute-start(bf16[96,256]{1,0:T(8,128)(2,1)S(1)} %add.1.refs_0_), channel_id=1, source_target_pairs={{0,8},{2,10},{4,12},{6,14},{8,0},{10,2},{12,4},{14,6},{1,9},{3,11}... | collective-permute-start | bytes 147464 | tf_op jit(solution)/shard_map/ppermute | solution.py:370
  35.0 2.4 %copy-start.3 = (f32[32,768]{1,0:T(8,128)S(1)}, f32[32,768]{1,0:T(8,128)}, u32[]{:S(2)}) copy-start(f32[32,768]{1,0:T(8,128)} %refs_4_.1) | copy-start | bytes 294916

commit v7 on v6

--- a/solution.py
+++ b/solution.py
@@ -11,7 +11,7 @@
 K = 16
 LANES = 128
 HALF = 64
-GROUP = 4
+GROUP = 2
 CHUNKS = 8
 BLOCKS = 4
 BLOCK = 4

time: 38.2 us -> 38.1 us (level)
  no operation moved by 1% of the time
where the time goes in v7:
time: 38.1 us; the launch traced here: 37.9 us
  starting transfers between devices  18.8 us (49%)
  Pallas kernels  10 us (26%)
  waiting for transfers between devices  8.26 us (22%)
  between operations  0.75 us (2%)
    ppermute x11, starting transfers between devices, swap(): return lax.ppermute(array, 'band', [(i, i ^ k) for i in range(bands)])  18.8 us
    ppermute x11, waiting for transfers between devices, swap(): return lax.ppermute(array, 'band', [(i, i ^ k) for i in range(bands)])  7.02 us
    pallas_call x1, Pallas kernels, body(): pl.pallas_call(prepare_kernel, out_shape=jax.ShapeDtypeStruct((freqs, cha...  2.05 us
    pallas_call x1, Pallas kernels, body(): pl.pallas_call(solve_kernel, out_shape=(jax.ShapeDtypeStruct(target.shape...  1.96 us
    pallas_call x1, Pallas kernels, body(): pl.pallas_call(rows_kernel, out_shape=(jax.ShapeDtypeStruct((freqs * filt...  1.9 us
    pallas_call x1, Pallas kernels, body(): pl.pallas_call(write_kernel, out_shape=jax.ShapeDtypeStruct(target.shape,...  1.67 us
    ppermute x1, waiting for transfers between devices, body(): peer = lax.ppermute(sums, 'filt', [(0, 1), (1, 0)])  1.24 us
    pallas_call x1, Pallas kernels, body(): pl.pallas_call(fetch_kernel, out_shape=(jax.ShapeDtypeStruct((rows, width...  1.23 us
  transfers between devices with their start and end apart: 12, of which 5 were waited for; matrix products, arithmetic and copies ran while one was open for 0% of the time, Pallas kernels for 10%

profile of v7, /device:TPU:0, one launch (start us, length us, event | category | flops | bytes accessed | tf_op | source)
XLA Modules:
  0.0 37.9 jit_solution(10612614148160431526)
XLA Ops:
  0.6 1.2 %fetch.1 = (bf16[272,512]{1,0:T(8,128)(2,1)S(1)}, bf16[512,512]{1,0:T(8,128)(2,1)S(1)}) custom-call(bf16[256,512]{1,0:T(8,128)(2,1)} %bitcast.2, bf16[24,512]{1,0:T(8,128)(2,1)} %bitcast.3, bf16[4,512,128]{2,1,0:T(8,128)(2,1)} %constant.8.clone.table_ref), custom_call_target="tpu_custom_call" | custom-call | tf_op jit(solution)/shard_map/fetch/pallas_call | solution.py:372
  1.9 0.5 %columns.1 = (bf16[272,128]{1,0:T(8,128)(2,1)S(1)}, bf16[272,128]{1,0:T(8,128)(2,1)S(1)}, bf16[272,128]{1,0:T(8,128)(2,1)S(1)}, bf16[272,128]{1,0:T(8,128)(2,1)S...) custom-call(bf16[272,512]{1,0:T(8,128)(2,1)S(1)} %get-tuple-element., ...), custom_call_target="tpu_custom_call" | custom-call | tf_op jit(solution)/shard_map/columns/pallas_call | solution.py:387
  2.3 6.0 %collective-permute-start = (bf16[272,128]{1,0:T(8,128)(2,1)S(1)}, bf16[272,128]{1,0:T(8,128)(2,1)S(1)}, u32[]{:S(2)}, u32[]{:S(2)}) collective-permute-start(bf16[272,128]{1,0:T(8,128)(2,1)S(1)} %get-tuple-element.19), channel_id=1, source_target_pairs={{0,14},{2,12},{4,10},{6,8},{8,6},{10,4},{12,2},{14,0},{1,15},{3,13... | collective-permute-start | bytes 208904 | tf_op jit(solution)/shard_map/ppermute | solution.py:370
  8.4 0.5 %collective-permute-start.1 = (bf16[272,128]{1,0:T(8,128)(2,1)S(1)}, bf16[272,128]{1,0:T(8,128)(2,1)S(1)}, u32[]{:S(2)}, u32[]{:S(2)}) collective-permute-start(bf16[272,128]{1,0:T(8,128)(2,1)S(1)} %get-tuple-element.20), channel_id=1, source_target_pairs={{0,2},{2,0},{4,6},{6,4},{8,10},{10,8},{12,14},{14,12},{1,3},{3,1},... | collective-permute-start | bytes 208904 | tf_op jit(solution)/shard_map/ppermute | solution.py:370
  8.9 0.4 collective-permute-start.2
  9.3 1.3 %collective-permute-start.3 = (bf16[272,128]{1,0:T(8,128)(2,1)S(1)}, bf16[272,128]{1,0:T(8,128)(2,1)S(1)}, u32[]{:S(2)}, u32[]{:S(2)}) collective-permute-start(bf16[272,128]{1,0:T(8,128)(2,1)S(1)} %get-tuple-element.22), channel_id=1, source_target_pairs={{0,4},{2,6},{4,0},{6,2},{8,12},{10,14},{12,8},{14,10},{1,5},{3,7},... | collective-permute-start | bytes 208904 | tf_op jit(solution)/shard_map/ppermute | solution.py:370
  10.6 1.2 %collective-permute-start.4 = (bf16[272,128]{1,0:T(8,128)(2,1)S(1)}, bf16[272,128]{1,0:T(8,128)(2,1)S(1)}, u32[]{:S(2)}, u32[]{:S(2)}) collective-permute-start(bf16[272,128]{1,0:T(8,128)(2,1)S(1)} %get-tuple-element.23), channel_id=1, source_target_pairs={{0,6},{2,4},{4,2},{6,0},{8,14},{10,12},{12,10},{14,8},{1,7},{3,5},... | collective-permute-start | bytes 208904 | tf_op jit(solution)/shard_map/ppermute | solution.py:370
  11.9 0.0 collective-permute-done.refs_0_
  11.9 2.9 %collective-permute-start.5 = (bf16[272,128]{1,0:T(8,128)(2,1)S(1)}, bf16[272,128]{1,0:T(8,128)(2,1)S(1)}, u32[]{:S(2)}, u32[]{:S(2)}) collective-permute-start(bf16[272,128]{1,0:T(8,128)(2,1)S(1)} %get-tuple-element.24), channel_id=1, source_target_pairs={{0,8},{2,10},{4,12},{6,14},{8,0},{10,2},{12,4},{14,6},{1,9},{3,11}... | collective-permute-start | bytes 208904 | tf_op jit(solution)/shard_map/ppermute | solution.py:370
  14.8 0.0 collective-permute-done.1.refs_1_
  14.8 0.0 copy-start.2
  14.8 0.4 %collective-permute-start.6 = (bf16[272,128]{1,0:T(8,128)(2,1)S(1)}, bf16[272,128]{1,0:T(8,128)(2,1)S(1)}, u32[]{:S(2)}, u32[]{:S(2)}) collective-permute-start(bf16[272,128]{1,0:T(8,128)(2,1)S(1)} %get-tuple-element.25), channel_id=1, source_target_pairs={{0,12},{2,14},{4,8},{6,10},{8,4},{10,6},{12,0},{14,2},{1,13},{3,15... | collective-permute-start | bytes 208904 | tf_op jit(solution)/shard_map/ppermute | solution.py:370
  15.2 2.0 %prepare.1.refs_9_.packed_ref = f32[64,3,32,128]{3,2,1,0:T(8,128)S(1)} custom-call(bf16[64,2,3,32,64]{4,3,2,1,0:T(8,128)(2,1)} %target_ref.1), custom_call_target="tpu_custom_call" | custom-call | tf_op jit(solution)/shard_map/prepare/pallas_call | solution.py:396
  17.2 0.0 copy-start
  17.3 0.0 copy-start.1
  17.3 0.0 collective-permute-done.2.refs_2_
  17.3 0.0 collective-permute-done.3.refs_3_
  17.3 0.0 collective-permute-done.4.refs_4_
  17.3 2.2 %collective-permute-done.5.refs_5_ = bf16[272,128]{1,0:T(8,128)(2,1)S(1)} collective-permute-done((bf16[272,128]{1,0:T(8,128)(2,1)S(1)}, bf16[272,128]{1,0:T(8,128)(2,1)S(1)}, u32[]{:S(2)}, u32[]{:S(2)}) %collective-permute-start.5) | collective-permute-done | bytes 69664 | tf_op jit(solution)/shard_map/ppermute | solution.py:370
  19.5 1.5 %collective-permute-done.6.refs_6_ = bf16[272,128]{1,0:T(8,128)(2,1)S(1)} collective-permute-done((bf16[272,128]{1,0:T(8,128)(2,1)S(1)}, bf16[272,128]{1,0:T(8,128)(2,1)S(1)}, u32[]{:S(2)}, u32[]{:S(2)}) %collective-permute-start.6) | collective-permute-done | bytes 69664 | tf_op jit(solution)/shard_map/ppermute | solution.py:370
  21.0 0.0 copy-done.2
  21.0 1.9 %rows.1 = (f32[2048,128]{1,0:T(8,128)S(1)}, f32[256,128]{1,0:T(8,128)S(1)}, bf16[256,128]{1,0:T(8,128)(2,1)S(1)}) custom-call(bf16[272,128]{1,0:T(8,128)(2,1)S(1)} %collective-permute-done.refs_0_, bf16[272,128]{1,0:T(8,128)(2,1)S(1)} %collective-permute-done.1.refs_1_, bf16[272,128]{1,0:T(8,128)(2,1)S(1)} %collective-permute-done.2.refs_2_, ...), custom_call_target="tpu_custom_call" | custom-call | tf_op jit(solution)/shard_map/rows/pallas_call | solution.py:406
  22.9 0.1 collective-permute-start.7
  22.9 1.2 %collective-permute-done.7.peer_ref = bf16[256,128]{1,0:T(8,128)(2,1)S(1)} collective-permute-done((bf16[256,128]{1,0:T(8,128)(2,1)S(1)}, bf16[256,128]{1,0:T(8,128)(2,1)S(1)}, u32[]{:S(2)}, u32[]{:S(2)}) %collective-permute-start.7) | collective-permute-done | bytes 65568 | tf_op jit(solution)/shard_map/ppermute | solution.py:423
  24.2 0.0 copy-done
  24.2 0.0 copy-done.1
  24.2 2.0 %solve.1 = (bf16[64,2,3,32,64]{4,3,2,1,0:T(8,128)(2,1)S(1)}, bf16[96,256]{1,0:T(8,128)(2,1)S(1)}) custom-call(f32[2048,128]{1,0:T(8,128)S(1)} %get-tuple-element.27.x_ref, f32[64,3,32,128]{3,2,1,0:T(8,128)S(1)} %prepare.1.refs_9_.packed_ref, f32[256,128]{1,0:T(8,128)S(1)} %get-tuple-element.28.own_ref, bf16[256,128]{1,0:T(8,128)(2,1)S(1)} %collective-permute-done.7.peer_ref, ...), custom_call_target="tpu_custom_call" | custom-call | tf_op jit(solution)/shard_map/solve/pallas_call | solution.py:425
  26.2 1.5 %collective-permute-start.8 = (bf16[96,256]{1,0:T(8,128)(2,1)S(1)}, bf16[96,256]{1,0:T(8,128)(2,1)S(1)}, u32[]{:S(2)}, u32[]{:S(2)}) collective-permute-start(bf16[96,256]{1,0:T(8,128)(2,1)S(1)} %get-tuple-element.31.a_ref), channel_id=1, source_target_pairs={{0,2},{2,0},{4,6},{6,4},{8,10},{10,8},{12,14},{14,12},{1,3},{3,1},... | collective-permute-start | bytes 147464 | tf_op jit(solution)/shard_map/ppermute | solution.py:370
  27.6 2.7 %collective-permute-done.8.b_ref = bf16[96,256]{1,0:T(8,128)(2,1)S(1)} collective-permute-done((bf16[96,256]{1,0:T(8,128)(2,1)S(1)}, bf16[96,256]{1,0:T(8,128)(2,1)S(1)}, u32[]{:S(2)}, u32[]{:S(2)}) %collective-permute-start.8) | collective-permute-done | bytes 49184 | tf_op jit(solution)/shard_map/ppermute | solution.py:370
  30.3 1.4 %collective-permute-start.11 = (bf16[96,256]{1,0:T(8,128)(2,1)S(1)}, bf16[96,256]{1,0:T(8,128)(2,1)S(1)}, u32[]{:S(2)}, u32[]{:S(2)}) collective-permute-start(bf16[96,256]{1,0:T(8,128)(2,1)S(1)} %add.1.refs_0_), channel_id=1, source_target_pairs={{0,12},{2,14},{4,8},{6,10},{8,4},{10,6},{12,0},{14,2},{1,13},{3,15... | collective-permute-start | bytes 147464 | tf_op jit(solution)/shard_map/ppermute | solution.py:370
  31.8 0.4 %collective-permute-start.10 = (bf16[96,256]{1,0:T(8,128)(2,1)S(1)}, bf16[96,256]{1,0:T(8,128)(2,1)S(1)}, u32[]{:S(2)}, u32[]{:S(2)}) collective-permute-start(bf16[96,256]{1,0:T(8,128)(2,1)S(1)} %add.1.refs_0_), channel_id=1, source_target_pairs={{0,4},{2,6},{4,0},{6,2},{8,12},{10,14},{12,8},{14,10},{1,5},{3,7},... | collective-permute-start | bytes 147464 | tf_op jit(solution)/shard_map/ppermute | solution.py:370
  32.2 2.6 %collective-permute-start.9 = (bf16[96,256]{1,0:T(8,128)(2,1)S(1)}, bf16[96,256]{1,0:T(8,128)(2,1)S(1)}, u32[]{:S(2)}, u32[]{:S(2)}) collective-permute-start(bf16[96,256]{1,0:T(8,128)(2,1)S(1)} %add.1.refs_0_), channel_id=1, source_target_pairs={{0,8},{2,10},{4,12},{6,14},{8,0},{10,2},{12,4},{14,6},{1,9},{3,11}... | collective-permute-start | bytes 147464 | tf_op jit(solution)/shard_map/ppermute | solution.py:370
  34.8 0.0 copy-start.3
  34.8 1.7 %write.1 = bf16[64,2,3,32,64]{4,3,2,1,0:T(8,128)(2,1)} custom-call(bf16[64,2,3,32,64]{4,3,2,1,0:T(8,128)(2,1)S(1)} %get-tuple-element.30.held_ref), custom_call_target="tpu_custom_call" | custom-call | tf_op jit(solution)/shard_map/write/pallas_call | solution.py:439
  36.5 0.0 collective-permute-done.11.refs_3_
  36.5 0.0 collective-permute-done.10.refs_2_
  36.5 0.7 %collective-permute-done.9.refs_1_ = bf16[96,256]{1,0:T(8,128)(2,1)S(1)} collective-permute-done((bf16[96,256]{1,0:T(8,128)(2,1)S(1)}, bf16[96,256]{1,0:T(8,128)(2,1)S(1)}, u32[]{:S(2)}, u32[]{:S(2)}) %collective-permute-start.9) | collective-permute-done | bytes 49184 | tf_op jit(solution)/shard_map/ppermute | solution.py:370
  37.1 0.0 copy-done.3
  37.2 0.8 %finish.1 = f32[32,768]{1,0:T(8,128)} custom-call(bf16[96,256]{1,0:T(8,128)(2,1)S(1)} %add.1.refs_0_, bf16[96,256]{1,0:T(8,128)(2,1)S(1)} %collective-permute-done.9.refs_1_, bf16[96,256]{1,0:T(8,128)(2,1)S(1)} %collective-permute-done.10.refs_2_, bf16[96,256]{1,0:T(8,128)(2,1)S(1)} %collective-permute-done.11.refs_3_, f32[32,768]{1,0:T(8,128)S(1)} %copy-done.3), custom_call_target="tpu_custom_call" | custom-call | tf_op jit(solution)/shard_map/finish/pallas_call | solution.py:457
  (1 shorter events, 0.0 us)
Async XLA Ops:
  2.3 9.5 %collective-permute-start = (bf16[272,128]{1,0:T(8,128)(2,1)S(1)}, bf16[272,128]{1,0:T(8,128)(2,1)S(1)}, u32[]{:S(2)}, u32[]{:S(2)}) collective-permute-start(bf16[272,128]{1,0:T(8,128)(2,1)S(1)} %get-tuple-element.19), channel_id=1, source_target_pairs={{0,14},{2,12},{4,10},{6,8},{8,6},{10,4},{12,2},{14,0},{1,15},{3,13... | collective-permute-start | bytes 208904 | tf_op jit(solution)/shard_map/ppermute | solution.py:370
  8.4 6.4 %collective-permute-start.1 = (bf16[272,128]{1,0:T(8,128)(2,1)S(1)}, bf16[272,128]{1,0:T(8,128)(2,1)S(1)}, u32[]{:S(2)}, u32[]{:S(2)}) collective-permute-start(bf16[272,128]{1,0:T(8,128)(2,1)S(1)} %get-tuple-element.20), channel_id=1, source_target_pairs={{0,2},{2,0},{4,6},{6,4},{8,10},{10,8},{12,14},{14,12},{1,3},{3,1},... | collective-permute-start | bytes 208904 | tf_op jit(solution)/shard_map/ppermute | solution.py:370
  8.9 8.4 %collective-permute-start.2 = (bf16[272,128]{1,0:T(8,128)(2,1)S(1)}, bf16[272,128]{1,0:T(8,128)(2,1)S(1)}, u32[]{:S(2)}, u32[]{:S(2)}) collective-permute-start(bf16[272,128]{1,0:T(8,128)(2,1)S(1)} %get-tuple-element.21), channel_id=1, source_target_pairs={{0,10},{2,8},{4,14},{6,12},{8,2},{10,0},{12,6},{14,4},{1,11},{3,9}... | collective-permute-start | bytes 208904 | tf_op jit(solution)/shard_map/ppermute | solution.py:370
  9.3 8.0 %collective-permute-start.3 = (bf16[272,128]{1,0:T(8,128)(2,1)S(1)}, bf16[272,128]{1,0:T(8,128)(2,1)S(1)}, u32[]{:S(2)}, u32[]{:S(2)}) collective-permute-start(bf16[272,128]{1,0:T(8,128)(2,1)S(1)} %get-tuple-element.22), channel_id=1, source_target_pairs={{0,4},{2,6},{4,0},{6,2},{8,12},{10,14},{12,8},{14,10},{1,5},{3,7},... | collective-permute-start | bytes 208904 | tf_op jit(solution)/shard_map/ppermute | solution.py:370
  10.6 6.7 %collective-permute-start.4 = (bf16[272,128]{1,0:T(8,128)(2,1)S(1)}, bf16[272,128]{1,0:T(8,128)(2,1)S(1)}, u32[]{:S(2)}, u32[]{:S(2)}) collective-permute-start(bf16[272,128]{1,0:T(8,128)(2,1)S(1)} %get-tuple-element.23), channel_id=1, source_target_pairs={{0,6},{2,4},{4,2},{6,0},{8,14},{10,12},{12,10},{14,8},{1,7},{3,5},... | collective-permute-start | bytes 208904 | tf_op jit(solution)/shard_map/ppermute | solution.py:370
  11.9 7.6 %collective-permute-start.5 = (bf16[272,128]{1,0:T(8,128)(2,1)S(1)}, bf16[272,128]{1,0:T(8,128)(2,1)S(1)}, u32[]{:S(2)}, u32[]{:S(2)}) collective-permute-start(bf16[272,128]{1,0:T(8,128)(2,1)S(1)} %get-tuple-element.24), channel_id=1, source_target_pairs={{0,8},{2,10},{4,12},{6,14},{8,0},{10,2},{12,4},{14,6},{1,9},{3,11}... | collective-permute-start | bytes 208904 | tf_op jit(solution)/shard_map/ppermute | solution.py:370
  14.8 6.2 %copy-start.2 = (bf16[2,8,16,256]{3,2,1,0:T(8,128)(2,1)S(1)}, bf16[2,8,16,256]{3,2,1,0:T(8,128)(2,1)}, u32[]{:S(2)}) copy-start(bf16[2,8,16,256]{3,2,1,0:T(8,128)(2,1)} %constant.9.clone.refs_8_) | copy-start | bytes 393220
  14.8 6.2 %collective-permute-start.6 = (bf16[272,128]{1,0:T(8,128)(2,1)S(1)}, bf16[272,128]{1,0:T(8,128)(2,1)S(1)}, u32[]{:S(2)}, u32[]{:S(2)}) collective-permute-start(bf16[272,128]{1,0:T(8,128)(2,1)S(1)} %get-tuple-element.25), channel_id=1, source_target_pairs={{0,12},{2,14},{4,8},{6,10},{8,4},{10,6},{12,0},{14,2},{1,13},{3,15... | collective-permute-start | bytes 208904 | tf_op jit(solution)/shard_map/ppermute | solution.py:370
  17.2 7.0 %copy-start = (f32[8,32,512]{2,1,0:T(8,128)S(1)}, f32[8,32,512]{2,1,0:T(8,128)}, u32[]{:S(2)}) copy-start(f32[8,32,512]{2,1,0:T(8,128)} %constant.11.clone.turn_ref) | copy-start | bytes 1572868
  17.3 6.9 %copy-start.1 = (bf16[256,512]{1,0:T(8,128)(2,1)S(1)}, bf16[256,512]{1,0:T(8,128)(2,1)}, u32[]{:S(2)}) copy-start(bf16[256,512]{1,0:T(8,128)(2,1)} %constant.10.clone.inverse_ref) | copy-start | bytes 786436
  22.9 1.3 %collective-permute-start.7 = (bf16[256,128]{1,0:T(8,128)(2,1)S(1)}, bf16[256,128]{1,0:T(8,128)(2,1)S(1)}, u32[]{:S(2)}, u32[]{:S(2)}) collective-permute-start(bf16[256,128]{1,0:T(8,128)(2,1)S(1)} %get-tuple-element.29), channel_id=1, source_target_pairs={{0,1},{1,0},{2,3},{3,2},{4,5},{5,4},{6,7},{7,6},{8,9},{9,8},{10,11... | collective-permute-start | bytes 196616 | tf_op jit(solution)/shard_map/ppermute | solution.py:423
  26.2 4.2 %collective-permute-start.8 = (bf16[96,256]{1,0:T(8,128)(2,1)S(1)}, bf16[96,256]{1,0:T(8,128)(2,1)S(1)}, u32[]{:S(2)}, u32[]{:S(2)}) collective-permute-start(bf16[96,256]{1,0:T(8,128)(2,1)S(1)} %get-tuple-element.31.a_ref), channel_id=1, source_target_pairs={{0,2},{2,0},{4,6},{6,4},{8,10},{10,8},{12,14},{14,12},{1,3},{3,1},... | collective-permute-start | bytes 147464 | tf_op jit(solution)/shard_map/ppermute | solution.py:370
  30.3 6.1 %collective-permute-start.11 = (bf16[96,256]{1,0:T(8,128)(2,1)S(1)}, bf16[96,256]{1,0:T(8,128)(2,1)S(1)}, u32[]{:S(2)}, u32[]{:S(2)}) collective-permute-start(bf16[96,256]{1,0:T(8,128)(2,1)S(1)} %add.1.refs_0_), channel_id=1, source_target_pairs={{0,12},{2,14},{4,8},{6,10},{8,4},{10,6},{12,0},{14,2},{1,13},{3,15... | collective-permute-start | bytes 147464 | tf_op jit(solution)/shard_map/ppermute | solution.py:370
  31.8 4.7 %collective-permute-start.10 = (bf16[96,256]{1,0:T(8,128)(2,1)S(1)}, bf16[96,256]{1,0:T(8,128)(2,1)S(1)}, u32[]{:S(2)}, u32[]{:S(2)}) collective-permute-start(bf16[96,256]{1,0:T(8,128)(2,1)S(1)} %add.1.refs_0_), channel_id=1, source_target_pairs={{0,4},{2,6},{4,0},{6,2},{8,12},{10,14},{12,8},{14,10},{1,5},{3,7},... | collective-permute-start | bytes 147464 | tf_op jit(solution)/shard_map/ppermute | solution.py:370
  32.2 5.0 %collective-permute-start.9 = (bf16[96,256]{1,0:T(8,128)(2,1)S(1)}, bf16[96,256]{1,0:T(8,128)(2,1)S(1)}, u32[]{:S(2)}, u32[]{:S(2)}) collective-permute-start(bf16[96,256]{1,0:T(8,128)(2,1)S(1)} %add.1.refs_0_), channel_id=1, source_target_pairs={{0,8},{2,10},{4,12},{6,14},{8,0},{10,2},{12,4},{14,6},{1,9},{3,11}... | collective-permute-start | bytes 147464 | tf_op jit(solution)/shard_map/ppermute | solution.py:370
  34.8 2.4 %copy-start.3 = (f32[32,768]{1,0:T(8,128)S(1)}, f32[32,768]{1,0:T(8,128)}, u32[]{:S(2)}) copy-start(f32[32,768]{1,0:T(8,128)} %refs_4_.1) | copy-start | bytes 294916
